TPU v7x, 32 devices: a whole 2x2x4 slice. The times are simulated.
32 devices in a mesh: groups: 2 (over y), seq: 8 (over z, x), section: 2 (over core).
Axes of the slice: x: 2, y: 2, z: 4, core: 2. Of those that a mesh axis runs over, the one named last changes fastest.
Arguments:
- skip_in: bfloat16 [2, 1024, 1536], P('groups', 'seq'), parts along dimension 0, may hold values from -6 to 6
- attn_gain: float32 [1536], replicated, may hold values from 0.25 to 1.75
- query_weight: bfloat16 [1536, 1024], P(None, 'section'), may hold values from -0.625 to 0.625
- kv_weight: bfloat16 [1536, 256], replicated, may hold values from -0.15625 to 0.15625
- pair_bias: float32 [2, 8, 32, 32], P('groups', 'section', 'seq'), parts along dimension 0, may hold values from -12 to 400
- out_weight: bfloat16 [1024, 1536], P('section'), may hold values from -0.1875 to 0.1875
- dec_gain: float32 [1536], replicated, may hold values from 0.25 to 1.75
- dec_weight: bfloat16 [5, 1536, 768], P(None, 'seq', 'section'), may hold values from -0.0625 to 0.0625
- dec_bias: float32 [768], P('section'), may hold values from -3 to 3
Outputs:
- decoded: bfloat16 [2, 1024, 768], P('groups', 'seq', 'section'), parts along dimension 0
There are 2 independent parts, one for each index of `groups`. A program takes and returns all parts, laid end to end along the dimension named above; an argument that names none is the same for every part. Nothing has to cross between parts.
All inputs are finite; a program needn't handle non-finite values.
Results may differ from a plain program's by a relative error of at most 0.0095.
Values may be sent and summed in bfloat16 or wider, within the bound.
No kernel may reach another device: no remote copies, remote signals or barrier semaphores. Data moves between devices by JAX's collectives and lax.ppermute only.
A program may use at most 64 MiB of HBM per device.

v0:
```python
import math

import jax
import jax.numpy as jnp
from jax import lax
from jax.sharding import PartitionSpec as P

HEAD = 128
KW = 5
PAIR = 16


def extended(block, sides, width):
    for axis, dim in sides:
        count = lax.axis_size(axis)
        forward = [(i, i + 1) for i in range(count - 1)]
        backward = [(target, source) for source, target in forward]
        low = lax.ppermute(
            lax.slice_in_dim(block, block.shape[dim] - width, None, axis=dim), axis, forward
        )
        high = lax.ppermute(lax.slice_in_dim(block, 0, width, axis=dim), axis, backward)
        block = jnp.concatenate([low, block, high], axis=dim)
    return block


def norm_scale(values_in, gain):
    wide = values_in.astype(jnp.float32)
    return wide * lax.rsqrt(jnp.mean(wide * wide, axis=-1, keepdims=True) + 1e-06) * gain


def body(
    skip_in,
    attn_gain,
    query_weight,
    kv_weight,
    pair_bias,
    out_weight,
    dec_gain,
    dec_weight,
    dec_bias,
):
    seq_count, local_rows, channels = skip_in.shape
    half_rows = local_rows // 2
    local_heads = query_weight.shape[1] // HEAD
    logit_scale = 1.0 / math.sqrt(HEAD)
    pooled = jnp.max(skip_in.reshape(seq_count, half_rows, 2, channels), axis=2)
    normed = norm_scale(pooled, attn_gain).astype(jnp.bfloat16)
    flattened = normed.reshape(seq_count * half_rows, channels)
    query_rows = jnp.dot(flattened, query_weight, preferred_element_type=jnp.float32).astype(
        jnp.bfloat16
    )
    query_rows = query_rows.reshape(seq_count, half_rows, local_heads, HEAD)
    row_bias = jnp.repeat(pair_bias, PAIR, axis=2)
    row_bias = jnp.pad(row_bias, ((0, 0), (0, 0), (0, 0), (0, 2)))
    quarter = half_rows // 2
    own_rows = lax.dynamic_slice_in_dim(normed, lax.axis_index("section") * quarter, quarter, 1)
    key_values = jnp.dot(
        own_rows.reshape(seq_count * quarter, channels),
        kv_weight,
        preferred_element_type=jnp.float32,
    )
    key_values = key_values.astype(jnp.bfloat16).reshape(seq_count, quarter, 2 * HEAD)
    piece = lax.all_gather(key_values, ("seq", "section"), axis=1, tiled=True)
    start = jnp.int32(0)
    running_max = jnp.full((seq_count, local_heads, half_rows), -1e30, jnp.float32)
    running_sum = jnp.zeros((seq_count, local_heads, half_rows), jnp.float32)
    weighted = jnp.zeros((seq_count, local_heads, half_rows, HEAD), jnp.float32)
    piece_rows = piece.shape[1]
    block_size = min(piece_rows, 2048)
    for offset in range(0, piece_rows, block_size):
        piece_len = min(block_size, piece_rows - offset)
        sub_piece = piece[:, offset : offset + piece_len]
        key_portion = sub_piece[:, :, :HEAD]
        value_part = sub_piece[:, :, HEAD:]
        first_row = start + offset
        blocks = lax.dynamic_slice_in_dim(row_bias, first_row // PAIR, piece_len // PAIR + 2, 3)
        spread = jnp.repeat(blocks, PAIR, axis=3)
        key_bias = lax.dynamic_slice_in_dim(spread, first_row % PAIR, piece_len, 3)
        scores = (
            jnp.einsum(
                "wtzj,wgj->wztg", query_rows, key_portion, preferred_element_type=jnp.float32
            )
            * logit_scale
            + key_bias
        )
        new_max = jnp.maximum(running_max, jnp.max(scores, axis=-1))
        rescale = jnp.exp(running_max - new_max)
        exponent_scores = jnp.exp(scores - new_max[..., None])
        running_sum = running_sum * rescale + jnp.sum(exponent_scores, axis=-1)
        weighted = weighted * rescale[..., None] + jnp.einsum(
            "umrl,ult->umrt",
            exponent_scores.astype(jnp.bfloat16),
            value_part,
            preferred_element_type=jnp.float32,
        )
        running_max = new_max
    folded = (running_max, running_sum, weighted)
    running_max, running_sum, weighted = folded
    context = (weighted / running_sum[..., None]).astype(jnp.bfloat16)
    context = jnp.transpose(context, (0, 2, 1, 3)).reshape(
        seq_count * half_rows, local_heads * HEAD
    )
    partial_value = jnp.dot(context, out_weight, preferred_element_type=jnp.float32).reshape(
        seq_count, half_rows, channels
    )
    summed = lax.psum(partial_value.astype(jnp.bfloat16), "section").astype(jnp.float32)
    attended = (pooled.astype(jnp.float32) + summed).astype(jnp.bfloat16)
    joined = (
        jnp.repeat(attended, 2, axis=1).astype(jnp.float32) + skip_in.astype(jnp.float32)
    ).astype(jnp.bfloat16)
    activated = jax.nn.gelu(norm_scale(joined, dec_gain)).astype(jnp.bfloat16)
    padded = extended(activated, (("seq", 1),), KW // 2)
    out_half = dec_weight.shape[2]
    piece = lax.all_gather(dec_weight, "seq", axis=1, tiled=True)
    piece_rows = piece.shape[1]
    stacked = jnp.concatenate(
        [padded[:, tap_index : tap_index + local_rows] for tap_index in range(KW)], axis=2
    )
    stacked = stacked.reshape(seq_count * local_rows, KW * piece_rows)
    convolved = jnp.dot(
        stacked, piece.reshape(KW * piece_rows, out_half), preferred_element_type=jnp.float32
    )
    residual = lax.dynamic_slice_in_dim(joined, lax.axis_index("section") * out_half, out_half, 2)
    decoded = (
        convolved.reshape(seq_count, local_rows, out_half) + dec_bias + residual.astype(jnp.float32)
    )
    return decoded.astype(jnp.bfloat16)


def solution(mesh):
    return jax.shard_map(
        body,
        mesh=mesh,
        in_specs=(
            P("groups", "seq", None),
            P(),
            P(None, "section"),
            P(),
            P("groups", "section", "seq", None),
            P("section", None),
            P(),
            P(None, "seq", "section"),
            P("section"),
        ),
        out_specs=P("groups", "seq", "section"),
        check_vma=False,
    )
```

profile of v0, /device:TPU:0, one launch (start us, length us, event | category | flops | bytes accessed | tf_op | source)
XLA Modules:
  0.0 150.7 jit_solution(8483585687084230014)
XLA Ops:
  7.4 0.0 copy-start
  7.4 0.0 copy-start.2
  7.4 0.0 copy-start.1
  7.4 0.0 all-reduce.3.cloned.1.call-start
  7.4 2.0 %reshape.220 = bf16[64,2,1536]{2,1,0:T(2,128)(2,1)} reshape(bf16[1,128,1536]{2,1,0:T(8,128)(2,1)} %param.9) | data formatting | bytes 786432 | tf_op jit(solution)/shard_map/reshape | solution.py:46
  9.4 2.0 %reduce_max.18 = bf16[64,1536]{1,0:T(8,128)(2,1)S(1)} reduce(bf16[64,2,1536]{2,1,0:T(2,128)(2,1)} %reshape.220, bf16[]{:T(256)} %constant.24.clone.1), dimensions={1}, to_apply=%region_0.0 | reduce | flops 98304 | bytes 589826 | tf_op jit(solution)/shard_map/reduce_max | solution.py:46
  11.4 0.0 copy-start.4
  11.4 0.1 fusion.37
  11.5 0.8 convert_bitcast_fusion
  12.3 0.1 dynamic-slice.1
  12.4 0.0 copy-done.2
  12.4 1.5 %convolution_convert_fusion.2 = bf16[32,256]{1,0:T(8,128)(2,1)S(1)} fusion(bf16[1536,256]{1,0:T(8,128)(2,1)} %param.12, f32[1,64,1536]{2,1,0:T(8,128)} %convert_bitcast_fusion, s32[]{:T(128)S(6)} %select_n.15, f32[1536]{0:T(1024)S(1)} %copy-done.2, f32[32]{0:T(128)S(1)} %dynamic-slice.1), kind=kOutput, calls=%fused_computation.18 | convolution fusion | flops 25321472 | bytes 1005700 | tf_op jit(solution)/shard_map/dot_general | solution.py:57
  13.9 25.2 %all-gather = bf16[512,256]{1,0:T(8,128)(2,1)} all-gather(bf16[32,256]{1,0:T(8,128)(2,1)S(1)} %convolution_convert_fusion.2), channel_id=2, replica_groups=mesh['groups'=2,'seq'=8,'section'=2] {'seq','section'}, dimensions={0}, use_global_device_ids=true | all-gather | bytes 278528 | tf_op jit(solution)/shard_map/all_gather | solution.py:63
  39.1 0.0 copy-done.1
  39.1 0.4 fusion.19
  39.6 0.0 copy-done.4
  39.6 0.1 copy.16
  39.7 0.1 broadcast_in_dim.31
  39.8 0.1 slice.41
  39.9 0.3 copy.19
  40.2 1.2 fusion.63
  41.4 0.2 fusion.31
  41.7 1.2 fusion.20
  42.9 0.1 copy.18
  42.9 0.0 copy-done
  42.9 1.1 fusion
  44.0 0.0 all-reduce.3.cloned.1.call-update
  44.0 0.0 all-gather.3.cloned.1.call-start
  44.1 0.5 all-gather.3.cloned.1.call-update
  44.6 15.0 %all-reduce.3.cloned.1.call-done = bf16[1,64,1536]{2,1,0:T(8,128)(2,1)} async-done(((bf16[1,64,1536]{2,1,0:T(8,128)(2,1)}), bf16[1,64,1536]{2,1,0:T(8,128)(2,1)}) %all-reduce.3.cloned.1.call-update) | async-done | bytes 196624 | tf_op jit(solution)/shard_map/psum | solution.py:106
  59.6 1.0 fusion.46
  60.6 0.0 copy-start.3
  60.6 0.3 broadcast_in_dim.34
  60.9 0.5 convert_element_type.120
  61.4 1.2 fusion.21
  62.6 0.0 copy-done.3
  62.6 0.4 fusion.25
  63.0 3.6 %collective-permute-start = (bf16[1,2,1536]{2,1,0:T(2,128)(2,1)S(1)}, bf16[1,2,1536]{2,1,0:T(2,128)(2,1)S(1)}, u32[]{:S(2)}, u32[]{:S(2)}) collective-permute-start(bf16[1,2,1536]{2,1,0:T(2,128)(2,1)S(1)} %get-tuple-element.8), channel_id=1, source_target_pairs={{0,2},{2,4},{4,6},{6,8},{8,10},{10,12},{12,14},{1,3},{3,5},{5,7},{... | collective-permute-start | bytes 18440 | tf_op jit(solution)/shard_map/ppermute | solution.py:18
  66.7 0.0 copy-start.5
  66.7 1.3 collective-permute-start.1
  68.0 0.0 collective-permute-done
  68.0 0.8 fusion.36
  68.8 0.9 fusion.41
  69.7 1.2 constant_dynamic-update-slice_fusion
  70.9 1.3 collective-permute-done.1
  72.2 0.9 fusion.34
  73.1 0.9 fusion.40
  74.0 64.1 %all-gather.3.cloned.1.call-done = bf16[5,1536,384]{2,1,0:T(8,128)(2,1)} async-done(((bf16[5,192,384]{2,1,0:T(8,128)(2,1)}), bf16[5,1536,384]{2,1,0:T(8,128)(2,1)}) %all-gather.3.cloned.1.call-update) | async-done | bytes 5898256 | tf_op jit(solution)/shard_map/all_gather | solution.py:114
  138.1 0.0 copy-done.5
  138.1 5.1 %fusion.14 = bf16[1,128,384]{2,1,0:T(8,128)(2,1)} fusion(bf16[7680,384]{1,0:T(8,128)(2,1)} %bitcast.79, bf16[1,128,7680]{2,1,0:T(8,128)(2,1)} %fusion.40, bf16[1,128,1536]{2,1,0:T(8,128)(2,1)S(1)} %get-tuple-element.6, s32[]{:T(128)S(6)} %select_n.16, f32[384]{0:T(512)S(1)} %copy-done.5), kind=kOutput, calls=%fused_computation.11 | convolution fusion | flops 755171328 | bytes 8062468 | tf_op jit(solution)/shard_map/dot_general | solution.py:120
  (7 shorter events, 0.1 us)
Async XLA Ops:
  7.4 35.6 %copy-start = (bf16[512,1536]{1,0:T(8,128)(2,1)S(1)}, bf16[512,1536]{1,0:T(8,128)(2,1)}, u32[]{:S(2)}) copy-start(bf16[512,1536]{1,0:T(8,128)(2,1)} %param.14) | copy-start | bytes 4718596
  7.4 5.0 %copy-start.2 = (f32[1536]{0:T(1024)S(1)}, f32[1536]{0:T(1024)}, u32[]{:S(2)}) copy-start(f32[1536]{0:T(1024)} %param.10) | copy-start | bytes 18436
  7.4 31.7 %copy-start.1 = (bf16[1536,512]{1,0:T(8,128)(2,1)S(1)}, bf16[1536,512]{1,0:T(8,128)(2,1)}, u32[]{:S(2)}) copy-start(bf16[1536,512]{1,0:T(8,128)(2,1)} %param.11) | copy-start | bytes 4718596
  7.4 52.2 %all-reduce.3.cloned.1.call-start = ((), (), s32[]{:S(2)}) async-start(), calls=%async_computation | async-start | bytes 393216 | tf_op jit(solution)/shard_map/psum | solution.py:106
  11.4 28.2 %copy-start.4 = (f32[1,4,4,32]{3,2,1,0:T(4,128)S(1)}, f32[1,4,4,32]{3,2,1,0:T(4,128)}, u32[]{:S(2)}) copy-start(f32[1,4,4,32]{3,2,1,0:T(4,128)} %param.13) | copy-start | bytes 6148
  44.0 94.0 %all-gather.3.cloned.1.call-start = ((), (), s32[]{:S(2)}) async-start(), calls=%async_computation.1 | async-start | bytes 6635520 | tf_op jit(solution)/shard_map/all_gather | solution.py:114
  60.6 2.1 %copy-start.3 = (f32[1536]{0:T(1024)S(1)}, f32[1536]{0:T(1024)}, u32[]{:S(2)}) copy-start(f32[1536]{0:T(1024)} %param.15) | copy-start | bytes 18436
  63.0 5.0 %collective-permute-start = (bf16[1,2,1536]{2,1,0:T(2,128)(2,1)S(1)}, bf16[1,2,1536]{2,1,0:T(2,128)(2,1)S(1)}, u32[]{:S(2)}, u32[]{:S(2)}) collective-permute-start(bf16[1,2,1536]{2,1,0:T(2,128)(2,1)S(1)} %get-tuple-element.8), channel_id=1, source_target_pairs={{0,2},{2,4},{4,6},{6,8},{8,10},{10,12},{12,14},{1,3},{3,5},{5,7},{... | collective-permute-start | bytes 18440 | tf_op jit(solution)/shard_map/ppermute | solution.py:18
  66.7 71.4 %copy-start.5 = (f32[384]{0:T(512)S(1)}, f32[384]{0:T(512)}, u32[]{:S(2)}) copy-start(f32[384]{0:T(512)} %param.17) | copy-start | bytes 4612
  66.7 5.5 %collective-permute-start.1 = (bf16[1,2,1536]{2,1,0:T(2,128)(2,1)S(1)}, bf16[1,2,1536]{2,1,0:T(2,128)(2,1)S(1)}, u32[]{:S(2)}, u32[]{:S(2)}) collective-permute-start(bf16[1,2,1536]{2,1,0:T(2,128)(2,1)S(1)} %get-tuple-element.7), channel_id=1, source_target_pairs={{2,0},{4,2},{6,4},{8,6},{10,8},{12,10},{14,12},{3,1},{5,3},{7,5},{... | collective-permute-start | bytes 18440 | tf_op jit(solution)/shard_map/ppermute | solution.py:21
Sparse Core Ops, SparseCore 0:
  44.2 15.3 all-reduce.2
Sparse Core Ops, SparseCore 1:
  46.7 91.3 all-gather.2
where the time goes:
time: 151 us
  waiting for transfers between devices  81 us (54%)
  blocking collectives  25.2 us (17%)
  between operations  15 us (10%)
  matrix products  10.6 us (7%)
  other arithmetic  10.3 us (7%)
  starting transfers between devices  4.96 us (3%)
  local copies, waits for them, and re-layouts  3.61 us (2%)
    all_gather x1, waiting for transfers between devices, body(): piece = lax.all_gather(dec_weight, 'seq', axis=1, tiled=True)  64.1 us
    all_gather x1, blocking collectives, body(): piece = lax.all_gather(key_values, ('seq', 'section'), axis=1, tiled=True)  25.2 us
    psum x1, waiting for transfers between devices, body(): lax.psum(partial_value.astype(jnp.bfloat16), 'section').astype(jnp.float32)  15 us
    dot_general x1, matrix products, body(): jnp.dot(stacked, piece.reshape(KW * piece_rows, out_half), preferred_elem...  5.14 us
    unnamed x4, other arithmetic  3.74 us
    ppermute x1, starting transfers between devices, extended(): lax.ppermute(lax.slice_in_dim(block, block.shape[dim] - width, None, axis...  3.62 us
  transfers between devices with their start and end apart: 4, of which 3 were waited for; matrix products, arithmetic and copies ran while one was open for 5% of the time, Pallas kernels for 0%

commit v1 on v0

--- a/solution.py
+++ b/solution.py
@@ -3,6 +3,8 @@
 import jax
 import jax.numpy as jnp
 from jax import lax
+from jax.experimental import pallas as pl
+from jax.experimental.pallas import tpu as pltpu
 from jax.sharding import PartitionSpec as P
 
 HEAD = 128
@@ -127,9 +129,302 @@
     return decoded.astype(jnp.bfloat16)
 
 
+ROWS = 80
+MSG = 112
+LIMIT = 56 * 1024 * 1024
+
+
+def exchange(values_in, axis, mask):
+    count = lax.axis_size(axis)
+    return lax.ppermute(values_in, axis, [(i, i ^ mask) for i in range(count)])
+
+
+def call(kernel, outs, args, scratch=(), spaces=None):
+    vmem = pl.BlockSpec(memory_space=pltpu.VMEM)
+    specs = [vmem] * len(args) if spaces is None else spaces
+    return pl.pallas_call(
+        kernel,
+        out_shape=[jax.ShapeDtypeStruct(shape, kind) for shape, kind in outs],
+        in_specs=specs,
+        out_specs=[vmem] * len(outs),
+        scratch_shapes=list(scratch),
+        compiler_params=pltpu.CompilerParams(vmem_limit_bytes=LIMIT),
+    )(*args)
+
+
+def split_three(wide):
+    high = wide.astype(jnp.bfloat16)
+    rest = wide - high.astype(jnp.float32)
+    middle = rest.astype(jnp.bfloat16)
+    low = (rest - middle.astype(jnp.float32)).astype(jnp.bfloat16)
+    return high, middle, low
+
+
+def normalize(wide, gain):
+    return wide * lax.rsqrt(jnp.mean(wide * wide, axis=-1, keepdims=True) + 1e-06) * gain
+
+
+def gelu(wide):
+    inner = math.sqrt(2.0 / math.pi) * (wide + 0.044715 * (wide * wide * wide))
+    return 0.5 * wide * (1.0 + jnp.tanh(inner))
+
+
+def spread_columns(wide, values_in):
+    for k in range(wide.shape[0]):
+        wide[k] = values_in[:, 128 * k : 128 * k + 128].astype(jnp.float32)
+
+
+def take_rows(wide, start, size):
+    return jnp.concatenate(
+        [wide[k, pl.ds(start, size, stride=2), :] for k in range(wide.shape[0])], axis=1
+    )
+
+
+def put_rows(wide, start, values_in):
+    for k in range(wide.shape[0]):
+        wide[k, pl.ds(start, values_in.shape[0], stride=2), :] = values_in[:, 128 * k : 128 * k + 128]
+
+
+def pool_kernel(skip_ref, gain_ref, weight_ref, bias_ref, message_ref, normed_ref, wide, lines):
+    half = skip_ref.shape[0] // 2
+    spread_columns(wide, skip_ref)
+    pooled = jnp.maximum(take_rows(wide, 0, half), take_rows(wide, 1, half))
+    normed = normalize(pooled, gain_ref[...]).astype(jnp.bfloat16)
+    normed_ref[...] = normed
+    lines[0:half, :] = jnp.dot(normed, weight_ref[...], preferred_element_type=jnp.float32)
+    last = skip_ref.shape[0]
+    for n, row in enumerate((0, 1, last - 2, last - 1)):
+        for k in range(12):
+            at = half + 6 * n + k // 2
+            lines[at : at + 1, 128 * (k % 2) : 128 * (k % 2) + 128] = wide[k, row : row + 1, :]
+    lines[88:MSG, :] = jnp.zeros((MSG - 88, 256), jnp.float32)
+    for n, term in enumerate(split_three(bias_ref[...])):
+        for h in range(4):
+            for k, cell in enumerate((0, 3)):
+                at = 88 + 8 * n + 2 * h + k
+                lines[at : at + 1, 0:32] = term[4 * h + cell : 4 * h + cell + 1, :].astype(
+                    jnp.float32
+                )
+    message_ref[...] = lines[...].astype(jnp.bfloat16)
+
+
+def reverse_bits(value):
+    return (value & 1) * 4 + (value & 2) + (value >> 2)
+
+
+def attention_kernel(
+    query_ref, message_ref, query_weight_ref, gain_ref, bias_ref, out_weight_ref, terms_ref, edge_ref
+):
+    me = lax.axis_index("seq")
+    count = lax.axis_size("seq")
+    low_slot = reverse_bits(me ^ jnp.maximum(me - 1, 0))
+    high_slot = reverse_bits(me ^ jnp.minimum(me + 1, count - 1))
+    low = message_ref[low_slot].astype(jnp.float32)
+    high = message_ref[high_slot].astype(jnp.float32)
+
+    def line(block, row):
+        start = 64 + 6 * row
+        return jnp.concatenate([block[start + k : start + k + 1, :] for k in range(6)], axis=1)
+
+    edges = jnp.concatenate(
+        [line(low, 2), line(low, 3), line(high, 0), line(high, 1)], axis=0
+    )
+    edge_ref[0:4, :] = edges
+    edge_ref[4:8, :] = jnp.zeros_like(edges)
+    pooled = jnp.concatenate(
+        [
+            jnp.maximum(edges[0:1], edges[1:2]),
+            jnp.maximum(edges[2:3], edges[3:4]),
+            jnp.zeros((14, edges.shape[1]), jnp.float32),
+        ],
+        axis=0,
+    )
+    normed = normalize(pooled, gain_ref[...]).astype(jnp.bfloat16)
+    halo_query = jnp.dot(normed, query_weight_ref[...], preferred_element_type=jnp.float32)
+    queries = jnp.concatenate([query_ref[...], halo_query.astype(jnp.bfloat16)], axis=0)
+    keys = jnp.concatenate([message_ref[k, 0:64, 0:HEAD] for k in range(8)], axis=0)
+    values = jnp.concatenate([message_ref[k, 0:64, HEAD : 2 * HEAD] for k in range(8)], axis=0)
+    cell = lax.broadcasted_iota(jnp.int32, (32, 512), 0)
+    column = lax.broadcasted_iota(jnp.int32, (32, 512), 1)
+    wanted = 4 * (reverse_bits(column >> 6) ^ me) + ((column & 63) >> 4)
+    spread = jnp.where(cell == wanted, 1.0, 0.0).astype(jnp.bfloat16)
+    bias = jnp.zeros((32, 512), jnp.float32)
+    for n, term in enumerate(split_three(bias_ref[...])):
+        at = 88 + 8 * n
+        table = jnp.concatenate(
+            [term, low[at : at + 8, 0:32].astype(jnp.bfloat16), high[at : at + 8, 0:32].astype(jnp.bfloat16)],
+            axis=0,
+        )
+        bias = bias + jnp.dot(table, spread, preferred_element_type=jnp.float32)
+    first = lax.broadcasted_iota(jnp.int32, (16, 512), 0) == 0
+    parts = []
+    for h in range(4):
+        scores = lax.dot_general(
+            queries[:, h * HEAD : (h + 1) * HEAD],
+            keys,
+            (((1,), (1,)), ((), ())),
+            preferred_element_type=jnp.float32,
+        )
+        rows = [jnp.broadcast_to(bias[4 * h + r : 4 * h + r + 1, :], (16, 512)) for r in range(4)]
+        rows.append(
+            jnp.where(first, bias[17 + 2 * h : 18 + 2 * h, :], bias[24 + 2 * h : 25 + 2 * h, :])
+        )
+        scores = scores * (1.0 / math.sqrt(HEAD)) + jnp.concatenate(rows, axis=0)
+        exps = jnp.exp(scores - jnp.max(scores, axis=-1, keepdims=True))
+        totals = jnp.sum(exps, axis=-1, keepdims=True)
+        mixed = jnp.dot(exps.astype(jnp.bfloat16), values, preferred_element_type=jnp.float32)
+        parts.append((mixed / totals).astype(jnp.bfloat16))
+    context = jnp.concatenate(parts, axis=1)
+    terms_ref[...] = jnp.dot(
+        context, out_weight_ref[...], preferred_element_type=jnp.float32
+    ).astype(jnp.bfloat16)
+
+
+def activate_kernel(
+    skip_ref, edge_ref, own_ref, other_ref, gain_ref, dec_bias_ref, keep_ref, send_ref, base_ref, wide, active
+):
+    me = lax.axis_index("seq")
+    section = lax.axis_index("section")
+    upper = me >> 2
+    gain = gain_ref[...]
+    spread_columns(wide, skip_ref)
+    even = take_rows(wide, 0, 64)
+    odd = take_rows(wide, 1, 64)
+    projected = own_ref[...].astype(jnp.float32) + other_ref[...].astype(jnp.float32)
+
+    def rounded(values_in):
+        return values_in.astype(jnp.bfloat16).astype(jnp.float32)
+
+    attended = rounded(jnp.maximum(even, odd) + projected[0:64])
+    even = rounded(attended + even)
+    odd = rounded(attended + odd)
+    put_rows(wide, 0, even)
+    put_rows(wide, 1, odd)
+    put_rows(active, 8, gelu(normalize(even, gain)))
+    put_rows(active, 9, gelu(normalize(odd, gain)))
+    edges = edge_ref[0:4, :]
+    low = rounded(jnp.maximum(edges[0:1], edges[1:2]) + projected[64:65])
+    high = rounded(jnp.maximum(edges[2:3], edges[3:4]) + projected[65:66])
+    joined = rounded(edges + jnp.concatenate([low, low, high, high], axis=0))
+    halo = gelu(normalize(joined, gain))
+    above = jnp.where(me > 0, halo[0:2], 0.0)
+    below = jnp.where(me < lax.axis_size("seq") - 1, halo[2:4], 0.0)
+    zeros = jnp.zeros((6, 128), jnp.float32)
+    for k in range(12):
+        columns = slice(128 * k, 128 * k + 128)
+        active[k, 0:8, :] = jnp.concatenate([zeros, above[:, columns]], axis=0)
+        active[k, 136:144, :] = jnp.concatenate([below[:, columns], zeros], axis=0)
+    for k in range(6):
+        keep_ref[:, 128 * k : 128 * k + 128] = active[upper * 6 + k].astype(jnp.bfloat16)
+    for k in range(3):
+        columns = slice(128 * k, 128 * k + 128)
+        send_ref[:, columns] = active[(1 - upper) * 6 + section * 3 + k].astype(jnp.bfloat16)
+        base_ref[:, columns] = wide[section * 3 + k] + dec_bias_ref[:, columns]
+
+
+def load_weight(own_ref, side_ref, next_ref, far_top_ref, far_bottom_ref, weight, semaphores):
+    slot = lax.axis_index("seq") & 3
+    pieces = (
+        (own_ref, slot * 192, 192),
+        (side_ref, (slot ^ 1) * 192, 192),
+        (next_ref, (slot ^ 2) * 192, 192),
+        (far_top_ref, (slot ^ 3) * 192, 96),
+        (far_bottom_ref, (slot ^ 3) * 192 + 96, 96),
+    )
+    copies = [
+        pltpu.make_async_copy(
+            ref, weight.at[:, pl.ds(pl.multiple_of(start, 32), size), :], semaphores.at[n]
+        )
+        for n, (ref, start, size) in enumerate(pieces)
+    ]
+    for copy in copies:
+        copy.start()
+    for copy in copies:
+        copy.wait()
+
+
+def shifted_sum(products):
+    total = products[0][6:134]
+    for tap in range(1, KW):
+        total = total + products[tap][6 + tap : 134 + tap]
+    return total
+
+
+def own_kernel(active_ref, base_ref, w0, w1, w2, w3, w4, out_ref, weight, semaphores):
+    load_weight(w0, w1, w2, w3, w4, weight, semaphores)
+    active = active_ref[...]
+    out_ref[...] = base_ref[...] + shifted_sum(
+        [jnp.dot(active, weight[t], preferred_element_type=jnp.float32) for t in range(KW)]
+    )
+
+
+def partner_kernel(first_ref, second_ref, w0, w1, w2, w3, w4, out_ref, weight, semaphores):
+    load_weight(w0, w1, w2, w3, w4, weight, semaphores)
+    section = lax.axis_index("section")
+    first, second = first_ref[...], second_ref[...]
+    near = pl.ds(pl.multiple_of(section * 384, 128), 384)
+    far = pl.ds(pl.multiple_of((1 - section) * 384, 128), 384)
+    out_ref[...] = shifted_sum(
+        [
+            jnp.dot(first, weight[t, near, :], preferred_element_type=jnp.float32)
+            + jnp.dot(second, weight[t, far, :], preferred_element_type=jnp.float32)
+            for t in range(KW)
+        ]
+    ).astype(jnp.bfloat16)
+
+
+def split_body(
+    skip_in, attn_gain, query_weight, kv_weight, pair_bias, out_weight, dec_gain, dec_weight, dec_bias
+):
+    bf16, f32 = jnp.bfloat16, jnp.float32
+    skip = skip_in[0]
+    rows, channels = skip.shape
+    gain = attn_gain.reshape(1, channels)
+    bias = pair_bias.reshape(16, 32)
+    taps, depth, width = dec_weight.shape
+    side = exchange(dec_weight, "seq", 1)
+    after = exchange(dec_weight, "seq", 2)
+    far_top = exchange(after[:, : depth // 2], "seq", 1)
+    far_bottom = exchange(side[:, depth // 2 :], "seq", 2)
+    message, normed = call(
+        pool_kernel,
+        [((MSG, 256), bf16), ((rows // 2, channels), bf16)],
+        [skip, gain, kv_weight, bias],
+        [pltpu.VMEM((channels // 128, rows, 128), f32), pltpu.VMEM((MSG, 256), f32)],
+    )
+    messages = message[None]
+    for mask in (4, 2, 1):
+        messages = jnp.concatenate([messages, exchange(messages, "seq", mask)], axis=0)
+    queries = jnp.dot(normed, query_weight, preferred_element_type=f32).astype(bf16)
+    terms, edges = call(
+        attention_kernel,
+        [((ROWS, channels), bf16), ((8, channels), f32)],
+        [queries, messages, query_weight, gain, bias, out_weight],
+    )
+    other = exchange(terms, "section", 1)
+    keep, send, base = call(
+        activate_kernel,
+        [((rows + 16, channels // 2), bf16), ((rows + 16, channels // 4), bf16), ((rows, width), f32)],
+        [skip, edges, terms, other, dec_gain.reshape(1, channels), dec_bias.reshape(1, width)],
+        [pltpu.VMEM((channels // 128, rows + extra, 128), f32) for extra in (0, 16)],
+    )
+    first = exchange(send, "seq", 4)
+    second = exchange(first, "section", 1)
+    weights = [dec_weight, side, after, far_top, far_bottom]
+    vmem = pl.BlockSpec(memory_space=pltpu.VMEM)
+    spaces = [vmem, vmem] + [pl.BlockSpec(memory_space=pl.ANY)] * 5
+    scratch = [pltpu.VMEM((taps, 4 * depth, width), bf16), pltpu.SemaphoreType.DMA((5,))]
+    (own,) = call(own_kernel, [((rows, width), f32)], [keep, base] + weights, scratch, spaces)
+    (partial,) = call(
+        partner_kernel, [((rows, width), bf16)], [first, second] + weights, scratch, spaces
+    )
+    decoded = own + exchange(partial, "seq", 4).astype(f32)
+    return decoded.astype(bf16)[None]
+
+
 def solution(mesh):
     return jax.shard_map(
-        body,
+        split_body if mesh.shape["seq"] == 8 else body,
         mesh=mesh,
         in_specs=(
             P("groups", "seq", None),

time: 151 us -> 74.6 us (0.49)
  waiting for transfers between devices: 81 us -> 29.8 us
  blocking collectives: 25.2 us -> 0 us
  Pallas kernels: 0 us -> 18.3 us
  between operations: 15 us -> 0.1 us
  starting transfers between devices: 4.96 us -> 15.1 us
  matrix products: 10.6 us -> 1.94 us
  other arithmetic: 10.3 us -> 4.08 us
    all_gather x1 -> x0, waiting for transfers between devices: 64.1 us -> none  [body(): piece = lax.all_gather(dec_weight, 'seq', axis=1, tiled=True)]
    ppermute x2 -> x11, waiting for transfers between devices: 1.35 us -> 29.8 us  [exchange(): return lax.ppermute(values_in, axis, [(i, i ^ mask) for i in range(count)])]
    all_gather x1 -> x0, blocking collectives: 25.2 us -> none  [body(): piece = lax.all_gather(key_values, ('seq', 'section'), axis=1, tiled=True)]
    pallas_call x0 -> x5, Pallas kernels: none -> 18.3 us  [call(): pl.pallas_call(kernel, out_shape=[jax.ShapeDtypeStruct(shape, kind) for s...]
    psum x1 -> x0, waiting for transfers between devices: 15 us -> none  [body(): lax.psum(partial_value.astype(jnp.bfloat16), 'section').astype(jnp.float32)]
    ppermute x2 -> x11, starting transfers between devices: 4.92 us -> 15.1 us  [exchange(): return lax.ppermute(values_in, axis, [(i, i ^ mask) for i in range(count)])]
    dot_general x6 -> x1, matrix products: 10.6 us -> 1.94 us  [split_body(): jnp.dot(normed, query_weight, preferred_element_type=f32).astype(bf16)]
    unnamed x4 -> x0, other arithmetic: 3.74 us -> none
  transfers between devices with their start and end apart: 4 -> 11, of which waited for: 3 -> 5; matrix products, arithmetic and copies ran while one was open for 5% -> 8% of each run, Pallas kernels for 0% -> 16%
where the time goes in v1:
time: 74.6 us; the launch traced here: 74.1 us
  waiting for transfers between devices  29.8 us (40%)
  Pallas kernels  18.3 us (25%)
  starting transfers between devices  15.1 us (20%)
  local copies, waits for them, and re-layouts  4.87 us (7%)
  other arithmetic  4.08 us (5%)
  matrix products  1.94 us (3%)
    ppermute x11, waiting for transfers between devices, exchange(): return lax.ppermute(values_in, axis, [(i, i ^ mask) for i in range(count)])  29.8 us
    pallas_call x5, Pallas kernels, call(): pl.pallas_call(kernel, out_shape=[jax.ShapeDtypeStruct(shape, kind) for s...  18.3 us
    ppermute x11, starting transfers between devices, exchange(): return lax.ppermute(values_in, axis, [(i, i ^ mask) for i in range(count)])  15.1 us
    concatenate x3, other arithmetic, split_body(): jnp.concatenate([messages, exchange(messages, 'seq', mask)], axis=0)  2.49 us
    unnamed x22, local copies, waits for them, and re-layouts  2.24 us
    dot_general x1, matrix products, split_body(): jnp.dot(normed, query_weight, preferred_element_type=f32).astype(bf16)  1.94 us
    broadcast_in_dim x1, other arithmetic, split_body(): return decoded.astype(bf16)[None]  1.59 us
  transfers between devices with their start and end apart: 11, of which 5 were waited for; matrix products, arithmetic and copies ran while one was open for 8% of the time, Pallas kernels for 16%

profile of v1, /device:TPU:0, one launch (start us, length us, event | category | flops | bytes accessed | tf_op | source)
XLA Modules:
  0.0 74.1 jit_solution(14695303179171904713)
XLA Ops:
  0.0 0.0 copy-start
  0.0 1.4 %reshape.12.gain_ref = f32[1,1536]{1,0:T(1,128)} reshape(f32[1536]{0:T(1024)} %param.10) | data formatting | bytes 12288 | tf_op jit(solution)/shard_map/reshape | solution.py:382
  1.4 2.3 %shard_map.91 = (bf16[112,256]{1,0:T(8,128)(2,1)}, bf16[64,1536]{1,0:T(8,128)(2,1)}) custom-call(bf16[128,1536]{1,0:T(8,128)(2,1)} %bitcast.7, f32[1,1536]{1,0:T(1,128)} %reshape.12.gain_ref, bf16[1536,256]{1,0:T(8,128)(2,1)} %weight_ref.1, f32[16,32]{1,0:T(8,128)} %bitcast.13), custom_call_target="tpu_custom_call" | custom-call | tf_op jit(solution)/shard_map/pallas_call | solution.py:145
  3.7 0.0 copy-start.5
  3.7 4.0 %collective-permute-start = (bf16[1,112,256]{2,1,0:T(8,128)(2,1)}, bf16[1,112,256]{2,1,0:T(8,128)(2,1)S(1)}, u32[]{:S(2)}, u32[]{:S(2)}) collective-permute-start(bf16[1,112,256]{2,1,0:T(8,128)(2,1)} %bitcast.9), channel_id=1, source_target_pairs={{0,8},{2,10},{4,12},{6,14},{8,0},{10,2},{12,4},{14,6},{1,9},{3,11}... | collective-permute-start | bytes 172040 | tf_op jit(solution)/shard_map/ppermute | solution.py:139
  7.7 1.5 %collective-permute-start.4 = (bf16[5,192,384]{2,1,0:T(8,128)(2,1)}, bf16[5,192,384]{2,1,0:T(8,128)(2,1)S(1)}, u32[]{:S(2)}, u32[]{:S(2)}) collective-permute-start(bf16[5,192,384]{2,1,0:T(8,128)(2,1)} %w0.3), channel_id=1, source_target_pairs={{0,2},{2,0},{4,6},{6,4},{8,10},{10,8},{12,14},{14,12},{1,3},{3,1},... | collective-permute-start | bytes 2211848 | tf_op jit(solution)/shard_map/ppermute | solution.py:139
  9.2 1.6 %collective-permute-start.5 = (bf16[5,192,384]{2,1,0:T(8,128)(2,1)}, bf16[5,192,384]{2,1,0:T(8,128)(2,1)S(1)}, u32[]{:S(2)}, u32[]{:S(2)}) collective-permute-start(bf16[5,192,384]{2,1,0:T(8,128)(2,1)} %w0.3), channel_id=1, source_target_pairs={{0,4},{2,6},{4,0},{6,2},{8,12},{10,14},{12,8},{14,10},{1,5},{3,7},... | collective-permute-start | bytes 2211848 | tf_op jit(solution)/shard_map/ppermute | solution.py:139
  10.8 0.0 collective-permute-done
  10.8 0.8 %pad_maximum_fusion.2 = bf16[2,112,256]{2,1,0:T(8,128)(2,1)S(1)} fusion(bf16[1,112,256]{2,1,0:T(8,128)(2,1)S(1)} %collective-permute-done, bf16[1,112,256]{2,1,0:T(8,128)(2,1)} %bitcast.10), kind=kLoop, calls=%fused_computation.4 | loop fusion | flops 57344 | bytes 229376 | tf_op jit(solution)/shard_map/concatenate | solution.py:397
  11.7 1.6 %collective-permute-start.1 = (bf16[2,112,256]{2,1,0:T(8,128)(2,1)S(1)}, bf16[2,112,256]{2,1,0:T(8,128)(2,1)S(1)}, u32[]{:S(2)}, u32[]{:S(2)}) collective-permute-start(bf16[2,112,256]{2,1,0:T(8,128)(2,1)S(1)} %pad_maximum_fusion.2), channel_id=1, source_target_pairs={{0,4},{2,6},{4,0},{6,2},{8,12},{10,14},{12,8},{14,10},{1,5},{3,7},... | collective-permute-start | bytes 344072 | tf_op jit(solution)/shard_map/ppermute | solution.py:139
  13.3 16.3 %collective-permute-done.1 = bf16[2,112,256]{2,1,0:T(8,128)(2,1)S(1)} collective-permute-done((bf16[2,112,256]{2,1,0:T(8,128)(2,1)S(1)}, bf16[2,112,256]{2,1,0:T(8,128)(2,1)S(1)}, u32[]{:S(2)}, u32[]{:S(2)}) %collective-permute-start.1) | collective-permute-done | bytes 114720 | tf_op jit(solution)/shard_map/ppermute | solution.py:139
  29.6 0.8 %pad_maximum_fusion.1 = bf16[4,112,256]{2,1,0:T(8,128)(2,1)S(1)} fusion(bf16[2,112,256]{2,1,0:T(8,128)(2,1)S(1)} %collective-permute-done.1, bf16[1,112,256]{2,1,0:T(8,128)(2,1)S(1)} %collective-permute-done, bf16[1,112,256]{2,1,0:T(8,128)(2,1)} %bitcast.11), kind=kLoop, calls=%fused_computation.2 | loop fusion | flops 229376 | bytes 458752 | tf_op jit(solution)/shard_map/concatenate | solution.py:397
  30.4 1.2 %collective-permute-start.2 = (bf16[4,112,256]{2,1,0:T(8,128)(2,1)S(1)}, bf16[4,112,256]{2,1,0:T(8,128)(2,1)S(1)}, u32[]{:S(2)}, u32[]{:S(2)}) collective-permute-start(bf16[4,112,256]{2,1,0:T(8,128)(2,1)S(1)} %pad_maximum_fusion.1), channel_id=1, source_target_pairs={{0,2},{2,0},{4,6},{6,4},{8,10},{10,8},{12,14},{14,12},{1,3},{3,1},... | collective-permute-start | bytes 688136 | tf_op jit(solution)/shard_map/ppermute | solution.py:139
  31.6 0.0 copy-done
  31.6 1.9 %convolution_convert_fusion.query_ref = bf16[64,512]{1,0:T(8,128)(2,1)} fusion(bf16[64,1536]{1,0:T(8,128)(2,1)} %get-tuple-element.12, bf16[1536,512]{1,0:T(8,128)(2,1)S(1)} %copy-done), kind=kOutput, calls=%fused_computation | convolution fusion | flops 100696064 | bytes 1835008 | tf_op jit(solution)/shard_map/dot_general | solution.py:398
  33.5 3.0 %collective-permute-done.2 = bf16[4,112,256]{2,1,0:T(8,128)(2,1)S(1)} collective-permute-done((bf16[4,112,256]{2,1,0:T(8,128)(2,1)S(1)}, bf16[4,112,256]{2,1,0:T(8,128)(2,1)S(1)}, u32[]{:S(2)}, u32[]{:S(2)}) %collective-permute-start.2) | collective-permute-done | bytes 229408 | tf_op jit(solution)/shard_map/ppermute | solution.py:139
  36.5 0.0 copy-done.5
  36.5 0.8 %pad_maximum_fusion.message_ref = bf16[8,112,256]{2,1,0:T(8,128)(2,1)} fusion(bf16[4,112,256]{2,1,0:T(8,128)(2,1)S(1)} %collective-permute-done.2, bf16[2,112,256]{2,1,0:T(8,128)(2,1)S(1)} %collective-permute-done.1, bf16[1,112,256]{2,1,0:T(8,128)(2,1)S(1)} %collective-permute-done, bf16[1,112,256]{2,1,0:T(8,128)(2,1)S(1)} %bitcast.12), kind=kLoop, calls=%fused_computation.1 | loop fusion | flops 688128 | bytes 917504 | tf_op jit(solution)/shard_map/concatenate | solution.py:397
  37.3 0.0 copy-start.9
  37.3 0.0 copy-start.10
  37.3 4.6 %shard_map.92 = (bf16[80,1536]{1,0:T(8,128)(2,1)}, f32[8,1536]{1,0:T(8,128)}) custom-call(bf16[64,512]{1,0:T(8,128)(2,1)} %convolution_convert_fusion.query_ref, bf16[8,112,256]{2,1,0:T(8,128)(2,1)} %pad_maximum_fusion.message_ref, bf16[1536,512]{1,0:T(8,128)(2,1)} %query_weight_ref.1, f32[1,1536]{1,0:T(1,128)} %reshape.12.gain_ref, f32[16,32]{1,0:T(8,128)} %bitcast.14, ...), custom_call_target="tpu_custom_call" | custom-call | tf_op jit(solution)/shard_map/pallas_call | solution.py:145
  42.0 0.0 collective-permute-start.3
  42.0 0.0 collective-permute-done.5.w2
  42.0 0.0 copy-start.2
  42.0 1.6 %collective-permute-start.6 = (bf16[5,96,384]{2,1,0:T(8,128)(2,1)S(1)}, bf16[5,96,384]{2,1,0:T(8,128)(2,1)S(1)}, u32[]{:S(2)}, u32[]{:S(2)}) collective-permute-start(bf16[5,96,384]{2,1,0:T(8,128)(2,1)S(1)} %slice.8), channel_id=1, source_target_pairs={{0,2},{2,0},{4,6},{6,4},{8,10},{10,8},{12,14},{14,12},{1,3},{3,1},... | collective-permute-start | bytes 1105928 | tf_op jit(solution)/shard_map/ppermute | solution.py:139
  43.6 0.0 collective-permute-done.4.w1
  43.6 0.0 copy-start.1
  43.7 0.9 %collective-permute-start.7 = (bf16[5,96,384]{2,1,0:T(8,128)(2,1)S(1)}, bf16[5,96,384]{2,1,0:T(8,128)(2,1)S(1)}, u32[]{:S(2)}, u32[]{:S(2)}) collective-permute-start(bf16[5,96,384]{2,1,0:T(8,128)(2,1)S(1)} %slice.9), channel_id=1, source_target_pairs={{0,4},{2,6},{4,0},{6,2},{8,12},{10,14},{12,8},{14,10},{1,5},{3,7},... | collective-permute-start | bytes 1105928 | tf_op jit(solution)/shard_map/ppermute | solution.py:139
  44.6 0.0 copy-done.9
  44.6 0.6 reshape.14.gain_ref
  45.2 0.0 copy-done.10
  45.2 0.5 reshape.15.dec_bias_ref
  45.7 0.0 collective-permute-done.3.other_ref
  45.7 0.0 copy-start.6
  45.7 0.7 copy-done.6
  46.4 2.8 %shard_map.93 = (bf16[144,768]{1,0:T(8,128)(2,1)}, bf16[144,384]{1,0:T(8,128)(2,1)}, f32[128,384]{1,0:T(8,128)}) custom-call(bf16[128,1536]{1,0:T(8,128)(2,1)} %bitcast.8, f32[8,1536]{1,0:T(8,128)} %get-tuple-element.14.edge_ref, bf16[80,1536]{1,0:T(8,128)(2,1)} %get-tuple-element.15.own_ref, bf16[80,1536]{1,0:T(8,128)(2,1)} %copy-done.6, ...), custom_call_target="tpu_custom_call" | custom-call | tf_op jit(solution)/shard_map/pallas_call | solution.py:145
  49.2 1.7 %collective-permute-start.8 = (bf16[144,384]{1,0:T(8,128)(2,1)}, bf16[144,384]{1,0:T(8,128)(2,1)S(1)}, u32[]{:S(2)}, u32[]{:S(2)}) collective-permute-start(bf16[144,384]{1,0:T(8,128)(2,1)} %get-tuple-element.18), channel_id=1, source_target_pairs={{0,8},{2,10},{4,12},{6,14},{8,0},{10,2},{12,4},{14,6},{1,9},{3,11}... | collective-permute-start | bytes 331784 | tf_op jit(solution)/shard_map/ppermute | solution.py:139
  50.9 6.7 %collective-permute-done.8.first_ref = bf16[144,384]{1,0:T(8,128)(2,1)S(1)} collective-permute-done((bf16[144,384]{1,0:T(8,128)(2,1)}, bf16[144,384]{1,0:T(8,128)(2,1)S(1)}, u32[]{:S(2)}, u32[]{:S(2)}) %collective-permute-start.8) | collective-permute-done | bytes 110624 | tf_op jit(solution)/shard_map/ppermute | solution.py:139
  57.6 0.0 copy-start.7
  57.6 0.0 collective-permute-start.9
  57.6 1.3 %collective-permute-done.9.second_ref = bf16[144,384]{1,0:T(8,128)(2,1)S(1)} collective-permute-done((bf16[144,384]{1,0:T(8,128)(2,1)S(1)}, bf16[144,384]{1,0:T(8,128)(2,1)S(1)}, u32[]{:S(2)}, u32[]{:S(2)}) %collective-permute-start.9) | collective-permute-done | bytes 110624 | tf_op jit(solution)/shard_map/ppermute | solution.py:139
  59.0 0.0 copy-start.8
  59.0 0.0 collective-permute-done.6.w3
  59.0 0.0 copy-start.3
  59.0 0.0 collective-permute-done.7.w4
  59.0 0.0 copy-done.2
  59.0 0.0 copy-done.1
  59.0 0.0 copy-done.7
  59.0 0.6 copy-done.8
  59.6 0.1 copy-done.3
  59.7 0.0 copy-start.4
  59.7 0.7 %copy-done.4 = bf16[5,96,384]{2,1,0:T(8,128)(2,1)} copy-done((bf16[5,96,384]{2,1,0:T(8,128)(2,1)}, bf16[5,96,384]{2,1,0:T(8,128)(2,1)S(1)}, u32[]{:S(2)}) %copy-start.4) | copy-done | bytes 368664
  60.5 4.3 %shard_map.95 = bf16[128,384]{1,0:T(8,128)(2,1)} custom-call(bf16[144,384]{1,0:T(8,128)(2,1)} %copy-done.7, bf16[144,384]{1,0:T(8,128)(2,1)} %copy-done.8, bf16[5,192,384]{2,1,0:T(8,128)(2,1)} %w0.3, bf16[5,192,384]{2,1,0:T(8,128)(2,1)} %copy-done.1, bf16[5,192,384]{2,1,0:T(8,128)(2,1)} %copy-done.2, bf16[5,96,384]{2,1,0:T(8,128)(2,1)} %copy-done.3, ...), custom_call_target="tpu_custom_call" | custom-call | tf_op jit(solution)/shard_map/pallas_call | solution.py:145
  64.8 1.0 %collective-permute-start.10 = (bf16[128,384]{1,0:T(8,128)(2,1)}, bf16[128,384]{1,0:T(8,128)(2,1)S(1)}, u32[]{:S(2)}, u32[]{:S(2)}) collective-permute-start(bf16[128,384]{1,0:T(8,128)(2,1)} %shard_map.95), channel_id=1, source_target_pairs={{0,8},{2,10},{4,12},{6,14},{8,0},{10,2},{12,4},{14,6},{1,9},{3,11}... | collective-permute-start | bytes 294920 | tf_op jit(solution)/shard_map/ppermute | solution.py:139
  65.8 4.3 %shard_map.94 = f32[128,384]{1,0:T(8,128)} custom-call(bf16[144,768]{1,0:T(8,128)(2,1)} %get-tuple-element.16.active_ref, f32[128,384]{1,0:T(8,128)} %get-tuple-element.17.base_ref, bf16[5,192,384]{2,1,0:T(8,128)(2,1)} %w0.3, bf16[5,192,384]{2,1,0:T(8,128)(2,1)} %copy-done.1, bf16[5,192,384]{2,1,0:T(8,128)(2,1)} %copy-done.2, bf16[5,96,384]{2,1,0:T(8,128)(2,1)} %copy-done.3, ...), custom_call_target="tpu_custom_call" | custom-call | tf_op jit(solution)/shard_map/pallas_call | solution.py:145
  70.1 2.5 %collective-permute-done.10 = bf16[128,384]{1,0:T(8,128)(2,1)S(1)} collective-permute-done((bf16[128,384]{1,0:T(8,128)(2,1)}, bf16[128,384]{1,0:T(8,128)(2,1)S(1)}, u32[]{:S(2)}, u32[]{:S(2)}) %collective-permute-start.10) | collective-permute-done | bytes 98336 | tf_op jit(solution)/shard_map/ppermute | solution.py:139
  72.5 1.6 %fusion = bf16[1,128,384]{2,1,0:T(8,128)(2,1)} fusion(f32[128,384]{1,0:T(8,128)} %shard_map.94, bf16[128,384]{1,0:T(8,128)(2,1)S(1)} %collective-permute-done.10), kind=kLoop, calls=%fused_computation.5 | loop fusion | flops 147456 | bytes 393216 | tf_op jit(solution)/shard_map/broadcast_in_dim | solution.py:422
  (2 shorter events, 0.1 us)
Async XLA Ops:
  0.0 31.6 %copy-start = (bf16[1536,512]{1,0:T(8,128)(2,1)S(1)}, bf16[1536,512]{1,0:T(8,128)(2,1)}, u32[]{:S(2)}) copy-start(bf16[1536,512]{1,0:T(8,128)(2,1)} %query_weight_ref.1) | copy-start | bytes 4718596
  3.7 32.8 %copy-start.5 = (bf16[112,256]{1,0:T(8,128)(2,1)S(1)}, bf16[112,256]{1,0:T(8,128)(2,1)}, u32[]{:S(2)}) copy-start(bf16[112,256]{1,0:T(8,128)(2,1)} %get-tuple-element.13) | copy-start | bytes 172036
  3.7 7.1 %collective-permute-start = (bf16[1,112,256]{2,1,0:T(8,128)(2,1)}, bf16[1,112,256]{2,1,0:T(8,128)(2,1)S(1)}, u32[]{:S(2)}, u32[]{:S(2)}) collective-permute-start(bf16[1,112,256]{2,1,0:T(8,128)(2,1)} %bitcast.9), channel_id=1, source_target_pairs={{0,8},{2,10},{4,12},{6,14},{8,0},{10,2},{12,4},{14,6},{1,9},{3,11}... | collective-permute-start | bytes 172040 | tf_op jit(solution)/shard_map/ppermute | solution.py:139
  7.7 35.9 %collective-permute-start.4 = (bf16[5,192,384]{2,1,0:T(8,128)(2,1)}, bf16[5,192,384]{2,1,0:T(8,128)(2,1)S(1)}, u32[]{:S(2)}, u32[]{:S(2)}) collective-permute-start(bf16[5,192,384]{2,1,0:T(8,128)(2,1)} %w0.3), channel_id=1, source_target_pairs={{0,2},{2,0},{4,6},{6,4},{8,10},{10,8},{12,14},{14,12},{1,3},{3,1},... | collective-permute-start | bytes 2211848 | tf_op jit(solution)/shard_map/ppermute | solution.py:139
  9.2 32.7 %collective-permute-start.5 = (bf16[5,192,384]{2,1,0:T(8,128)(2,1)}, bf16[5,192,384]{2,1,0:T(8,128)(2,1)S(1)}, u32[]{:S(2)}, u32[]{:S(2)}) collective-permute-start(bf16[5,192,384]{2,1,0:T(8,128)(2,1)} %w0.3), channel_id=1, source_target_pairs={{0,4},{2,6},{4,0},{6,2},{8,12},{10,14},{12,8},{14,10},{1,5},{3,7},... | collective-permute-start | bytes 2211848 | tf_op jit(solution)/shard_map/ppermute | solution.py:139
  11.7 17.9 %collective-permute-start.1 = (bf16[2,112,256]{2,1,0:T(8,128)(2,1)S(1)}, bf16[2,112,256]{2,1,0:T(8,128)(2,1)S(1)}, u32[]{:S(2)}, u32[]{:S(2)}) collective-permute-start(bf16[2,112,256]{2,1,0:T(8,128)(2,1)S(1)} %pad_maximum_fusion.2), channel_id=1, source_target_pairs={{0,4},{2,6},{4,0},{6,2},{8,12},{10,14},{12,8},{14,10},{1,5},{3,7},... | collective-permute-start | bytes 344072 | tf_op jit(solution)/shard_map/ppermute | solution.py:139
  30.4 6.1 %collective-permute-start.2 = (bf16[4,112,256]{2,1,0:T(8,128)(2,1)S(1)}, bf16[4,112,256]{2,1,0:T(8,128)(2,1)S(1)}, u32[]{:S(2)}, u32[]{:S(2)}) collective-permute-start(bf16[4,112,256]{2,1,0:T(8,128)(2,1)S(1)} %pad_maximum_fusion.1), channel_id=1, source_target_pairs={{0,2},{2,0},{4,6},{6,4},{8,10},{10,8},{12,14},{14,12},{1,3},{3,1},... | collective-permute-start | bytes 688136 | tf_op jit(solution)/shard_map/ppermute | solution.py:139
  37.3 7.2 %copy-start.9 = (f32[1536]{0:T(1024)S(1)}, f32[1536]{0:T(1024)}, u32[]{:S(2)}) copy-start(f32[1536]{0:T(1024)} %param.15) | copy-start | bytes 18436
  37.3 7.8 %copy-start.10 = (f32[384]{0:T(512)S(1)}, f32[384]{0:T(512)}, u32[]{:S(2)}) copy-start(f32[384]{0:T(512)} %param.17) | copy-start | bytes 4612
  42.0 3.7 %collective-permute-start.3 = (bf16[80,1536]{1,0:T(8,128)(2,1)}, bf16[80,1536]{1,0:T(8,128)(2,1)S(1)}, u32[]{:S(2)}, u32[]{:S(2)}) collective-permute-start(bf16[80,1536]{1,0:T(8,128)(2,1)} %get-tuple-element.15.own_ref), channel_id=1, source_target_pairs={{0,1},{1,0},{2,3},{3,2},{4,5},{5,4},{6,7},{7,6},{8,9},{9,8},{10,11... | collective-permute-start | bytes 737288 | tf_op jit(solution)/shard_map/ppermute | solution.py:139
  42.0 17.0 %copy-start.2 = (bf16[5,192,384]{2,1,0:T(8,128)(2,1)}, bf16[5,192,384]{2,1,0:T(8,128)(2,1)S(1)}, u32[]{:S(2)}) copy-start(bf16[5,192,384]{2,1,0:T(8,128)(2,1)S(1)} %collective-permute-done.5.w2) | copy-start | bytes 2211844
  42.0 16.9 %collective-permute-start.6 = (bf16[5,96,384]{2,1,0:T(8,128)(2,1)S(1)}, bf16[5,96,384]{2,1,0:T(8,128)(2,1)S(1)}, u32[]{:S(2)}, u32[]{:S(2)}) collective-permute-start(bf16[5,96,384]{2,1,0:T(8,128)(2,1)S(1)} %slice.8), channel_id=1, source_target_pairs={{0,2},{2,0},{4,6},{6,4},{8,10},{10,8},{12,14},{14,12},{1,3},{3,1},... | collective-permute-start | bytes 1105928 | tf_op jit(solution)/shard_map/ppermute | solution.py:139
  43.6 15.4 %copy-start.1 = (bf16[5,192,384]{2,1,0:T(8,128)(2,1)}, bf16[5,192,384]{2,1,0:T(8,128)(2,1)S(1)}, u32[]{:S(2)}) copy-start(bf16[5,192,384]{2,1,0:T(8,128)(2,1)S(1)} %collective-permute-done.4.w1) | copy-start | bytes 2211844
  43.7 15.3 %collective-permute-start.7 = (bf16[5,96,384]{2,1,0:T(8,128)(2,1)S(1)}, bf16[5,96,384]{2,1,0:T(8,128)(2,1)S(1)}, u32[]{:S(2)}, u32[]{:S(2)}) collective-permute-start(bf16[5,96,384]{2,1,0:T(8,128)(2,1)S(1)} %slice.9), channel_id=1, source_target_pairs={{0,4},{2,6},{4,0},{6,2},{8,12},{10,14},{12,8},{14,10},{1,5},{3,7},... | collective-permute-start | bytes 1105928 | tf_op jit(solution)/shard_map/ppermute | solution.py:139
  45.7 0.7 copy-start.6
  49.2 8.4 %collective-permute-start.8 = (bf16[144,384]{1,0:T(8,128)(2,1)}, bf16[144,384]{1,0:T(8,128)(2,1)S(1)}, u32[]{:S(2)}, u32[]{:S(2)}) collective-permute-start(bf16[144,384]{1,0:T(8,128)(2,1)} %get-tuple-element.18), channel_id=1, source_target_pairs={{0,8},{2,10},{4,12},{6,14},{8,0},{10,2},{12,4},{14,6},{1,9},{3,11}... | collective-permute-start | bytes 331784 | tf_op jit(solution)/shard_map/ppermute | solution.py:139
  57.6 1.4 %copy-start.7 = (bf16[144,384]{1,0:T(8,128)(2,1)}, bf16[144,384]{1,0:T(8,128)(2,1)S(1)}, u32[]{:S(2)}) copy-start(bf16[144,384]{1,0:T(8,128)(2,1)S(1)} %collective-permute-done.8.first_ref) | copy-start | bytes 331780
  57.6 1.3 %collective-permute-start.9 = (bf16[144,384]{1,0:T(8,128)(2,1)S(1)}, bf16[144,384]{1,0:T(8,128)(2,1)S(1)}, u32[]{:S(2)}, u32[]{:S(2)}) collective-permute-start(bf16[144,384]{1,0:T(8,128)(2,1)S(1)} %collective-permute-done.8.first_ref), channel_id=1, source_target_pairs={{0,1},{1,0},{2,3},{3,2},{4,5},{5,4},{6,7},{7,6},{8,9},{9,8},{10,11... | collective-permute-start | bytes 331784 | tf_op jit(solution)/shard_map/ppermute | solution.py:139
  59.0 0.6 copy-start.8
  59.0 0.8 %copy-start.3 = (bf16[5,96,384]{2,1,0:T(8,128)(2,1)}, bf16[5,96,384]{2,1,0:T(8,128)(2,1)S(1)}, u32[]{:S(2)}) copy-start(bf16[5,96,384]{2,1,0:T(8,128)(2,1)S(1)} %collective-permute-done.6.w3) | copy-start | bytes 1105924
  59.7 0.8 %copy-start.4 = (bf16[5,96,384]{2,1,0:T(8,128)(2,1)}, bf16[5,96,384]{2,1,0:T(8,128)(2,1)S(1)}, u32[]{:S(2)}) copy-start(bf16[5,96,384]{2,1,0:T(8,128)(2,1)S(1)} %collective-permute-done.7.w4) | copy-start | bytes 1105924
  64.8 7.7 %collective-permute-start.10 = (bf16[128,384]{1,0:T(8,128)(2,1)}, bf16[128,384]{1,0:T(8,128)(2,1)S(1)}, u32[]{:S(2)}, u32[]{:S(2)}) collective-permute-start(bf16[128,384]{1,0:T(8,128)(2,1)} %shard_map.95), channel_id=1, source_target_pairs={{0,8},{2,10},{4,12},{6,14},{8,0},{10,2},{12,4},{14,6},{1,9},{3,11}... | collective-permute-start | bytes 294920 | tf_op jit(solution)/shard_map/ppermute | solution.py:139

commit v2 on v1

--- a/solution.py
+++ b/solution.py
@@ -131,7 +131,7 @@
 
 ROWS = 80
 MSG = 112
-LIMIT = 56 * 1024 * 1024
+LIMIT = 24 * 1024 * 1024
 
 
 def exchange(values_in, axis, mask):
@@ -139,13 +139,12 @@
     return lax.ppermute(values_in, axis, [(i, i ^ mask) for i in range(count)])
 
 
-def call(kernel, outs, args, scratch=(), spaces=None):
+def call(kernel, outs, args, scratch=()):
     vmem = pl.BlockSpec(memory_space=pltpu.VMEM)
-    specs = [vmem] * len(args) if spaces is None else spaces
     return pl.pallas_call(
         kernel,
         out_shape=[jax.ShapeDtypeStruct(shape, kind) for shape, kind in outs],
-        in_specs=specs,
+        in_specs=[vmem] * len(args),
         out_specs=[vmem] * len(outs),
         scratch_shapes=list(scratch),
         compiler_params=pltpu.CompilerParams(vmem_limit_bytes=LIMIT),
@@ -160,6 +159,10 @@
     return high, middle, low
 
 
+def own_bias(bias_ref):
+    return jnp.concatenate([bias_ref[0, h] for h in range(4)], axis=0)
+
+
 def normalize(wide, gain):
     return wide * lax.rsqrt(jnp.mean(wide * wide, axis=-1, keepdims=True) + 1e-06) * gain
 
@@ -189,7 +192,7 @@
     half = skip_ref.shape[0] // 2
     spread_columns(wide, skip_ref)
     pooled = jnp.maximum(take_rows(wide, 0, half), take_rows(wide, 1, half))
-    normed = normalize(pooled, gain_ref[...]).astype(jnp.bfloat16)
+    normed = normalize(pooled, gain_ref[...][None, :]).astype(jnp.bfloat16)
     normed_ref[...] = normed
     lines[0:half, :] = jnp.dot(normed, weight_ref[...], preferred_element_type=jnp.float32)
     last = skip_ref.shape[0]
@@ -198,7 +201,7 @@
             at = half + 6 * n + k // 2
             lines[at : at + 1, 128 * (k % 2) : 128 * (k % 2) + 128] = wide[k, row : row + 1, :]
     lines[88:MSG, :] = jnp.zeros((MSG - 88, 256), jnp.float32)
-    for n, term in enumerate(split_three(bias_ref[...])):
+    for n, term in enumerate(split_three(own_bias(bias_ref))):
         for h in range(4):
             for k, cell in enumerate((0, 3)):
                 at = 88 + 8 * n + 2 * h + k
@@ -213,14 +216,18 @@
 
 
 def attention_kernel(
-    query_ref, message_ref, query_weight_ref, gain_ref, bias_ref, out_weight_ref, terms_ref, edge_ref
+    query_ref, near_ref, side_ref, query_weight_ref, gain_ref, bias_ref, out_weight_ref, terms_ref, edge_ref
 ):
     me = lax.axis_index("seq")
     count = lax.axis_size("seq")
     low_slot = reverse_bits(me ^ jnp.maximum(me - 1, 0))
     high_slot = reverse_bits(me ^ jnp.minimum(me + 1, count - 1))
-    low = message_ref[low_slot].astype(jnp.float32)
-    high = message_ref[high_slot].astype(jnp.float32)
+
+    def block_of(slot):
+        near = near_ref[slot & 3].astype(jnp.float32)
+        return jnp.where(slot < 4, near, side_ref[slot & 3].astype(jnp.float32))
+
+    low, high = block_of(low_slot), block_of(high_slot)
 
     def line(block, row):
         start = 64 + 6 * row
@@ -239,17 +246,18 @@
         ],
         axis=0,
     )
-    normed = normalize(pooled, gain_ref[...]).astype(jnp.bfloat16)
+    normed = normalize(pooled, gain_ref[...][None, :]).astype(jnp.bfloat16)
     halo_query = jnp.dot(normed, query_weight_ref[...], preferred_element_type=jnp.float32)
     queries = jnp.concatenate([query_ref[...], halo_query.astype(jnp.bfloat16)], axis=0)
-    keys = jnp.concatenate([message_ref[k, 0:64, 0:HEAD] for k in range(8)], axis=0)
-    values = jnp.concatenate([message_ref[k, 0:64, HEAD : 2 * HEAD] for k in range(8)], axis=0)
+    pieces = [ref[k, 0:64, :] for ref in (near_ref, side_ref) for k in range(4)]
+    keys = jnp.concatenate([piece[:, 0:HEAD] for piece in pieces], axis=0)
+    values = jnp.concatenate([piece[:, HEAD : 2 * HEAD] for piece in pieces], axis=0)
     cell = lax.broadcasted_iota(jnp.int32, (32, 512), 0)
     column = lax.broadcasted_iota(jnp.int32, (32, 512), 1)
     wanted = 4 * (reverse_bits(column >> 6) ^ me) + ((column & 63) >> 4)
     spread = jnp.where(cell == wanted, 1.0, 0.0).astype(jnp.bfloat16)
     bias = jnp.zeros((32, 512), jnp.float32)
-    for n, term in enumerate(split_three(bias_ref[...])):
+    for n, term in enumerate(split_three(own_bias(bias_ref))):
         at = 88 + 8 * n
         table = jnp.concatenate(
             [term, low[at : at + 8, 0:32].astype(jnp.bfloat16), high[at : at + 8, 0:32].astype(jnp.bfloat16)],
@@ -286,7 +294,7 @@
     me = lax.axis_index("seq")
     section = lax.axis_index("section")
     upper = me >> 2
-    gain = gain_ref[...]
+    gain = gain_ref[...][None, :]
     spread_columns(wide, skip_ref)
     even = take_rows(wide, 0, 64)
     odd = take_rows(wide, 1, 64)
@@ -319,28 +327,20 @@
     for k in range(3):
         columns = slice(128 * k, 128 * k + 128)
         send_ref[:, columns] = active[(1 - upper) * 6 + section * 3 + k].astype(jnp.bfloat16)
-        base_ref[:, columns] = wide[section * 3 + k] + dec_bias_ref[:, columns]
-
-
-def load_weight(own_ref, side_ref, next_ref, far_top_ref, far_bottom_ref, weight, semaphores):
+        base_ref[:, columns] = wide[section * 3 + k] + dec_bias_ref[columns][None, :]
+
+
+def load_weight(own_ref, side_ref, next_ref, far_first_ref, far_last_ref, weight):
     slot = lax.axis_index("seq") & 3
-    pieces = (
-        (own_ref, slot * 192, 192),
-        (side_ref, (slot ^ 1) * 192, 192),
-        (next_ref, (slot ^ 2) * 192, 192),
-        (far_top_ref, (slot ^ 3) * 192, 96),
-        (far_bottom_ref, (slot ^ 3) * 192 + 96, 96),
-    )
-    copies = [
-        pltpu.make_async_copy(
-            ref, weight.at[:, pl.ds(pl.multiple_of(start, 32), size), :], semaphores.at[n]
-        )
-        for n, (ref, start, size) in enumerate(pieces)
-    ]
-    for copy in copies:
-        copy.start()
-    for copy in copies:
-        copy.wait()
+    split = far_first_ref.shape[0]
+    for relation, ref in enumerate((own_ref, side_ref, next_ref)):
+        start = pl.multiple_of((slot ^ relation) * 192, 64)
+        for tap in range(KW):
+            weight[tap, pl.ds(start, 192), :] = ref[tap]
+    start = pl.multiple_of((slot ^ 3) * 192, 64)
+    for tap in range(KW):
+        piece = far_first_ref[tap] if tap < split else far_last_ref[tap - split]
+        weight[tap, pl.ds(start, 192), :] = piece
 
 
 def shifted_sum(products):
@@ -350,16 +350,16 @@
     return total
 
 
-def own_kernel(active_ref, base_ref, w0, w1, w2, w3, w4, out_ref, weight, semaphores):
-    load_weight(w0, w1, w2, w3, w4, weight, semaphores)
+def own_kernel(active_ref, base_ref, w0, w1, w2, w3, w4, out_ref, weight):
+    load_weight(w0, w1, w2, w3, w4, weight)
     active = active_ref[...]
     out_ref[...] = base_ref[...] + shifted_sum(
         [jnp.dot(active, weight[t], preferred_element_type=jnp.float32) for t in range(KW)]
     )
 
 
-def partner_kernel(first_ref, second_ref, w0, w1, w2, w3, w4, out_ref, weight, semaphores):
-    load_weight(w0, w1, w2, w3, w4, weight, semaphores)
+def partner_kernel(first_ref, second_ref, w0, w1, w2, w3, w4, out_ref, weight):
+    load_weight(w0, w1, w2, w3, w4, weight)
     section = lax.axis_index("section")
     first, second = first_ref[...], second_ref[...]
     near = pl.ds(pl.multiple_of(section * 384, 128), 384)
@@ -379,44 +379,44 @@
     bf16, f32 = jnp.bfloat16, jnp.float32
     skip = skip_in[0]
     rows, channels = skip.shape
-    gain = attn_gain.reshape(1, channels)
-    bias = pair_bias.reshape(16, 32)
     taps, depth, width = dec_weight.shape
-    side = exchange(dec_weight, "seq", 1)
-    after = exchange(dec_weight, "seq", 2)
-    far_top = exchange(after[:, : depth // 2], "seq", 1)
-    far_bottom = exchange(side[:, depth // 2 :], "seq", 2)
     message, normed = call(
         pool_kernel,
         [((MSG, 256), bf16), ((rows // 2, channels), bf16)],
-        [skip, gain, kv_weight, bias],
+        [skip, attn_gain, kv_weight, pair_bias],
         [pltpu.VMEM((channels // 128, rows, 128), f32), pltpu.VMEM((MSG, 256), f32)],
     )
     messages = message[None]
-    for mask in (4, 2, 1):
-        messages = jnp.concatenate([messages, exchange(messages, "seq", mask)], axis=0)
+    messages = jnp.concatenate([messages, exchange(messages, "seq", 4)], axis=0)
+    messages = jnp.concatenate([messages, exchange(messages, "seq", 2)], axis=0)
+    held, messages = lax.optimization_barrier((dec_weight, messages))
+    after = exchange(held, "seq", 2)
+    messages_side = exchange(messages, "seq", 1)
+    held, messages_side = lax.optimization_barrier((held, messages_side))
+    side = exchange(held, "seq", 1)
+    split = (taps + 1) // 2
+    far_first = exchange(after[:split], "seq", 1)
+    far_last = exchange(side[split:], "seq", 2)
     queries = jnp.dot(normed, query_weight, preferred_element_type=f32).astype(bf16)
     terms, edges = call(
         attention_kernel,
         [((ROWS, channels), bf16), ((8, channels), f32)],
-        [queries, messages, query_weight, gain, bias, out_weight],
+        [queries, messages, messages_side, query_weight, attn_gain, pair_bias, out_weight],
     )
     other = exchange(terms, "section", 1)
     keep, send, base = call(
         activate_kernel,
         [((rows + 16, channels // 2), bf16), ((rows + 16, channels // 4), bf16), ((rows, width), f32)],
-        [skip, edges, terms, other, dec_gain.reshape(1, channels), dec_bias.reshape(1, width)],
+        [skip, edges, terms, other, dec_gain, dec_bias],
         [pltpu.VMEM((channels // 128, rows + extra, 128), f32) for extra in (0, 16)],
     )
     first = exchange(send, "seq", 4)
     second = exchange(first, "section", 1)
-    weights = [dec_weight, side, after, far_top, far_bottom]
-    vmem = pl.BlockSpec(memory_space=pltpu.VMEM)
-    spaces = [vmem, vmem] + [pl.BlockSpec(memory_space=pl.ANY)] * 5
-    scratch = [pltpu.VMEM((taps, 4 * depth, width), bf16), pltpu.SemaphoreType.DMA((5,))]
-    (own,) = call(own_kernel, [((rows, width), f32)], [keep, base] + weights, scratch, spaces)
+    weights = [dec_weight, side, after, far_first, far_last]
+    scratch = [pltpu.VMEM((taps, 4 * depth, width), bf16)]
+    (own,) = call(own_kernel, [((rows, width), f32)], [keep, base] + weights, scratch)
     (partial,) = call(
-        partner_kernel, [((rows, width), bf16)], [first, second] + weights, scratch, spaces
+        partner_kernel, [((rows, width), bf16)], [first, second] + weights, scratch
     )
     decoded = own + exchange(partial, "seq", 4).astype(f32)
     return decoded.astype(bf16)[None]

time: 74.6 us -> 62.2 us (0.83)
  Pallas kernels: 18.3 us -> 5.24 us
  waiting for transfers between devices: 29.8 us -> 33.3 us
  starting transfers between devices: 15.1 us -> 18.5 us
  other arithmetic: 4.08 us -> 0.7 us
  matrix products: 1.94 us -> 0.38 us
  local copies, waits for them, and re-layouts: 4.87 us -> 3.75 us
    pallas_call x5, Pallas kernels: 18.3 us -> 5.24 us  [call(): pl.pallas_call(kernel, out_shape=[jax.ShapeDtypeStruct(shape, kind) for s...]
    ppermute x11, waiting for transfers between devices: 29.8 us -> 33.3 us  [exchange(): return lax.ppermute(values_in, axis, [(i, i ^ mask) for i in range(count)])]
    ppermute x11, starting transfers between devices: 15.1 us -> 18.5 us  [exchange(): return lax.ppermute(values_in, axis, [(i, i ^ mask) for i in range(count)])]
    reshape x3 -> x0, local copies, waits for them, and re-layouts: 2.55 us -> none  [the longest x1 1.41 us: split_body(): gain = attn_gain.reshape(1, channels)]
    concatenate x3 -> x2, other arithmetic: 2.49 us -> 0.04 us  [the longest x1 0.03 us: split_body(): messages = jnp.concatenate([messages, exchange(messages, 'seq', 2)], axis=0)]
    dot_general x1, matrix products: 1.94 us -> 0.38 us  [split_body(): jnp.dot(normed, query_weight, preferred_element_type=f32).astype(bf16)]
    unnamed x22 -> x20, local copies, waits for them, and re-layouts: 2.24 us -> 3.67 us
    broadcast_in_dim x1, other arithmetic: 1.59 us -> 0.67 us  [split_body(): return decoded.astype(bf16)[None]]
  transfers between devices with their start and end apart: 11 -> 11, of which waited for: 5 -> 8; matrix products, arithmetic and copies ran while one was open for 8% -> 1% of each run, Pallas kernels for 16% -> 6%
where the time goes in v2:
time: 62.2 us; the launch traced here: 62 us
  waiting for transfers between devices  33.3 us (54%)
  starting transfers between devices  18.5 us (30%)
  Pallas kernels  5.24 us (8%)
  local copies, waits for them, and re-layouts  3.75 us (6%)
  other arithmetic  0.7 us (1%)
    ppermute x11, waiting for transfers between devices, exchange(): return lax.ppermute(values_in, axis, [(i, i ^ mask) for i in range(count)])  33.3 us
    ppermute x11, starting transfers between devices, exchange(): return lax.ppermute(values_in, axis, [(i, i ^ mask) for i in range(count)])  18.5 us
    pallas_call x5, Pallas kernels, call(): pl.pallas_call(kernel, out_shape=[jax.ShapeDtypeStruct(shape, kind) for s...  5.24 us
    unnamed x20, local copies, waits for them, and re-layouts  3.67 us
  transfers between devices with their start and end apart: 11, of which 8 were waited for; matrix products, arithmetic and copies ran while one was open for 1% of the time, Pallas kernels for 6%

profile of v2, /device:TPU:0, one launch (start us, length us, event | category | flops | bytes accessed | tf_op | source)
XLA Modules:
  0.0 62.0 jit_solution(11423516164041480822)
XLA Ops:
  0.0 0.0 copy-start
  0.0 0.0 copy-start.3
  0.0 1.1 %copy-done.3 = bf16[1,128,1536]{2,1,0:T(8,128)(2,1)S(1)} copy-done((bf16[1,128,1536]{2,1,0:T(8,128)(2,1)S(1)}, bf16[1,128,1536]{2,1,0:T(8,128)(2,1)}, u32[]{:S(2)}) %copy-start.3) | copy-done | bytes 393240
  1.1 0.0 copy-start.5
  1.1 1.1 %copy-done.5 = bf16[1536,256]{1,0:T(8,128)(2,1)S(1)} copy-done((bf16[1536,256]{1,0:T(8,128)(2,1)S(1)}, bf16[1536,256]{1,0:T(8,128)(2,1)}, u32[]{:S(2)}) %copy-start.5) | copy-done | bytes 786456
  2.3 0.0 copy-start.6
  2.3 0.7 %copy-done.6 = f32[1536]{0:T(1024)S(1)} copy-done((f32[1536]{0:T(1024)S(1)}, f32[1536]{0:T(1024)}, u32[]{:S(2)}) %copy-start.6) | copy-done | bytes 6168
  2.9 0.0 copy-start.7
  3.0 0.7 %copy-done.7 = f32[1,4,4,32]{3,2,1,0:T(4,128)S(1)} copy-done((f32[1,4,4,32]{3,2,1,0:T(4,128)S(1)}, f32[1,4,4,32]{3,2,1,0:T(4,128)}, u32[]{:S(2)}) %copy-start.7) | copy-done | bytes 2072
  3.6 0.0 copy-start.2
  3.6 0.4 shard_map.91
  4.1 4.1 %collective-permute-start = (bf16[1,112,256]{2,1,0:T(8,128)(2,1)S(1)}, bf16[1,112,256]{2,1,0:T(8,128)(2,1)S(1)}, u32[]{:S(2)}, u32[]{:S(2)}) collective-permute-start(bf16[1,112,256]{2,1,0:T(8,128)(2,1)S(1)} %bitcast.8), channel_id=1, source_target_pairs={{0,8},{2,10},{4,12},{6,14},{8,0},{10,2},{12,4},{14,6},{1,9},{3,11}... | collective-permute-start | bytes 172040 | tf_op jit(solution)/shard_map/ppermute | solution.py:139
  8.2 2.8 %collective-permute-done = bf16[1,112,256]{2,1,0:T(8,128)(2,1)S(1)} collective-permute-done((bf16[1,112,256]{2,1,0:T(8,128)(2,1)S(1)}, bf16[1,112,256]{2,1,0:T(8,128)(2,1)S(1)}, u32[]{:S(2)}, u32[]{:S(2)}) %collective-permute-start) | collective-permute-done | bytes 57376 | tf_op jit(solution)/shard_map/ppermute | solution.py:139
  10.9 1.4 %collective-permute-start.1 = (bf16[2,112,256]{2,1,0:T(8,128)(2,1)S(1)}, bf16[2,112,256]{2,1,0:T(8,128)(2,1)S(1)}, u32[]{:S(2)}, u32[]{:S(2)}) collective-permute-start(bf16[2,112,256]{2,1,0:T(8,128)(2,1)S(1)} %pad_maximum_fusion.1), channel_id=1, source_target_pairs={{0,4},{2,6},{4,0},{6,2},{8,12},{10,14},{12,8},{14,10},{1,5},{3,7},... | collective-permute-start | bytes 344072 | tf_op jit(solution)/shard_map/ppermute | solution.py:139
  12.3 3.5 %collective-permute-done.1 = bf16[2,112,256]{2,1,0:T(8,128)(2,1)S(1)} collective-permute-done((bf16[2,112,256]{2,1,0:T(8,128)(2,1)S(1)}, bf16[2,112,256]{2,1,0:T(8,128)(2,1)S(1)}, u32[]{:S(2)}, u32[]{:S(2)}) %collective-permute-start.1) | collective-permute-done | bytes 114720 | tf_op jit(solution)/shard_map/ppermute | solution.py:139
  15.8 1.8 %collective-permute-start.2 = (bf16[4,112,256]{2,1,0:T(8,128)(2,1)S(1)}, bf16[4,112,256]{2,1,0:T(8,128)(2,1)S(1)}, u32[]{:S(2)}, u32[]{:S(2)}) collective-permute-start(bf16[4,112,256]{2,1,0:T(8,128)(2,1)S(1)} %pad_maximum_fusion.near_ref), channel_id=1, source_target_pairs={{0,2},{2,0},{4,6},{6,4},{8,10},{10,8},{12,14},{14,12},{1,3},{3,1},... | collective-permute-start | bytes 688136 | tf_op jit(solution)/shard_map/ppermute | solution.py:139
  17.6 1.2 %collective-permute-start.5 = (bf16[5,192,384]{2,1,0:T(8,128)(2,1)}, bf16[5,192,384]{2,1,0:T(8,128)(2,1)S(1)}, u32[]{:S(2)}, u32[]{:S(2)}) collective-permute-start(bf16[5,192,384]{2,1,0:T(8,128)(2,1)} %w0.3), channel_id=1, source_target_pairs={{0,4},{2,6},{4,0},{6,2},{8,12},{10,14},{12,8},{14,10},{1,5},{3,7},... | collective-permute-start | bytes 2211848 | tf_op jit(solution)/shard_map/ppermute | solution.py:139
  18.8 4.2 %collective-permute-done.2.side_ref = bf16[4,112,256]{2,1,0:T(8,128)(2,1)S(1)} collective-permute-done((bf16[4,112,256]{2,1,0:T(8,128)(2,1)S(1)}, bf16[4,112,256]{2,1,0:T(8,128)(2,1)S(1)}, u32[]{:S(2)}, u32[]{:S(2)}) %collective-permute-start.2) | collective-permute-done | bytes 229408 | tf_op jit(solution)/shard_map/ppermute | solution.py:139
  23.0 1.9 %collective-permute-start.4 = (bf16[5,192,384]{2,1,0:T(8,128)(2,1)}, bf16[5,192,384]{2,1,0:T(8,128)(2,1)S(1)}, u32[]{:S(2)}, u32[]{:S(2)}) collective-permute-start(bf16[5,192,384]{2,1,0:T(8,128)(2,1)} %w0.3), channel_id=1, source_target_pairs={{0,2},{2,0},{4,6},{6,4},{8,10},{10,8},{12,14},{14,12},{1,3},{3,1},... | collective-permute-start | bytes 2211848 | tf_op jit(solution)/shard_map/ppermute | solution.py:139
  24.9 0.0 copy-done
  24.9 0.4 convolution_convert_fusion.query_ref
  25.3 0.0 copy-done.2
  25.3 0.0 copy-start.8
  25.3 0.0 copy-start.9
  25.4 1.9 %shard_map.92 = (bf16[80,1536]{1,0:T(8,128)(2,1)S(1)}, f32[8,1536]{1,0:T(8,128)S(1)}) custom-call(bf16[64,512]{1,0:T(8,128)(2,1)S(1)} %convolution_convert_fusion.query_ref, bf16[4,112,256]{2,1,0:T(8,128)(2,1)S(1)} %pad_maximum_fusion.near_ref, bf16[4,112,256]{2,1,0:T(8,128)(2,1)S(1)} %collective-permute-done.2.side_ref, bf16[1536,512]{1,0:T(8,128)(2,1)S(1)} %copy-done, ...), custom_call_target="tpu_custom_call" | custom-call | tf_op jit(solution)/shard_map/pallas_call | solution.py:144
  27.2 0.0 copy-start.4
  27.2 0.0 copy-start.1
  27.2 0.1 collective-permute-start.3
  27.3 5.7 %collective-permute-done.5.w2 = bf16[5,192,384]{2,1,0:T(8,128)(2,1)S(1)} collective-permute-done((bf16[5,192,384]{2,1,0:T(8,128)(2,1)}, bf16[5,192,384]{2,1,0:T(8,128)(2,1)S(1)}, u32[]{:S(2)}, u32[]{:S(2)}) %collective-permute-start.5) | collective-permute-done | bytes 737312 | tf_op jit(solution)/shard_map/ppermute | solution.py:139
  33.0 0.6 collective-permute-start.6
  33.6 8.9 %collective-permute-done.4.w1 = bf16[5,192,384]{2,1,0:T(8,128)(2,1)S(1)} collective-permute-done((bf16[5,192,384]{2,1,0:T(8,128)(2,1)}, bf16[5,192,384]{2,1,0:T(8,128)(2,1)S(1)}, u32[]{:S(2)}, u32[]{:S(2)}) %collective-permute-start.4) | collective-permute-done | bytes 737312 | tf_op jit(solution)/shard_map/ppermute | solution.py:139
  42.5 1.1 %collective-permute-start.7 = (bf16[2,192,384]{2,1,0:T(8,128)(2,1)S(1)}, bf16[2,192,384]{2,1,0:T(8,128)(2,1)S(1)}, u32[]{:S(2)}, u32[]{:S(2)}) collective-permute-start(bf16[2,192,384]{2,1,0:T(8,128)(2,1)S(1)} %slice.9), channel_id=1, source_target_pairs={{0,4},{2,6},{4,0},{6,2},{8,12},{10,14},{12,8},{14,10},{1,5},{3,7},... | collective-permute-start | bytes 884744 | tf_op jit(solution)/shard_map/ppermute | solution.py:139
  43.6 0.0 collective-permute-done.3.other_ref
  43.6 0.0 copy-done.8
  43.6 0.0 copy-done.9
  43.6 0.0 copy-done.4
  43.6 0.7 %shard_map.93 = (bf16[144,768]{1,0:T(8,128)(2,1)S(1)}, bf16[144,384]{1,0:T(8,128)(2,1)S(1)}, f32[128,384]{1,0:T(8,128)S(1)}) custom-call(bf16[128,1536]{1,0:T(8,128)(2,1)S(1)} %bitcast.7, f32[8,1536]{1,0:T(8,128)S(1)} %get-tuple-element.21.edge_ref, bf16[80,1536]{1,0:T(8,128)(2,1)S(1)} %get-tuple-element.22.own_ref, ...), custom_call_target="tpu_custom_call" | custom-call | tf_op jit(solution)/shard_map/pallas_call | solution.py:144
  44.4 3.4 %collective-permute-start.8 = (bf16[144,384]{1,0:T(8,128)(2,1)S(1)}, bf16[144,384]{1,0:T(8,128)(2,1)S(1)}, u32[]{:S(2)}, u32[]{:S(2)}) collective-permute-start(bf16[144,384]{1,0:T(8,128)(2,1)S(1)} %get-tuple-element.26), channel_id=1, source_target_pairs={{0,8},{2,10},{4,12},{6,14},{8,0},{10,2},{12,4},{14,6},{1,9},{3,11}... | collective-permute-start | bytes 331784 | tf_op jit(solution)/shard_map/ppermute | solution.py:139
  47.8 2.7 %collective-permute-done.8.first_ref = bf16[144,384]{1,0:T(8,128)(2,1)S(1)} collective-permute-done((bf16[144,384]{1,0:T(8,128)(2,1)S(1)}, bf16[144,384]{1,0:T(8,128)(2,1)S(1)}, u32[]{:S(2)}, u32[]{:S(2)}) %collective-permute-start.8) | collective-permute-done | bytes 110624 | tf_op jit(solution)/shard_map/ppermute | solution.py:139
  50.5 0.0 collective-permute-start.9
  50.5 1.3 %collective-permute-done.9.second_ref = bf16[144,384]{1,0:T(8,128)(2,1)S(1)} collective-permute-done((bf16[144,384]{1,0:T(8,128)(2,1)S(1)}, bf16[144,384]{1,0:T(8,128)(2,1)S(1)}, u32[]{:S(2)}, u32[]{:S(2)}) %collective-permute-start.9) | collective-permute-done | bytes 110624 | tf_op jit(solution)/shard_map/ppermute | solution.py:139
  51.9 0.0 collective-permute-done.6.w3
  51.9 0.0 collective-permute-done.7.w4
  51.9 0.0 copy-done.1
  51.9 1.2 %shard_map.95 = bf16[128,384]{1,0:T(8,128)(2,1)S(1)} custom-call(bf16[144,384]{1,0:T(8,128)(2,1)S(1)} %collective-permute-done.8.first_ref, bf16[144,384]{1,0:T(8,128)(2,1)S(1)} %collective-permute-done.9.second_ref, bf16[5,192,384]{2,1,0:T(8,128)(2,1)S(1)} %copy-done.1, bf16[5,192,384]{2,1,0:T(8,128)(2,1)S(1)} %collective-permute-done.4.w1, ...), custom_call_target="tpu_custom_call" | custom-call | tf_op jit(solution)/shard_map/pallas_call | solution.py:144
  53.1 3.0 %collective-permute-start.10 = (bf16[128,384]{1,0:T(8,128)(2,1)S(1)}, bf16[128,384]{1,0:T(8,128)(2,1)S(1)}, u32[]{:S(2)}, u32[]{:S(2)}) collective-permute-start(bf16[128,384]{1,0:T(8,128)(2,1)S(1)} %shard_map.95), channel_id=1, source_target_pairs={{0,8},{2,10},{4,12},{6,14},{8,0},{10,2},{12,4},{14,6},{1,9},{3,11}... | collective-permute-start | bytes 294920 | tf_op jit(solution)/shard_map/ppermute | solution.py:139
  56.1 1.0 %shard_map.94 = f32[128,384]{1,0:T(8,128)S(1)} custom-call(bf16[144,768]{1,0:T(8,128)(2,1)S(1)} %get-tuple-element.23.active_ref, f32[128,384]{1,0:T(8,128)S(1)} %get-tuple-element.24.base_ref, bf16[5,192,384]{2,1,0:T(8,128)(2,1)S(1)} %copy-done.1, bf16[5,192,384]{2,1,0:T(8,128)(2,1)S(1)} %collective-permute-done.4.w1, ...), custom_call_target="tpu_custom_call" | custom-call | tf_op jit(solution)/shard_map/pallas_call | solution.py:144
  57.1 4.2 %collective-permute-done.10 = bf16[128,384]{1,0:T(8,128)(2,1)S(1)} collective-permute-done((bf16[128,384]{1,0:T(8,128)(2,1)S(1)}, bf16[128,384]{1,0:T(8,128)(2,1)S(1)}, u32[]{:S(2)}, u32[]{:S(2)}) %collective-permute-start.10) | collective-permute-done | bytes 98336 | tf_op jit(solution)/shard_map/ppermute | solution.py:139
  61.3 0.7 %fusion = bf16[1,128,384]{2,1,0:T(8,128)(2,1)} fusion(f32[128,384]{1,0:T(8,128)S(1)} %shard_map.94, bf16[128,384]{1,0:T(8,128)(2,1)S(1)} %collective-permute-done.10), kind=kLoop, calls=%fused_computation.4 | loop fusion | flops 147456 | bytes 393216 | tf_op jit(solution)/shard_map/broadcast_in_dim | solution.py:422
  (4 shorter events, 0.1 us)
Async XLA Ops:
  0.0 24.9 %copy-start = (bf16[1536,512]{1,0:T(8,128)(2,1)S(1)}, bf16[1536,512]{1,0:T(8,128)(2,1)}, u32[]{:S(2)}) copy-start(bf16[1536,512]{1,0:T(8,128)(2,1)} %query_weight_ref.1) | copy-start | bytes 4718596
  0.0 1.1 %copy-start.3 = (bf16[1,128,1536]{2,1,0:T(8,128)(2,1)S(1)}, bf16[1,128,1536]{2,1,0:T(8,128)(2,1)}, u32[]{:S(2)}) copy-start(bf16[1,128,1536]{2,1,0:T(8,128)(2,1)} %param.9) | copy-start | bytes 1179652
  1.1 1.1 %copy-start.5 = (bf16[1536,256]{1,0:T(8,128)(2,1)S(1)}, bf16[1536,256]{1,0:T(8,128)(2,1)}, u32[]{:S(2)}) copy-start(bf16[1536,256]{1,0:T(8,128)(2,1)} %weight_ref.1) | copy-start | bytes 2359300
  2.3 0.7 %copy-start.6 = (f32[1536]{0:T(1024)S(1)}, f32[1536]{0:T(1024)}, u32[]{:S(2)}) copy-start(f32[1536]{0:T(1024)} %gain_ref.4) | copy-start | bytes 18436
  2.9 0.7 %copy-start.7 = (f32[1,4,4,32]{3,2,1,0:T(4,128)S(1)}, f32[1,4,4,32]{3,2,1,0:T(4,128)}, u32[]{:S(2)}) copy-start(f32[1,4,4,32]{3,2,1,0:T(4,128)} %bias_ref.3) | copy-start | bytes 6148
  3.6 21.7 %copy-start.2 = (bf16[512,1536]{1,0:T(8,128)(2,1)S(1)}, bf16[512,1536]{1,0:T(8,128)(2,1)}, u32[]{:S(2)}) copy-start(bf16[512,1536]{1,0:T(8,128)(2,1)} %out_weight_ref.1) | copy-start | bytes 4718596
  4.1 6.9 %collective-permute-start = (bf16[1,112,256]{2,1,0:T(8,128)(2,1)S(1)}, bf16[1,112,256]{2,1,0:T(8,128)(2,1)S(1)}, u32[]{:S(2)}, u32[]{:S(2)}) collective-permute-start(bf16[1,112,256]{2,1,0:T(8,128)(2,1)S(1)} %bitcast.8), channel_id=1, source_target_pairs={{0,8},{2,10},{4,12},{6,14},{8,0},{10,2},{12,4},{14,6},{1,9},{3,11}... | collective-permute-start | bytes 172040 | tf_op jit(solution)/shard_map/ppermute | solution.py:139
  10.9 4.9 %collective-permute-start.1 = (bf16[2,112,256]{2,1,0:T(8,128)(2,1)S(1)}, bf16[2,112,256]{2,1,0:T(8,128)(2,1)S(1)}, u32[]{:S(2)}, u32[]{:S(2)}) collective-permute-start(bf16[2,112,256]{2,1,0:T(8,128)(2,1)S(1)} %pad_maximum_fusion.1), channel_id=1, source_target_pairs={{0,4},{2,6},{4,0},{6,2},{8,12},{10,14},{12,8},{14,10},{1,5},{3,7},... | collective-permute-start | bytes 344072 | tf_op jit(solution)/shard_map/ppermute | solution.py:139
  15.8 7.2 %collective-permute-start.2 = (bf16[4,112,256]{2,1,0:T(8,128)(2,1)S(1)}, bf16[4,112,256]{2,1,0:T(8,128)(2,1)S(1)}, u32[]{:S(2)}, u32[]{:S(2)}) collective-permute-start(bf16[4,112,256]{2,1,0:T(8,128)(2,1)S(1)} %pad_maximum_fusion.near_ref), channel_id=1, source_target_pairs={{0,2},{2,0},{4,6},{6,4},{8,10},{10,8},{12,14},{14,12},{1,3},{3,1},... | collective-permute-start | bytes 688136 | tf_op jit(solution)/shard_map/ppermute | solution.py:139
  17.6 15.4 %collective-permute-start.5 = (bf16[5,192,384]{2,1,0:T(8,128)(2,1)}, bf16[5,192,384]{2,1,0:T(8,128)(2,1)S(1)}, u32[]{:S(2)}, u32[]{:S(2)}) collective-permute-start(bf16[5,192,384]{2,1,0:T(8,128)(2,1)} %w0.3), channel_id=1, source_target_pairs={{0,4},{2,6},{4,0},{6,2},{8,12},{10,14},{12,8},{14,10},{1,5},{3,7},... | collective-permute-start | bytes 2211848 | tf_op jit(solution)/shard_map/ppermute | solution.py:139
  23.0 19.4 %collective-permute-start.4 = (bf16[5,192,384]{2,1,0:T(8,128)(2,1)}, bf16[5,192,384]{2,1,0:T(8,128)(2,1)S(1)}, u32[]{:S(2)}, u32[]{:S(2)}) collective-permute-start(bf16[5,192,384]{2,1,0:T(8,128)(2,1)} %w0.3), channel_id=1, source_target_pairs={{0,2},{2,0},{4,6},{6,4},{8,10},{10,8},{12,14},{14,12},{1,3},{3,1},... | collective-permute-start | bytes 2211848 | tf_op jit(solution)/shard_map/ppermute | solution.py:139
  25.3 18.3 %copy-start.8 = (f32[1536]{0:T(1024)S(1)}, f32[1536]{0:T(1024)}, u32[]{:S(2)}) copy-start(f32[1536]{0:T(1024)} %gain_ref.5) | copy-start | bytes 18436
  25.3 18.3 %copy-start.9 = (f32[384]{0:T(512)S(1)}, f32[384]{0:T(512)}, u32[]{:S(2)}) copy-start(f32[384]{0:T(512)} %dec_bias_ref.1) | copy-start | bytes 4612
  27.2 16.4 %copy-start.4 = (bf16[1,128,1536]{2,1,0:T(8,128)(2,1)S(1)}, bf16[1,128,1536]{2,1,0:T(8,128)(2,1)}, u32[]{:S(2)}) copy-start(bf16[1,128,1536]{2,1,0:T(8,128)(2,1)} %param.9) | copy-start | bytes 1179652
  27.2 24.6 %copy-start.1 = (bf16[5,192,384]{2,1,0:T(8,128)(2,1)S(1)}, bf16[5,192,384]{2,1,0:T(8,128)(2,1)}, u32[]{:S(2)}) copy-start(bf16[5,192,384]{2,1,0:T(8,128)(2,1)} %w0.3) | copy-start | bytes 2211844
  27.2 16.4 %collective-permute-start.3 = (bf16[80,1536]{1,0:T(8,128)(2,1)S(1)}, bf16[80,1536]{1,0:T(8,128)(2,1)S(1)}, u32[]{:S(2)}, u32[]{:S(2)}) collective-permute-start(bf16[80,1536]{1,0:T(8,128)(2,1)S(1)} %get-tuple-element.22.own_ref), channel_id=1, source_target_pairs={{0,1},{1,0},{2,3},{3,2},{4,5},{5,4},{6,7},{7,6},{8,9},{9,8},{10,11... | collective-permute-start | bytes 737288 | tf_op jit(solution)/shard_map/ppermute | solution.py:139
  33.0 18.8 %collective-permute-start.6 = (bf16[3,192,384]{2,1,0:T(8,128)(2,1)S(1)}, bf16[3,192,384]{2,1,0:T(8,128)(2,1)S(1)}, u32[]{:S(2)}, u32[]{:S(2)}) collective-permute-start(bf16[3,192,384]{2,1,0:T(8,128)(2,1)S(1)} %slice.8), channel_id=1, source_target_pairs={{0,2},{2,0},{4,6},{6,4},{8,10},{10,8},{12,14},{14,12},{1,3},{3,1},... | collective-permute-start | bytes 1327112 | tf_op jit(solution)/shard_map/ppermute | solution.py:139
  42.5 9.4 %collective-permute-start.7 = (bf16[2,192,384]{2,1,0:T(8,128)(2,1)S(1)}, bf16[2,192,384]{2,1,0:T(8,128)(2,1)S(1)}, u32[]{:S(2)}, u32[]{:S(2)}) collective-permute-start(bf16[2,192,384]{2,1,0:T(8,128)(2,1)S(1)} %slice.9), channel_id=1, source_target_pairs={{0,4},{2,6},{4,0},{6,2},{8,12},{10,14},{12,8},{14,10},{1,5},{3,7},... | collective-permute-start | bytes 884744 | tf_op jit(solution)/shard_map/ppermute | solution.py:139
  44.4 6.2 %collective-permute-start.8 = (bf16[144,384]{1,0:T(8,128)(2,1)S(1)}, bf16[144,384]{1,0:T(8,128)(2,1)S(1)}, u32[]{:S(2)}, u32[]{:S(2)}) collective-permute-start(bf16[144,384]{1,0:T(8,128)(2,1)S(1)} %get-tuple-element.26), channel_id=1, source_target_pairs={{0,8},{2,10},{4,12},{6,14},{8,0},{10,2},{12,4},{14,6},{1,9},{3,11}... | collective-permute-start | bytes 331784 | tf_op jit(solution)/shard_map/ppermute | solution.py:139
  50.5 1.3 %collective-permute-start.9 = (bf16[144,384]{1,0:T(8,128)(2,1)S(1)}, bf16[144,384]{1,0:T(8,128)(2,1)S(1)}, u32[]{:S(2)}, u32[]{:S(2)}) collective-permute-start(bf16[144,384]{1,0:T(8,128)(2,1)S(1)} %collective-permute-done.8.first_ref), channel_id=1, source_target_pairs={{0,1},{1,0},{2,3},{3,2},{4,5},{5,4},{6,7},{7,6},{8,9},{9,8},{10,11... | collective-permute-start | bytes 331784 | tf_op jit(solution)/shard_map/ppermute | solution.py:139
  53.1 8.2 %collective-permute-start.10 = (bf16[128,384]{1,0:T(8,128)(2,1)S(1)}, bf16[128,384]{1,0:T(8,128)(2,1)S(1)}, u32[]{:S(2)}, u32[]{:S(2)}) collective-permute-start(bf16[128,384]{1,0:T(8,128)(2,1)S(1)} %shard_map.95), channel_id=1, source_target_pairs={{0,8},{2,10},{4,12},{6,14},{8,0},{10,2},{12,4},{14,6},{1,9},{3,11}... | collective-permute-start | bytes 294920 | tf_op jit(solution)/shard_map/ppermute | solution.py:139

commit v3 on v2

--- a/solution.py
+++ b/solution.py
@@ -139,15 +139,15 @@
     return lax.ppermute(values_in, axis, [(i, i ^ mask) for i in range(count)])
 
 
-def call(kernel, outs, args, scratch=()):
+def call(kernel, outs, args, scratch=(), spaces=None, limit=LIMIT):
     vmem = pl.BlockSpec(memory_space=pltpu.VMEM)
     return pl.pallas_call(
         kernel,
         out_shape=[jax.ShapeDtypeStruct(shape, kind) for shape, kind in outs],
-        in_specs=[vmem] * len(args),
+        in_specs=[vmem] * len(args) if spaces is None else spaces,
         out_specs=[vmem] * len(outs),
         scratch_shapes=list(scratch),
-        compiler_params=pltpu.CompilerParams(vmem_limit_bytes=LIMIT),
+        compiler_params=pltpu.CompilerParams(vmem_limit_bytes=limit),
     )(*args)
 
 
@@ -188,12 +188,46 @@
         wide[k, pl.ds(start, values_in.shape[0], stride=2), :] = values_in[:, 128 * k : 128 * k + 128]
 
 
-def pool_kernel(skip_ref, gain_ref, weight_ref, bias_ref, message_ref, normed_ref, wide, lines):
+def pool_kernel(
+    skip_hbm,
+    gain_hbm,
+    weight_hbm,
+    bias_hbm,
+    dec_hbm,
+    message_ref,
+    normed_ref,
+    piece_ref,
+    skip_ref,
+    gain_ref,
+    weight_ref,
+    bias_ref,
+    wide,
+    lines,
+    semaphores,
+):
+    group = lax.axis_index("groups")
+    pieces = dec_hbm.shape[0] // 2
+    pairs = (
+        (skip_hbm, skip_ref),
+        (gain_hbm, gain_ref),
+        (bias_hbm, bias_ref),
+        (weight_hbm, weight_ref),
+        (dec_hbm.at[pl.ds(group * pieces, pieces)], piece_ref),
+    )
+    copies = [
+        pltpu.make_async_copy(source, target, semaphores.at[n])
+        for n, (source, target) in enumerate(pairs)
+    ]
+    for copy in copies:
+        copy.start()
+    for copy in copies[:3]:
+        copy.wait()
     half = skip_ref.shape[0] // 2
     spread_columns(wide, skip_ref)
     pooled = jnp.maximum(take_rows(wide, 0, half), take_rows(wide, 1, half))
     normed = normalize(pooled, gain_ref[...][None, :]).astype(jnp.bfloat16)
     normed_ref[...] = normed
+    copies[3].wait()
     lines[0:half, :] = jnp.dot(normed, weight_ref[...], preferred_element_type=jnp.float32)
     last = skip_ref.shape[0]
     for n, row in enumerate((0, 1, last - 2, last - 1)):
@@ -209,6 +243,7 @@
                     jnp.float32
                 )
     message_ref[...] = lines[...].astype(jnp.bfloat16)
+    copies[4].wait()
 
 
 def reverse_bits(value):
@@ -330,17 +365,21 @@
         base_ref[:, columns] = wide[section * 3 + k] + dec_bias_ref[columns][None, :]
 
 
-def load_weight(own_ref, side_ref, next_ref, far_first_ref, far_last_ref, weight):
+def load_weight(own_ref, remote_refs, weight):
     slot = lax.axis_index("seq") & 3
-    split = far_first_ref.shape[0]
-    for relation, ref in enumerate((own_ref, side_ref, next_ref)):
-        start = pl.multiple_of((slot ^ relation) * 192, 64)
-        for tap in range(KW):
-            weight[tap, pl.ds(start, 192), :] = ref[tap]
-    start = pl.multiple_of((slot ^ 3) * 192, 64)
-    for tap in range(KW):
-        piece = far_first_ref[tap] if tap < split else far_last_ref[tap - split]
-        weight[tap, pl.ds(start, 192), :] = piece
+    group = lax.axis_index("groups")
+    for n in range(2 * KW):
+        weight[(n // 2) * 8 + 2 * slot + n % 2] = own_ref[n]
+    for n, ref in enumerate(remote_refs):
+        block = slot ^ (n // 2 + 1)
+        first = KW * (group if n % 2 == 0 else 1 - group)
+        for k in range(KW):
+            chunk = first + k
+            weight[(chunk // 2) * 8 + 2 * block + chunk % 2] = ref[k]
+
+
+def tap_weight(weight, tap, start, size):
+    return weight[pl.ds(8 * tap + start, size)].reshape(size * weight.shape[1], weight.shape[2])
 
 
 def shifted_sum(products):
@@ -350,24 +389,26 @@
     return total
 
 
-def own_kernel(active_ref, base_ref, w0, w1, w2, w3, w4, out_ref, weight):
-    load_weight(w0, w1, w2, w3, w4, weight)
+def own_kernel(active_ref, base_ref, w0, w1, w2, w3, w4, w5, w6, out_ref, weight):
+    load_weight(w0, (w1, w2, w3, w4, w5, w6), weight)
     active = active_ref[...]
     out_ref[...] = base_ref[...] + shifted_sum(
-        [jnp.dot(active, weight[t], preferred_element_type=jnp.float32) for t in range(KW)]
-    )
-
-
-def partner_kernel(first_ref, second_ref, w0, w1, w2, w3, w4, out_ref, weight):
-    load_weight(w0, w1, w2, w3, w4, weight)
+        [
+            jnp.dot(active, tap_weight(weight, t, 0, 8), preferred_element_type=jnp.float32)
+            for t in range(KW)
+        ]
+    )
+
+
+def partner_kernel(first_ref, second_ref, w0, w1, w2, w3, w4, w5, w6, out_ref, weight):
+    load_weight(w0, (w1, w2, w3, w4, w5, w6), weight)
     section = lax.axis_index("section")
     first, second = first_ref[...], second_ref[...]
-    near = pl.ds(pl.multiple_of(section * 384, 128), 384)
-    far = pl.ds(pl.multiple_of((1 - section) * 384, 128), 384)
+    near, far = 4 * section, 4 * (1 - section)
     out_ref[...] = shifted_sum(
         [
-            jnp.dot(first, weight[t, near, :], preferred_element_type=jnp.float32)
-            + jnp.dot(second, weight[t, far, :], preferred_element_type=jnp.float32)
+            jnp.dot(first, tap_weight(weight, t, near, 4), preferred_element_type=jnp.float32)
+            + jnp.dot(second, tap_weight(weight, t, far, 4), preferred_element_type=jnp.float32)
             for t in range(KW)
         ]
     ).astype(jnp.bfloat16)
@@ -380,23 +421,30 @@
     skip = skip_in[0]
     rows, channels = skip.shape
     taps, depth, width = dec_weight.shape
-    message, normed = call(
+    chunks = dec_weight.reshape(2 * taps, depth // 2, width)
+    message, normed, piece = call(
         pool_kernel,
-        [((MSG, 256), bf16), ((rows // 2, channels), bf16)],
-        [skip, attn_gain, kv_weight, pair_bias],
-        [pltpu.VMEM((channels // 128, rows, 128), f32), pltpu.VMEM((MSG, 256), f32)],
+        [((MSG, 256), bf16), ((rows // 2, channels), bf16), ((taps, depth // 2, width), bf16)],
+        [skip, attn_gain, kv_weight, pair_bias, chunks],
+        [
+            pltpu.VMEM((rows, channels), bf16),
+            pltpu.VMEM((channels,), f32),
+            pltpu.VMEM(kv_weight.shape, bf16),
+            pltpu.VMEM(pair_bias.shape, f32),
+            pltpu.VMEM((channels // 128, rows, 128), f32),
+            pltpu.VMEM((MSG, 256), f32),
+            pltpu.SemaphoreType.DMA((5,)),
+        ],
+        [pl.BlockSpec(memory_space=pl.ANY)] * 5,
+        60 * 1024 * 1024,
     )
     messages = message[None]
     messages = jnp.concatenate([messages, exchange(messages, "seq", 4)], axis=0)
+    side = exchange(piece, "seq", 1)
     messages = jnp.concatenate([messages, exchange(messages, "seq", 2)], axis=0)
-    held, messages = lax.optimization_barrier((dec_weight, messages))
-    after = exchange(held, "seq", 2)
+    after = exchange(lax.optimization_barrier((piece, messages))[0], "seq", 2)
     messages_side = exchange(messages, "seq", 1)
-    held, messages_side = lax.optimization_barrier((held, messages_side))
-    side = exchange(held, "seq", 1)
-    split = (taps + 1) // 2
-    far_first = exchange(after[:split], "seq", 1)
-    far_last = exchange(side[split:], "seq", 2)
+    side_rest = exchange(lax.optimization_barrier((side, messages))[0], "groups", 1)
     queries = jnp.dot(normed, query_weight, preferred_element_type=f32).astype(bf16)
     terms, edges = call(
         attention_kernel,
@@ -411,9 +459,13 @@
         [pltpu.VMEM((channels // 128, rows + extra, 128), f32) for extra in (0, 16)],
     )
     first = exchange(send, "seq", 4)
+    held = lax.optimization_barrier((after, send))[0]
+    after_rest = exchange(held, "groups", 1)
+    far = exchange(held, "seq", 1)
+    far_rest = exchange(lax.optimization_barrier((side_rest, send))[0], "seq", 2)
     second = exchange(first, "section", 1)
-    weights = [dec_weight, side, after, far_first, far_last]
-    scratch = [pltpu.VMEM((taps, 4 * depth, width), bf16)]
+    weights = [chunks, side, side_rest, after, after_rest, far, far_rest]
+    scratch = [pltpu.VMEM((8 * taps, depth // 2, width), bf16)]
     (own,) = call(own_kernel, [((rows, width), f32)], [keep, base] + weights, scratch)
     (partial,) = call(
         partner_kernel, [((rows, width), bf16)], [first, second] + weights, scratch

time: 62.2 us -> 51.1 us (0.82)
  waiting for transfers between devices: 33.3 us -> 17 us
  starting transfers between devices: 18.5 us -> 22.5 us
  local copies, waits for them, and re-layouts: 3.75 us -> 0.05 us
  Pallas kernels: 5.24 us -> 7.38 us
  other arithmetic: 0.7 us -> 2.34 us
  matrix products: 0.38 us -> 1.31 us
    ppermute x11 -> x13, waiting for transfers between devices: 33.3 us -> 17 us  [exchange(): return lax.ppermute(values_in, axis, [(i, i ^ mask) for i in range(count)])]
    ppermute x11 -> x13, starting transfers between devices: 18.5 us -> 22.5 us  [exchange(): return lax.ppermute(values_in, axis, [(i, i ^ mask) for i in range(count)])]
    unnamed x20 -> x16, local copies, waits for them, and re-layouts: 3.67 us -> 0.05 us
    pallas_call x5, Pallas kernels: 5.24 us -> 7.38 us  [call(): pl.pallas_call(kernel, out_shape=[jax.ShapeDtypeStruct(shape, kind) for s...]
    dot_general x1, matrix products: 0.38 us -> 1.31 us  [split_body(): jnp.dot(normed, query_weight, preferred_element_type=f32).astype(bf16)]
    concatenate x1, other arithmetic: 0.01 us -> 0.83 us  [split_body(): messages = jnp.concatenate([messages, exchange(messages, 'seq', 4)], axis=0)]
    concatenate x1, other arithmetic: 0.03 us -> 0.84 us  [split_body(): messages = jnp.concatenate([messages, exchange(messages, 'seq', 2)], axis=0)]
  transfers between devices with their start and end apart: 11 -> 13, of which waited for: 8 -> 7; matrix products, arithmetic and copies ran while one was open for 1% -> 6% of each run, Pallas kernels for 6% -> 7%
where the time goes in v3:
time: 51.1 us; the launch traced here: 50.7 us
  starting transfers between devices  22.5 us (44%)
  waiting for transfers between devices  17 us (33%)
  Pallas kernels  7.38 us (14%)
  other arithmetic  2.34 us (5%)
  matrix products  1.31 us (3%)
    ppermute x13, starting transfers between devices, exchange(): return lax.ppermute(values_in, axis, [(i, i ^ mask) for i in range(count)])  22.5 us
    ppermute x13, waiting for transfers between devices, exchange(): return lax.ppermute(values_in, axis, [(i, i ^ mask) for i in range(count)])  17 us
    pallas_call x5, Pallas kernels, call(): pl.pallas_call(kernel, out_shape=[jax.ShapeDtypeStruct(shape, kind) for s...  7.38 us
    dot_general x1, matrix products, split_body(): jnp.dot(normed, query_weight, preferred_element_type=f32).astype(bf16)  1.31 us
  transfers between devices with their start and end apart: 13, of which 7 were waited for; matrix products, arithmetic and copies ran while one was open for 6% of the time, Pallas kernels for 7%

profile of v3, /device:TPU:0, one launch (start us, length us, event | category | flops | bytes accessed | tf_op | source)
XLA Modules:
  0.0 50.7 jit_solution(12384311736457699606)
XLA Ops:
  0.0 0.0 copy-start.1
  0.0 2.6 %shard_map.91 = (bf16[112,256]{1,0:T(8,128)(2,1)}, bf16[64,1536]{1,0:T(8,128)(2,1)}, bf16[5,96,384]{2,1,0:T(8,128)(2,1)}) custom-call(bf16[128,1536]{1,0:T(8,128)(2,1)} %bitcast.10, f32[1536]{0:T(1024)} %gain_ref.2, bf16[1536,256]{1,0:T(8,128)(2,1)} %weight_hbm.1, f32[1,4,4,32]{3,2,1,0:T(4,128)} %bias_ref.1, bf16[10,96,384]{2,1,0:T(8,128)(2,1)} %bitcast.7), custom_call_target="tpu_custom_call" | custom-call | tf_op jit(solution)/shard_map/pallas_call | solution.py:144
  2.6 0.0 copy-start.2
  2.6 0.0 copy-start.4
  2.6 0.0 copy-start.5
  2.6 4.1 %collective-permute-start = (bf16[1,112,256]{2,1,0:T(8,128)(2,1)}, bf16[1,112,256]{2,1,0:T(8,128)(2,1)S(1)}, u32[]{:S(2)}, u32[]{:S(2)}) collective-permute-start(bf16[1,112,256]{2,1,0:T(8,128)(2,1)} %bitcast.12), channel_id=1, source_target_pairs={{0,8},{2,10},{4,12},{6,14},{8,0},{10,2},{12,4},{14,6},{1,9},{3,11}... | collective-permute-start | bytes 172040 | tf_op jit(solution)/shard_map/ppermute | solution.py:139
  6.7 1.5 %collective-permute-start.4 = (bf16[5,96,384]{2,1,0:T(8,128)(2,1)}, bf16[5,96,384]{2,1,0:T(8,128)(2,1)S(1)}, u32[]{:S(2)}, u32[]{:S(2)}) collective-permute-start(bf16[5,96,384]{2,1,0:T(8,128)(2,1)} %get-tuple-element.25), channel_id=1, source_target_pairs={{0,2},{2,0},{4,6},{6,4},{8,10},{10,8},{12,14},{14,12},{1,3},{3,1},... | collective-permute-start | bytes 1105928 | tf_op jit(solution)/shard_map/ppermute | solution.py:139
  8.2 1.5 %collective-permute-done = bf16[1,112,256]{2,1,0:T(8,128)(2,1)S(1)} collective-permute-done((bf16[1,112,256]{2,1,0:T(8,128)(2,1)}, bf16[1,112,256]{2,1,0:T(8,128)(2,1)S(1)}, u32[]{:S(2)}, u32[]{:S(2)}) %collective-permute-start) | collective-permute-done | bytes 57376 | tf_op jit(solution)/shard_map/ppermute | solution.py:139
  9.7 0.8 %pad_maximum_fusion.1 = bf16[2,112,256]{2,1,0:T(8,128)(2,1)S(1)} fusion(bf16[1,112,256]{2,1,0:T(8,128)(2,1)S(1)} %collective-permute-done, bf16[1,112,256]{2,1,0:T(8,128)(2,1)} %bitcast.13), kind=kLoop, calls=%fused_computation.3 | loop fusion | flops 57344 | bytes 229376 | tf_op jit(solution)/shard_map/concatenate | solution.py:442
  10.5 1.4 %collective-permute-start.1 = (bf16[2,112,256]{2,1,0:T(8,128)(2,1)S(1)}, bf16[2,112,256]{2,1,0:T(8,128)(2,1)S(1)}, u32[]{:S(2)}, u32[]{:S(2)}) collective-permute-start(bf16[2,112,256]{2,1,0:T(8,128)(2,1)S(1)} %pad_maximum_fusion.1), channel_id=1, source_target_pairs={{0,4},{2,6},{4,0},{6,2},{8,12},{10,14},{12,8},{14,10},{1,5},{3,7},... | collective-permute-start | bytes 344072 | tf_op jit(solution)/shard_map/ppermute | solution.py:139
  11.9 3.5 %collective-permute-done.1 = bf16[2,112,256]{2,1,0:T(8,128)(2,1)S(1)} collective-permute-done((bf16[2,112,256]{2,1,0:T(8,128)(2,1)S(1)}, bf16[2,112,256]{2,1,0:T(8,128)(2,1)S(1)}, u32[]{:S(2)}, u32[]{:S(2)}) %collective-permute-start.1) | collective-permute-done | bytes 114720 | tf_op jit(solution)/shard_map/ppermute | solution.py:139
  15.4 0.8 %pad_maximum_fusion.near_ref = bf16[4,112,256]{2,1,0:T(8,128)(2,1)S(1)} fusion(bf16[2,112,256]{2,1,0:T(8,128)(2,1)S(1)} %collective-permute-done.1, bf16[1,112,256]{2,1,0:T(8,128)(2,1)S(1)} %collective-permute-done, bf16[1,112,256]{2,1,0:T(8,128)(2,1)} %bitcast.14), kind=kLoop, calls=%fused_computation.1 | loop fusion | flops 229376 | bytes 458752 | tf_op jit(solution)/shard_map/concatenate | solution.py:444
  16.2 1.8 %collective-permute-start.2 = (bf16[4,112,256]{2,1,0:T(8,128)(2,1)S(1)}, bf16[4,112,256]{2,1,0:T(8,128)(2,1)S(1)}, u32[]{:S(2)}, u32[]{:S(2)}) collective-permute-start(bf16[4,112,256]{2,1,0:T(8,128)(2,1)S(1)} %pad_maximum_fusion.near_ref), channel_id=1, source_target_pairs={{0,2},{2,0},{4,6},{6,4},{8,10},{10,8},{12,14},{14,12},{1,3},{3,1},... | collective-permute-start | bytes 688136 | tf_op jit(solution)/shard_map/ppermute | solution.py:139
  18.0 1.2 %collective-permute-start.6 = (bf16[5,96,384]{2,1,0:T(8,128)(2,1)}, bf16[5,96,384]{2,1,0:T(8,128)(2,1)S(1)}, u32[]{:S(2)}, u32[]{:S(2)}) collective-permute-start(bf16[5,96,384]{2,1,0:T(8,128)(2,1)} %get-tuple-element.25), channel_id=1, source_target_pairs={{0,4},{2,6},{4,0},{6,2},{8,12},{10,14},{12,8},{14,10},{1,5},{3,7},... | collective-permute-start | bytes 1105928 | tf_op jit(solution)/shard_map/ppermute | solution.py:139
  19.2 0.0 collective-permute-done.4.w1
  19.2 1.5 %collective-permute-start.5 = (bf16[5,96,384]{2,1,0:T(8,128)(2,1)S(1)}, bf16[5,96,384]{2,1,0:T(8,128)(2,1)S(1)}, u32[]{:S(2)}, u32[]{:S(2)}) collective-permute-start(bf16[5,96,384]{2,1,0:T(8,128)(2,1)S(1)} %collective-permute-done.4.w1), channel_id=1, source_target_pairs={{0,16},{16,0},{1,17},{17,1},{2,18},{18,2},{3,19},{19,3},{4,20},{20... | collective-permute-start | bytes 1105928 | tf_op jit(solution)/shard_map/ppermute | solution.py:139
  20.7 0.0 copy-done.1
  20.7 1.3 %convolution_convert_fusion.query_ref = bf16[64,512]{1,0:T(8,128)(2,1)S(1)} fusion(bf16[64,1536]{1,0:T(8,128)(2,1)} %get-tuple-element.17, bf16[1536,512]{1,0:T(8,128)(2,1)S(1)} %copy-done.1), kind=kOutput, calls=%fused_computation | convolution fusion | flops 100696064 | bytes 1835008 | tf_op jit(solution)/shard_map/dot_general | solution.py:448
  22.0 0.0 copy-start.3
  22.0 0.0 copy-start.6
  22.0 0.0 copy-start.7
  22.0 0.0 copy-start
  22.1 0.3 collective-permute-done.2.side_ref
  22.3 0.0 copy-done.2
  22.3 0.0 copy-done.4
  22.3 0.0 copy-done.5
  22.3 1.8 %shard_map.92 = (bf16[80,1536]{1,0:T(8,128)(2,1)S(1)}, f32[8,1536]{1,0:T(8,128)S(1)}) custom-call(bf16[64,512]{1,0:T(8,128)(2,1)S(1)} %convolution_convert_fusion.query_ref, bf16[4,112,256]{2,1,0:T(8,128)(2,1)S(1)} %pad_maximum_fusion.near_ref, bf16[4,112,256]{2,1,0:T(8,128)(2,1)S(1)} %collective-permute-done.2.side_ref, bf16[1536,512]{1,0:T(8,128)(2,1)S(1)} %copy-done.1, ...), custom_call_target="tpu_custom_call" | custom-call | tf_op jit(solution)/shard_map/pallas_call | solution.py:144
  24.2 0.1 collective-permute-start.3
  24.2 1.5 %collective-permute-done.3.other_ref = bf16[80,1536]{1,0:T(8,128)(2,1)S(1)} collective-permute-done((bf16[80,1536]{1,0:T(8,128)(2,1)S(1)}, bf16[80,1536]{1,0:T(8,128)(2,1)S(1)}, u32[]{:S(2)}, u32[]{:S(2)}) %collective-permute-start.3) | collective-permute-done | bytes 245792 | tf_op jit(solution)/shard_map/ppermute | solution.py:139
  25.7 0.0 copy-done.3
  25.7 0.0 copy-done.6
  25.7 0.0 copy-done.7
  25.7 0.7 %shard_map.93 = (bf16[144,768]{1,0:T(8,128)(2,1)S(1)}, bf16[144,384]{1,0:T(8,128)(2,1)S(1)}, f32[128,384]{1,0:T(8,128)S(1)}) custom-call(bf16[128,1536]{1,0:T(8,128)(2,1)S(1)} %bitcast.11, f32[8,1536]{1,0:T(8,128)S(1)} %get-tuple-element.19.edge_ref, bf16[80,1536]{1,0:T(8,128)(2,1)S(1)} %get-tuple-element.20.own_ref, ...), custom_call_target="tpu_custom_call" | custom-call | tf_op jit(solution)/shard_map/pallas_call | solution.py:144
  26.5 0.0 collective-permute-done.6.w3
  26.5 1.8 %collective-permute-start.7 = (bf16[5,96,384]{2,1,0:T(8,128)(2,1)S(1)}, bf16[5,96,384]{2,1,0:T(8,128)(2,1)S(1)}, u32[]{:S(2)}, u32[]{:S(2)}) collective-permute-start(bf16[5,96,384]{2,1,0:T(8,128)(2,1)S(1)} %collective-permute-done.6.w3), channel_id=1, source_target_pairs={{0,16},{16,0},{1,17},{17,1},{2,18},{18,2},{3,19},{19,3},{4,20},{20... | collective-permute-start | bytes 1105928 | tf_op jit(solution)/shard_map/ppermute | solution.py:139
  28.3 1.5 %collective-permute-start.8 = (bf16[5,96,384]{2,1,0:T(8,128)(2,1)S(1)}, bf16[5,96,384]{2,1,0:T(8,128)(2,1)S(1)}, u32[]{:S(2)}, u32[]{:S(2)}) collective-permute-start(bf16[5,96,384]{2,1,0:T(8,128)(2,1)S(1)} %collective-permute-done.6.w3), channel_id=1, source_target_pairs={{0,2},{2,0},{4,6},{6,4},{8,10},{10,8},{12,14},{14,12},{1,3},{3,1},... | collective-permute-start | bytes 1105928 | tf_op jit(solution)/shard_map/ppermute | solution.py:139
  29.8 0.0 collective-permute-done.5.w2
  29.8 1.2 %collective-permute-start.9 = (bf16[5,96,384]{2,1,0:T(8,128)(2,1)S(1)}, bf16[5,96,384]{2,1,0:T(8,128)(2,1)S(1)}, u32[]{:S(2)}, u32[]{:S(2)}) collective-permute-start(bf16[5,96,384]{2,1,0:T(8,128)(2,1)S(1)} %collective-permute-done.5.w2), channel_id=1, source_target_pairs={{0,4},{2,6},{4,0},{6,2},{8,12},{10,14},{12,8},{14,10},{1,5},{3,7},... | collective-permute-start | bytes 1105928 | tf_op jit(solution)/shard_map/ppermute | solution.py:139
  31.0 3.1 %collective-permute-start.10 = (bf16[144,384]{1,0:T(8,128)(2,1)S(1)}, bf16[144,384]{1,0:T(8,128)(2,1)S(1)}, u32[]{:S(2)}, u32[]{:S(2)}) collective-permute-start(bf16[144,384]{1,0:T(8,128)(2,1)S(1)} %get-tuple-element.26), channel_id=1, source_target_pairs={{0,8},{2,10},{4,12},{6,14},{8,0},{10,2},{12,4},{14,6},{1,9},{3,11}... | collective-permute-start | bytes 331784 | tf_op jit(solution)/shard_map/ppermute | solution.py:139
  34.1 6.9 %collective-permute-done.10.first_ref = bf16[144,384]{1,0:T(8,128)(2,1)S(1)} collective-permute-done((bf16[144,384]{1,0:T(8,128)(2,1)S(1)}, bf16[144,384]{1,0:T(8,128)(2,1)S(1)}, u32[]{:S(2)}, u32[]{:S(2)}) %collective-permute-start.10) | collective-permute-done | bytes 110624 | tf_op jit(solution)/shard_map/ppermute | solution.py:139
  40.9 0.0 collective-permute-start.11
  40.9 1.3 %collective-permute-done.11.second_ref = bf16[144,384]{1,0:T(8,128)(2,1)S(1)} collective-permute-done((bf16[144,384]{1,0:T(8,128)(2,1)S(1)}, bf16[144,384]{1,0:T(8,128)(2,1)S(1)}, u32[]{:S(2)}, u32[]{:S(2)}) %collective-permute-start.11) | collective-permute-done | bytes 110624 | tf_op jit(solution)/shard_map/ppermute | solution.py:139
  42.2 0.0 collective-permute-done.7.w4
  42.2 0.0 collective-permute-done.8.w5
  42.2 0.0 collective-permute-done.9.w6
  42.2 0.0 copy-done
  42.3 1.2 %shard_map.95 = bf16[128,384]{1,0:T(8,128)(2,1)S(1)} custom-call(bf16[144,384]{1,0:T(8,128)(2,1)S(1)} %collective-permute-done.10.first_ref, bf16[144,384]{1,0:T(8,128)(2,1)S(1)} %collective-permute-done.11.second_ref, bf16[10,96,384]{2,1,0:T(8,128)(2,1)S(1)} %bitcast.8, bf16[5,96,384]{2,1,0:T(8,128)(2,1)S(1)} %collective-permute-done.4.w1, ...), custom_call_target="tpu_custom_call" | custom-call | tf_op jit(solution)/shard_map/pallas_call | solution.py:144
  43.5 3.5 %collective-permute-start.12 = (bf16[128,384]{1,0:T(8,128)(2,1)S(1)}, bf16[128,384]{1,0:T(8,128)(2,1)S(1)}, u32[]{:S(2)}, u32[]{:S(2)}) collective-permute-start(bf16[128,384]{1,0:T(8,128)(2,1)S(1)} %shard_map.95), channel_id=1, source_target_pairs={{0,8},{2,10},{4,12},{6,14},{8,0},{10,2},{12,4},{14,6},{1,9},{3,11}... | collective-permute-start | bytes 294920 | tf_op jit(solution)/shard_map/ppermute | solution.py:139
  46.9 1.0 %shard_map.94 = f32[128,384]{1,0:T(8,128)S(1)} custom-call(bf16[144,768]{1,0:T(8,128)(2,1)S(1)} %get-tuple-element.21.active_ref, f32[128,384]{1,0:T(8,128)S(1)} %get-tuple-element.22.base_ref, bf16[10,96,384]{2,1,0:T(8,128)(2,1)S(1)} %bitcast.9, bf16[5,96,384]{2,1,0:T(8,128)(2,1)S(1)} %collective-permute-done.4.w1, ...), custom_call_target="tpu_custom_call" | custom-call | tf_op jit(solution)/shard_map/pallas_call | solution.py:144
  48.0 2.1 %collective-permute-done.12 = bf16[128,384]{1,0:T(8,128)(2,1)S(1)} collective-permute-done((bf16[128,384]{1,0:T(8,128)(2,1)S(1)}, bf16[128,384]{1,0:T(8,128)(2,1)S(1)}, u32[]{:S(2)}, u32[]{:S(2)}) %collective-permute-start.12) | collective-permute-done | bytes 98336 | tf_op jit(solution)/shard_map/ppermute | solution.py:139
  50.0 0.7 %fusion = bf16[1,128,384]{2,1,0:T(8,128)(2,1)} fusion(f32[128,384]{1,0:T(8,128)S(1)} %shard_map.94, bf16[128,384]{1,0:T(8,128)(2,1)S(1)} %collective-permute-done.12), kind=kLoop, calls=%fused_computation.4 | loop fusion | flops 147456 | bytes 393216 | tf_op jit(solution)/shard_map/broadcast_in_dim | solution.py:474
Async XLA Ops:
  0.0 20.7 %copy-start.1 = (bf16[1536,512]{1,0:T(8,128)(2,1)S(1)}, bf16[1536,512]{1,0:T(8,128)(2,1)}, u32[]{:S(2)}) copy-start(bf16[1536,512]{1,0:T(8,128)(2,1)} %query_weight_ref.1) | copy-start | bytes 4718596
  2.6 19.7 %copy-start.2 = (bf16[512,1536]{1,0:T(8,128)(2,1)S(1)}, bf16[512,1536]{1,0:T(8,128)(2,1)}, u32[]{:S(2)}) copy-start(bf16[512,1536]{1,0:T(8,128)(2,1)} %out_weight_ref.1) | copy-start | bytes 4718596
  2.6 19.7 %copy-start.4 = (f32[1536]{0:T(1024)S(1)}, f32[1536]{0:T(1024)}, u32[]{:S(2)}) copy-start(f32[1536]{0:T(1024)} %gain_ref.2) | copy-start | bytes 18436
  2.6 19.7 %copy-start.5 = (f32[1,4,4,32]{3,2,1,0:T(4,128)S(1)}, f32[1,4,4,32]{3,2,1,0:T(4,128)}, u32[]{:S(2)}) copy-start(f32[1,4,4,32]{3,2,1,0:T(4,128)} %bias_ref.1) | copy-start | bytes 6148
  2.6 7.1 %collective-permute-start = (bf16[1,112,256]{2,1,0:T(8,128)(2,1)}, bf16[1,112,256]{2,1,0:T(8,128)(2,1)S(1)}, u32[]{:S(2)}, u32[]{:S(2)}) collective-permute-start(bf16[1,112,256]{2,1,0:T(8,128)(2,1)} %bitcast.12), channel_id=1, source_target_pairs={{0,8},{2,10},{4,12},{6,14},{8,0},{10,2},{12,4},{14,6},{1,9},{3,11}... | collective-permute-start | bytes 172040 | tf_op jit(solution)/shard_map/ppermute | solution.py:139
  6.7 12.5 %collective-permute-start.4 = (bf16[5,96,384]{2,1,0:T(8,128)(2,1)}, bf16[5,96,384]{2,1,0:T(8,128)(2,1)S(1)}, u32[]{:S(2)}, u32[]{:S(2)}) collective-permute-start(bf16[5,96,384]{2,1,0:T(8,128)(2,1)} %get-tuple-element.25), channel_id=1, source_target_pairs={{0,2},{2,0},{4,6},{6,4},{8,10},{10,8},{12,14},{14,12},{1,3},{3,1},... | collective-permute-start | bytes 1105928 | tf_op jit(solution)/shard_map/ppermute | solution.py:139
  10.5 4.9 %collective-permute-start.1 = (bf16[2,112,256]{2,1,0:T(8,128)(2,1)S(1)}, bf16[2,112,256]{2,1,0:T(8,128)(2,1)S(1)}, u32[]{:S(2)}, u32[]{:S(2)}) collective-permute-start(bf16[2,112,256]{2,1,0:T(8,128)(2,1)S(1)} %pad_maximum_fusion.1), channel_id=1, source_target_pairs={{0,4},{2,6},{4,0},{6,2},{8,12},{10,14},{12,8},{14,10},{1,5},{3,7},... | collective-permute-start | bytes 344072 | tf_op jit(solution)/shard_map/ppermute | solution.py:139
  16.2 6.1 %collective-permute-start.2 = (bf16[4,112,256]{2,1,0:T(8,128)(2,1)S(1)}, bf16[4,112,256]{2,1,0:T(8,128)(2,1)S(1)}, u32[]{:S(2)}, u32[]{:S(2)}) collective-permute-start(bf16[4,112,256]{2,1,0:T(8,128)(2,1)S(1)} %pad_maximum_fusion.near_ref), channel_id=1, source_target_pairs={{0,2},{2,0},{4,6},{6,4},{8,10},{10,8},{12,14},{14,12},{1,3},{3,1},... | collective-permute-start | bytes 688136 | tf_op jit(solution)/shard_map/ppermute | solution.py:139
  18.0 8.5 %collective-permute-start.6 = (bf16[5,96,384]{2,1,0:T(8,128)(2,1)}, bf16[5,96,384]{2,1,0:T(8,128)(2,1)S(1)}, u32[]{:S(2)}, u32[]{:S(2)}) collective-permute-start(bf16[5,96,384]{2,1,0:T(8,128)(2,1)} %get-tuple-element.25), channel_id=1, source_target_pairs={{0,4},{2,6},{4,0},{6,2},{8,12},{10,14},{12,8},{14,10},{1,5},{3,7},... | collective-permute-start | bytes 1105928 | tf_op jit(solution)/shard_map/ppermute | solution.py:139
  19.2 10.6 %collective-permute-start.5 = (bf16[5,96,384]{2,1,0:T(8,128)(2,1)S(1)}, bf16[5,96,384]{2,1,0:T(8,128)(2,1)S(1)}, u32[]{:S(2)}, u32[]{:S(2)}) collective-permute-start(bf16[5,96,384]{2,1,0:T(8,128)(2,1)S(1)} %collective-permute-done.4.w1), channel_id=1, source_target_pairs={{0,16},{16,0},{1,17},{17,1},{2,18},{18,2},{3,19},{19,3},{4,20},{20... | collective-permute-start | bytes 1105928 | tf_op jit(solution)/shard_map/ppermute | solution.py:139
  22.0 3.7 %copy-start.3 = (bf16[1,128,1536]{2,1,0:T(8,128)(2,1)S(1)}, bf16[1,128,1536]{2,1,0:T(8,128)(2,1)}, u32[]{:S(2)}) copy-start(bf16[1,128,1536]{2,1,0:T(8,128)(2,1)} %param.9) | copy-start | bytes 1179652
  22.0 3.7 %copy-start.6 = (f32[1536]{0:T(1024)S(1)}, f32[1536]{0:T(1024)}, u32[]{:S(2)}) copy-start(f32[1536]{0:T(1024)} %gain_ref.3) | copy-start | bytes 18436
  22.0 3.7 %copy-start.7 = (f32[384]{0:T(512)S(1)}, f32[384]{0:T(512)}, u32[]{:S(2)}) copy-start(f32[384]{0:T(512)} %dec_bias_ref.1) | copy-start | bytes 4612
  22.0 20.2 %copy-start = (bf16[5,192,384]{2,1,0:T(8,128)(2,1)S(1)}, bf16[5,192,384]{2,1,0:T(8,128)(2,1)}, u32[]{:S(2)}) copy-start(bf16[5,192,384]{2,1,0:T(8,128)(2,1)} %param.16) | copy-start | bytes 2211844
  24.2 1.6 %collective-permute-start.3 = (bf16[80,1536]{1,0:T(8,128)(2,1)S(1)}, bf16[80,1536]{1,0:T(8,128)(2,1)S(1)}, u32[]{:S(2)}, u32[]{:S(2)}) collective-permute-start(bf16[80,1536]{1,0:T(8,128)(2,1)S(1)} %get-tuple-element.20.own_ref), channel_id=1, source_target_pairs={{0,1},{1,0},{2,3},{3,2},{4,5},{5,4},{6,7},{7,6},{8,9},{9,8},{10,11... | collective-permute-start | bytes 737288 | tf_op jit(solution)/shard_map/ppermute | solution.py:139
  26.5 15.7 %collective-permute-start.7 = (bf16[5,96,384]{2,1,0:T(8,128)(2,1)S(1)}, bf16[5,96,384]{2,1,0:T(8,128)(2,1)S(1)}, u32[]{:S(2)}, u32[]{:S(2)}) collective-permute-start(bf16[5,96,384]{2,1,0:T(8,128)(2,1)S(1)} %collective-permute-done.6.w3), channel_id=1, source_target_pairs={{0,16},{16,0},{1,17},{17,1},{2,18},{18,2},{3,19},{19,3},{4,20},{20... | collective-permute-start | bytes 1105928 | tf_op jit(solution)/shard_map/ppermute | solution.py:139
  28.3 13.9 %collective-permute-start.8 = (bf16[5,96,384]{2,1,0:T(8,128)(2,1)S(1)}, bf16[5,96,384]{2,1,0:T(8,128)(2,1)S(1)}, u32[]{:S(2)}, u32[]{:S(2)}) collective-permute-start(bf16[5,96,384]{2,1,0:T(8,128)(2,1)S(1)} %collective-permute-done.6.w3), channel_id=1, source_target_pairs={{0,2},{2,0},{4,6},{6,4},{8,10},{10,8},{12,14},{14,12},{1,3},{3,1},... | collective-permute-start | bytes 1105928 | tf_op jit(solution)/shard_map/ppermute | solution.py:139
  29.8 12.5 %collective-permute-start.9 = (bf16[5,96,384]{2,1,0:T(8,128)(2,1)S(1)}, bf16[5,96,384]{2,1,0:T(8,128)(2,1)S(1)}, u32[]{:S(2)}, u32[]{:S(2)}) collective-permute-start(bf16[5,96,384]{2,1,0:T(8,128)(2,1)S(1)} %collective-permute-done.5.w2), channel_id=1, source_target_pairs={{0,4},{2,6},{4,0},{6,2},{8,12},{10,14},{12,8},{14,10},{1,5},{3,7},... | collective-permute-start | bytes 1105928 | tf_op jit(solution)/shard_map/ppermute | solution.py:139
  31.0 10.0 %collective-permute-start.10 = (bf16[144,384]{1,0:T(8,128)(2,1)S(1)}, bf16[144,384]{1,0:T(8,128)(2,1)S(1)}, u32[]{:S(2)}, u32[]{:S(2)}) collective-permute-start(bf16[144,384]{1,0:T(8,128)(2,1)S(1)} %get-tuple-element.26), channel_id=1, source_target_pairs={{0,8},{2,10},{4,12},{6,14},{8,0},{10,2},{12,4},{14,6},{1,9},{3,11}... | collective-permute-start | bytes 331784 | tf_op jit(solution)/shard_map/ppermute | solution.py:139
  40.9 1.3 %collective-permute-start.11 = (bf16[144,384]{1,0:T(8,128)(2,1)S(1)}, bf16[144,384]{1,0:T(8,128)(2,1)S(1)}, u32[]{:S(2)}, u32[]{:S(2)}) collective-permute-start(bf16[144,384]{1,0:T(8,128)(2,1)S(1)} %collective-permute-done.10.first_ref), channel_id=1, source_target_pairs={{0,1},{1,0},{2,3},{3,2},{4,5},{5,4},{6,7},{7,6},{8,9},{9,8},{10,11... | collective-permute-start | bytes 331784 | tf_op jit(solution)/shard_map/ppermute | solution.py:139
  43.5 6.6 %collective-permute-start.12 = (bf16[128,384]{1,0:T(8,128)(2,1)S(1)}, bf16[128,384]{1,0:T(8,128)(2,1)S(1)}, u32[]{:S(2)}, u32[]{:S(2)}) collective-permute-start(bf16[128,384]{1,0:T(8,128)(2,1)S(1)} %shard_map.95), channel_id=1, source_target_pairs={{0,8},{2,10},{4,12},{6,14},{8,0},{10,2},{12,4},{14,6},{1,9},{3,11}... | collective-permute-start | bytes 294920 | tf_op jit(solution)/shard_map/ppermute | solution.py:139

commit v4 on v3

--- a/solution.py
+++ b/solution.py
@@ -130,7 +130,7 @@
 
 
 ROWS = 80
-MSG = 112
+MSG = 48
 LIMIT = 24 * 1024 * 1024
 
 
@@ -222,54 +222,76 @@
         copy.start()
     for copy in copies[:3]:
         copy.wait()
+    section = lax.axis_index("section")
     half = skip_ref.shape[0] // 2
+    quarter = half // 2
     spread_columns(wide, skip_ref)
     pooled = jnp.maximum(take_rows(wide, 0, half), take_rows(wide, 1, half))
-    normed = normalize(pooled, gain_ref[...][None, :]).astype(jnp.bfloat16)
-    normed_ref[...] = normed
+    normed_ref[...] = normalize(pooled, gain_ref[...][None, :]).astype(jnp.bfloat16)
     copies[3].wait()
-    lines[0:half, :] = jnp.dot(normed, weight_ref[...], preferred_element_type=jnp.float32)
-    last = skip_ref.shape[0]
-    for n, row in enumerate((0, 1, last - 2, last - 1)):
+    own = normed_ref[pl.ds(pl.multiple_of(section * quarter, 16), quarter), :]
+    lines[0:quarter, :] = jnp.dot(own, weight_ref[...], preferred_element_type=jnp.float32)
+    for n in range(2):
+        row = section * (skip_ref.shape[0] - 2) + n
         for k in range(12):
-            at = half + 6 * n + k // 2
-            lines[at : at + 1, 128 * (k % 2) : 128 * (k % 2) + 128] = wide[k, row : row + 1, :]
-    lines[88:MSG, :] = jnp.zeros((MSG - 88, 256), jnp.float32)
-    for n, term in enumerate(split_three(own_bias(bias_ref))):
-        for h in range(4):
-            for k, cell in enumerate((0, 3)):
-                at = 88 + 8 * n + 2 * h + k
-                lines[at : at + 1, 0:32] = term[4 * h + cell : 4 * h + cell + 1, :].astype(
-                    jnp.float32
-                )
+            at = quarter + 6 * n + k // 2
+            lines[at : at + 1, 128 * (k % 2) : 128 * (k % 2) + 128] = wide[k, pl.ds(row, 1), :]
+    terms = [term.astype(jnp.float32) for term in split_three(own_bias(bias_ref))]
+    packed = [
+        jnp.concatenate(
+            [term[4 * h + cell : 4 * h + cell + 1, :] for cell in (0, 3) for h in range(4)], axis=1
+        )
+        for term in terms
+    ]
+    lines[MSG - 4 : MSG, :] = jnp.concatenate(packed + [jnp.zeros((1, 256), jnp.float32)], axis=0)
     message_ref[...] = lines[...].astype(jnp.bfloat16)
     copies[4].wait()
 
 
-def reverse_bits(value):
-    return (value & 1) * 4 + (value & 2) + (value >> 2)
+def join_kernel(first_ref, second_ref, out_ref):
+    count = first_ref.shape[0]
+    out_ref[0:count] = first_ref[...]
+    out_ref[count:] = second_ref[...]
+
+
+def swap_bits(value):
+    return 4 * (value & 1) + (value & 2) + (value & 4) // 4
 
 
 def attention_kernel(
-    query_ref, near_ref, side_ref, query_weight_ref, gain_ref, bias_ref, out_weight_ref, terms_ref, edge_ref
+    query_ref,
+    near_ref,
+    near_other_ref,
+    side_ref,
+    side_other_ref,
+    query_weight_ref,
+    gain_ref,
+    bias_ref,
+    out_weight_ref,
+    terms_ref,
+    edge_ref,
 ):
     me = lax.axis_index("seq")
+    section = lax.axis_index("section")
     count = lax.axis_size("seq")
-    low_slot = reverse_bits(me ^ jnp.maximum(me - 1, 0))
-    high_slot = reverse_bits(me ^ jnp.minimum(me + 1, count - 1))
-
-    def block_of(slot):
-        near = near_ref[slot & 3].astype(jnp.float32)
-        return jnp.where(slot < 4, near, side_ref[slot & 3].astype(jnp.float32))
-
-    low, high = block_of(low_slot), block_of(high_slot)
+    low_slot = swap_bits(me ^ jnp.maximum(me - 1, 0))
+    high_slot = swap_bits(me ^ jnp.minimum(me + 1, count - 1))
+
+    def block_of(slot, near, side):
+        return jnp.where(
+            slot < 4, near[slot & 3].astype(jnp.float32), side[slot & 3].astype(jnp.float32)
+        )
+
+    low, high = (block_of(slot, near_ref, side_ref) for slot in (low_slot, high_slot))
+    low_edge = jnp.where(section == 1, low, block_of(low_slot, near_other_ref, side_other_ref))
+    high_edge = jnp.where(section == 0, high, block_of(high_slot, near_other_ref, side_other_ref))
 
     def line(block, row):
-        start = 64 + 6 * row
+        start = 32 + 6 * row
         return jnp.concatenate([block[start + k : start + k + 1, :] for k in range(6)], axis=1)
 
     edges = jnp.concatenate(
-        [line(low, 2), line(low, 3), line(high, 0), line(high, 1)], axis=0
+        [line(low_edge, 0), line(low_edge, 1), line(high_edge, 0), line(high_edge, 1)], axis=0
     )
     edge_ref[0:4, :] = edges
     edge_ref[4:8, :] = jnp.zeros_like(edges)
@@ -284,20 +306,23 @@
     normed = normalize(pooled, gain_ref[...][None, :]).astype(jnp.bfloat16)
     halo_query = jnp.dot(normed, query_weight_ref[...], preferred_element_type=jnp.float32)
     queries = jnp.concatenate([query_ref[...], halo_query.astype(jnp.bfloat16)], axis=0)
-    pieces = [ref[k, 0:64, :] for ref in (near_ref, side_ref) for k in range(4)]
+    pieces = []
+    for mine, others in ((near_ref, near_other_ref), (side_ref, side_other_ref)):
+        for k in range(4):
+            pieces += [mine[k, 0:32, :], others[k, 0:32, :]]
     keys = jnp.concatenate([piece[:, 0:HEAD] for piece in pieces], axis=0)
     values = jnp.concatenate([piece[:, HEAD : 2 * HEAD] for piece in pieces], axis=0)
     cell = lax.broadcasted_iota(jnp.int32, (32, 512), 0)
     column = lax.broadcasted_iota(jnp.int32, (32, 512), 1)
-    wanted = 4 * (reverse_bits(column >> 6) ^ me) + ((column & 63) >> 4)
+    inner = 2 * (((column >> 5) & 1) ^ section) + ((column & 31) >> 4)
+    wanted = 4 * (swap_bits(column >> 6) ^ me) + inner
     spread = jnp.where(cell == wanted, 1.0, 0.0).astype(jnp.bfloat16)
-    bias = jnp.zeros((32, 512), jnp.float32)
+    bias = jnp.zeros((24, 512), jnp.float32)
     for n, term in enumerate(split_three(own_bias(bias_ref))):
-        at = 88 + 8 * n
-        table = jnp.concatenate(
-            [term, low[at : at + 8, 0:32].astype(jnp.bfloat16), high[at : at + 8, 0:32].astype(jnp.bfloat16)],
-            axis=0,
-        )
+        at = MSG - 4 + n
+        rows = [low[at : at + 1, 128 + 32 * h : 160 + 32 * h] for h in range(4)]
+        rows += [high[at : at + 1, 32 * h : 32 * h + 32] for h in range(4)]
+        table = jnp.concatenate([term.astype(jnp.float32)] + rows, axis=0).astype(jnp.bfloat16)
         bias = bias + jnp.dot(table, spread, preferred_element_type=jnp.float32)
     first = lax.broadcasted_iota(jnp.int32, (16, 512), 0) == 0
     parts = []
@@ -310,7 +335,7 @@
         )
         rows = [jnp.broadcast_to(bias[4 * h + r : 4 * h + r + 1, :], (16, 512)) for r in range(4)]
         rows.append(
-            jnp.where(first, bias[17 + 2 * h : 18 + 2 * h, :], bias[24 + 2 * h : 25 + 2 * h, :])
+            jnp.where(first, bias[16 + h : 17 + h, :], bias[20 + h : 21 + h, :])
         )
         scores = scores * (1.0 / math.sqrt(HEAD)) + jnp.concatenate(rows, axis=0)
         exps = jnp.exp(scores - jnp.max(scores, axis=-1, keepdims=True))
@@ -425,7 +450,10 @@
     message, normed, piece = call(
         pool_kernel,
         [((MSG, 256), bf16), ((rows // 2, channels), bf16), ((taps, depth // 2, width), bf16)],
-        [skip, attn_gain, kv_weight, pair_bias, chunks],
+        [
+            pltpu.with_memory_space_constraint(values_in, pltpu.HBM)
+            for values_in in (skip, attn_gain, kv_weight, pair_bias, chunks)
+        ],
         [
             pltpu.VMEM((rows, channels), bf16),
             pltpu.VMEM((channels,), f32),
@@ -436,20 +464,31 @@
             pltpu.SemaphoreType.DMA((5,)),
         ],
         [pl.BlockSpec(memory_space=pl.ANY)] * 5,
-        60 * 1024 * 1024,
-    )
-    messages = message[None]
-    messages = jnp.concatenate([messages, exchange(messages, "seq", 4)], axis=0)
+    )
+    def joined(values_in, mask):
+        count = values_in.shape[0]
+        return call(
+            join_kernel,
+            [((2 * count,) + values_in.shape[1:], bf16)],
+            [values_in, exchange(values_in, "seq", mask)],
+        )[0]
+
+    def behind(values_in, gate):
+        return lax.optimization_barrier((values_in, gate))[0]
+
+    near = joined(message[None], 4)
     side = exchange(piece, "seq", 1)
-    messages = jnp.concatenate([messages, exchange(messages, "seq", 2)], axis=0)
-    after = exchange(lax.optimization_barrier((piece, messages))[0], "seq", 2)
-    messages_side = exchange(messages, "seq", 1)
-    side_rest = exchange(lax.optimization_barrier((side, messages))[0], "groups", 1)
+    near = joined(near, 2)
+    after = exchange(behind(piece, near), "seq", 2)
+    across = exchange(near, "seq", 1)
+    near_other = exchange(near, "section", 1)
+    side_rest = exchange(behind(side, near), "groups", 1)
+    across_other = exchange(across, "section", 1)
     queries = jnp.dot(normed, query_weight, preferred_element_type=f32).astype(bf16)
     terms, edges = call(
         attention_kernel,
         [((ROWS, channels), bf16), ((8, channels), f32)],
-        [queries, messages, messages_side, query_weight, attn_gain, pair_bias, out_weight],
+        [queries, near, near_other, across, across_other, query_weight, attn_gain, pair_bias, out_weight],
     )
     other = exchange(terms, "section", 1)
     keep, send, base = call(
@@ -459,10 +498,10 @@
         [pltpu.VMEM((channels // 128, rows + extra, 128), f32) for extra in (0, 16)],
     )
     first = exchange(send, "seq", 4)
-    held = lax.optimization_barrier((after, send))[0]
+    held = behind(after, send)
     after_rest = exchange(held, "groups", 1)
     far = exchange(held, "seq", 1)
-    far_rest = exchange(lax.optimization_barrier((side_rest, send))[0], "seq", 2)
+    far_rest = exchange(behind(side_rest, send), "seq", 2)
     second = exchange(first, "section", 1)
     weights = [chunks, side, side_rest, after, after_rest, far, far_rest]
     scratch = [pltpu.VMEM((8 * taps, depth // 2, width), bf16)]

time: 51.1 us -> 50.9 us (level)
  waiting for transfers between devices: 17 us -> 20.9 us
  other arithmetic: 2.34 us -> 0.66 us
  matrix products: 1.31 us -> 0.38 us
  Pallas kernels: 7.38 us -> 6.56 us
    ppermute x13 -> x15, waiting for transfers between devices: 17 us -> 20.9 us  [exchange(): return lax.ppermute(values_in, axis, [(i, i ^ mask) for i in range(count)])]
    concatenate x2 -> x0, other arithmetic: 1.67 us -> none  [the longest x1 0.84 us: split_body(): messages = jnp.concatenate([messages, exchange(messages, 'seq', 2)], axis=0)]
    dot_general x1, matrix products: 1.31 us -> 0.38 us  [split_body(): jnp.dot(normed, query_weight, preferred_element_type=f32).astype(bf16)]
    pallas_call x5 -> x7, Pallas kernels: 7.38 us -> 6.56 us  [call(): pl.pallas_call(kernel, out_shape=[jax.ShapeDtypeStruct(shape, kind) for s...]
    ppermute x13 -> x15, starting transfers between devices: 22.5 us -> 22.1 us  [exchange(): return lax.ppermute(values_in, axis, [(i, i ^ mask) for i in range(count)])]
  transfers between devices with their start and end apart: 13 -> 15, of which waited for: 7 -> 9; matrix products, arithmetic and copies ran while one was open for 6% -> 1% of each run, Pallas kernels for 7% -> 7%
where the time goes in v4:
time: 50.9 us; the launch traced here: 50.8 us
  starting transfers between devices  22.1 us (43%)
  waiting for transfers between devices  20.9 us (41%)
  Pallas kernels  6.56 us (13%)
  other arithmetic  0.66 us (1%)
    ppermute x15, starting transfers between devices, exchange(): return lax.ppermute(values_in, axis, [(i, i ^ mask) for i in range(count)])  22.1 us
    ppermute x15, waiting for transfers between devices, exchange(): return lax.ppermute(values_in, axis, [(i, i ^ mask) for i in range(count)])  20.9 us
    pallas_call x7, Pallas kernels, call(): pl.pallas_call(kernel, out_shape=[jax.ShapeDtypeStruct(shape, kind) for s...  6.56 us
  transfers between devices with their start and end apart: 15, of which 9 were waited for; matrix products, arithmetic and copies ran while one was open for 1% of the time, Pallas kernels for 7%

profile of v4, /device:TPU:0, one launch (start us, length us, event | category | flops | bytes accessed | tf_op | source)
XLA Modules:
  0.0 50.8 jit_solution(286522008049205104)
XLA Ops:
  0.0 0.0 copy-start.1
  0.0 0.0 copy-start.2
  0.0 0.0 copy-start.4
  0.0 0.0 copy-start.5
  0.0 1.7 %shard_map.91 = (bf16[48,256]{1,0:T(8,128)(2,1)S(1)}, bf16[64,1536]{1,0:T(8,128)(2,1)S(1)}, bf16[5,96,384]{2,1,0:T(8,128)(2,1)S(1)}) custom-call(bf16[128,1536]{1,0:T(8,128)(2,1)} %bitcast.10, f32[1536]{0:T(1024)} %gain_ref.2, bf16[1536,256]{1,0:T(8,128)(2,1)} %weight_hbm.1, f32[1,4,4,32]{3,2,1,0:T(4,128)} %bias_ref.1, bf16[10,96,384]{2,1,0:T(8,128)(2,1)} %bitcast.7), custom_call_target="tpu_custom_call" | custom-call | tf_op jit(solution)/shard_map/pallas_call | solution.py:144
  1.7 3.0 %collective-permute-start.6 = (bf16[5,96,384]{2,1,0:T(8,128)(2,1)S(1)}, bf16[5,96,384]{2,1,0:T(8,128)(2,1)S(1)}, u32[]{:S(2)}, u32[]{:S(2)}) collective-permute-start(bf16[5,96,384]{2,1,0:T(8,128)(2,1)S(1)} %get-tuple-element.25), channel_id=1, source_target_pairs={{0,2},{2,0},{4,6},{6,4},{8,10},{10,8},{12,14},{14,12},{1,3},{3,1},... | collective-permute-start | bytes 1105928 | tf_op jit(solution)/shard_map/ppermute | solution.py:139
  4.8 2.6 %collective-permute-start = (bf16[1,48,256]{2,1,0:T(8,128)(2,1)S(1)}, bf16[1,48,256]{2,1,0:T(8,128)(2,1)S(1)}, u32[]{:S(2)}, u32[]{:S(2)}) collective-permute-start(bf16[1,48,256]{2,1,0:T(8,128)(2,1)S(1)} %bitcast.12), channel_id=1, source_target_pairs={{0,8},{2,10},{4,12},{6,14},{8,0},{10,2},{12,4},{14,6},{1,9},{3,11}... | collective-permute-start | bytes 73736 | tf_op jit(solution)/shard_map/ppermute | solution.py:139
  7.3 2.1 %collective-permute-done.second_ref = bf16[1,48,256]{2,1,0:T(8,128)(2,1)S(1)} collective-permute-done((bf16[1,48,256]{2,1,0:T(8,128)(2,1)S(1)}, bf16[1,48,256]{2,1,0:T(8,128)(2,1)S(1)}, u32[]{:S(2)}, u32[]{:S(2)}) %collective-permute-start) | collective-permute-done | bytes 24608 | tf_op jit(solution)/shard_map/ppermute | solution.py:139
  9.5 1.6 %collective-permute-start.1 = (bf16[2,48,256]{2,1,0:T(8,128)(2,1)S(1)}, bf16[2,48,256]{2,1,0:T(8,128)(2,1)S(1)}, u32[]{:S(2)}, u32[]{:S(2)}) collective-permute-start(bf16[2,48,256]{2,1,0:T(8,128)(2,1)S(1)} %shard_map.92.first_ref), channel_id=1, source_target_pairs={{0,4},{2,6},{4,0},{6,2},{8,12},{10,14},{12,8},{14,10},{1,5},{3,7},... | collective-permute-start | bytes 147464 | tf_op jit(solution)/shard_map/ppermute | solution.py:139
  11.1 2.5 %collective-permute-done.1.second_ref = bf16[2,48,256]{2,1,0:T(8,128)(2,1)S(1)} collective-permute-done((bf16[2,48,256]{2,1,0:T(8,128)(2,1)S(1)}, bf16[2,48,256]{2,1,0:T(8,128)(2,1)S(1)}, u32[]{:S(2)}, u32[]{:S(2)}) %collective-permute-start.1) | collective-permute-done | bytes 49184 | tf_op jit(solution)/shard_map/ppermute | solution.py:139
  13.6 0.5 collective-permute-start.3
  14.1 0.0 collective-permute-start.2
  14.1 1.7 %collective-permute-start.8 = (bf16[5,96,384]{2,1,0:T(8,128)(2,1)S(1)}, bf16[5,96,384]{2,1,0:T(8,128)(2,1)S(1)}, u32[]{:S(2)}, u32[]{:S(2)}) collective-permute-start(bf16[5,96,384]{2,1,0:T(8,128)(2,1)S(1)} %get-tuple-element.25), channel_id=1, source_target_pairs={{0,4},{2,6},{4,0},{6,2},{8,12},{10,14},{12,8},{14,10},{1,5},{3,7},... | collective-permute-start | bytes 1105928 | tf_op jit(solution)/shard_map/ppermute | solution.py:139
  15.8 2.5 %collective-permute-done.3.side_ref = bf16[4,48,256]{2,1,0:T(8,128)(2,1)S(1)} collective-permute-done((bf16[4,48,256]{2,1,0:T(8,128)(2,1)S(1)}, bf16[4,48,256]{2,1,0:T(8,128)(2,1)S(1)}, u32[]{:S(2)}, u32[]{:S(2)}) %collective-permute-start.3) | collective-permute-done | bytes 98336 | tf_op jit(solution)/shard_map/ppermute | solution.py:139
  18.3 0.0 collective-permute-start.4
  18.3 0.0 collective-permute-done.6.w1
  18.3 1.5 %collective-permute-start.7 = (bf16[5,96,384]{2,1,0:T(8,128)(2,1)S(1)}, bf16[5,96,384]{2,1,0:T(8,128)(2,1)S(1)}, u32[]{:S(2)}, u32[]{:S(2)}) collective-permute-start(bf16[5,96,384]{2,1,0:T(8,128)(2,1)S(1)} %collective-permute-done.6.w1), channel_id=1, source_target_pairs={{0,16},{16,0},{1,17},{17,1},{2,18},{18,2},{3,19},{19,3},{4,20},{20... | collective-permute-start | bytes 1105928 | tf_op jit(solution)/shard_map/ppermute | solution.py:139
  19.8 0.0 copy-done.1
  19.8 0.4 convolution_convert_fusion.query_ref
  20.2 0.0 copy-start.3
  20.2 0.0 copy-start.6
  20.2 0.0 copy-start.7
  20.2 0.0 copy-start
  20.2 0.0 collective-permute-done.2.near_other_ref
  20.3 0.0 collective-permute-done.4.side_other_ref
  20.3 0.0 copy-done.2
  20.3 0.0 copy-done.4
  20.3 0.0 copy-done.5
  20.3 1.8 %shard_map.94 = (bf16[80,1536]{1,0:T(8,128)(2,1)S(1)}, f32[8,1536]{1,0:T(8,128)S(1)}) custom-call(bf16[64,512]{1,0:T(8,128)(2,1)S(1)} %convolution_convert_fusion.query_ref, bf16[4,48,256]{2,1,0:T(8,128)(2,1)S(1)} %shard_map.93.near_ref, bf16[4,48,256]{2,1,0:T(8,128)(2,1)S(1)} %collective-permute-done.2.near_other_ref, ...), custom_call_target="tpu_custom_call" | custom-call | tf_op jit(solution)/shard_map/pallas_call | solution.py:144
  22.1 0.3 collective-permute-start.5
  22.4 1.3 %collective-permute-done.5.other_ref = bf16[80,1536]{1,0:T(8,128)(2,1)S(1)} collective-permute-done((bf16[80,1536]{1,0:T(8,128)(2,1)S(1)}, bf16[80,1536]{1,0:T(8,128)(2,1)S(1)}, u32[]{:S(2)}, u32[]{:S(2)}) %collective-permute-start.5) | collective-permute-done | bytes 245792 | tf_op jit(solution)/shard_map/ppermute | solution.py:139
  23.7 0.0 copy-done.3
  23.7 0.0 copy-done.6
  23.7 0.0 copy-done.7
  23.7 0.7 %shard_map.95 = (bf16[144,768]{1,0:T(8,128)(2,1)S(1)}, bf16[144,384]{1,0:T(8,128)(2,1)S(1)}, f32[128,384]{1,0:T(8,128)S(1)}) custom-call(bf16[128,1536]{1,0:T(8,128)(2,1)S(1)} %bitcast.11, f32[8,1536]{1,0:T(8,128)S(1)} %get-tuple-element.19.edge_ref, bf16[80,1536]{1,0:T(8,128)(2,1)S(1)} %get-tuple-element.20.own_ref, ...), custom_call_target="tpu_custom_call" | custom-call | tf_op jit(solution)/shard_map/pallas_call | solution.py:144
  24.5 0.6 %collective-permute-done.8.w3 = bf16[5,96,384]{2,1,0:T(8,128)(2,1)S(1)} collective-permute-done((bf16[5,96,384]{2,1,0:T(8,128)(2,1)S(1)}, bf16[5,96,384]{2,1,0:T(8,128)(2,1)S(1)}, u32[]{:S(2)}, u32[]{:S(2)}) %collective-permute-start.8) | collective-permute-done | bytes 368672 | tf_op jit(solution)/shard_map/ppermute | solution.py:139
  25.1 1.7 %collective-permute-start.9 = (bf16[5,96,384]{2,1,0:T(8,128)(2,1)S(1)}, bf16[5,96,384]{2,1,0:T(8,128)(2,1)S(1)}, u32[]{:S(2)}, u32[]{:S(2)}) collective-permute-start(bf16[5,96,384]{2,1,0:T(8,128)(2,1)S(1)} %collective-permute-done.8.w3), channel_id=1, source_target_pairs={{0,16},{16,0},{1,17},{17,1},{2,18},{18,2},{3,19},{19,3},{4,20},{20... | collective-permute-start | bytes 1105928 | tf_op jit(solution)/shard_map/ppermute | solution.py:139
  26.7 1.5 %collective-permute-start.10 = (bf16[5,96,384]{2,1,0:T(8,128)(2,1)S(1)}, bf16[5,96,384]{2,1,0:T(8,128)(2,1)S(1)}, u32[]{:S(2)}, u32[]{:S(2)}) collective-permute-start(bf16[5,96,384]{2,1,0:T(8,128)(2,1)S(1)} %collective-permute-done.8.w3), channel_id=1, source_target_pairs={{0,2},{2,0},{4,6},{6,4},{8,10},{10,8},{12,14},{14,12},{1,3},{3,1},... | collective-permute-start | bytes 1105928 | tf_op jit(solution)/shard_map/ppermute | solution.py:139
  28.2 1.5 %collective-permute-done.7.w2 = bf16[5,96,384]{2,1,0:T(8,128)(2,1)S(1)} collective-permute-done((bf16[5,96,384]{2,1,0:T(8,128)(2,1)S(1)}, bf16[5,96,384]{2,1,0:T(8,128)(2,1)S(1)}, u32[]{:S(2)}, u32[]{:S(2)}) %collective-permute-start.7) | collective-permute-done | bytes 368672 | tf_op jit(solution)/shard_map/ppermute | solution.py:139
  29.7 1.6 %collective-permute-start.11 = (bf16[5,96,384]{2,1,0:T(8,128)(2,1)S(1)}, bf16[5,96,384]{2,1,0:T(8,128)(2,1)S(1)}, u32[]{:S(2)}, u32[]{:S(2)}) collective-permute-start(bf16[5,96,384]{2,1,0:T(8,128)(2,1)S(1)} %collective-permute-done.7.w2), channel_id=1, source_target_pairs={{0,4},{2,6},{4,0},{6,2},{8,12},{10,14},{12,8},{14,10},{1,5},{3,7},... | collective-permute-start | bytes 1105928 | tf_op jit(solution)/shard_map/ppermute | solution.py:139
  31.2 2.7 %collective-permute-start.12 = (bf16[144,384]{1,0:T(8,128)(2,1)S(1)}, bf16[144,384]{1,0:T(8,128)(2,1)S(1)}, u32[]{:S(2)}, u32[]{:S(2)}) collective-permute-start(bf16[144,384]{1,0:T(8,128)(2,1)S(1)} %get-tuple-element.26), channel_id=1, source_target_pairs={{0,8},{2,10},{4,12},{6,14},{8,0},{10,2},{12,4},{14,6},{1,9},{3,11}... | collective-permute-start | bytes 331784 | tf_op jit(solution)/shard_map/ppermute | solution.py:139
  34.0 7.0 %collective-permute-done.12.first_ref = bf16[144,384]{1,0:T(8,128)(2,1)S(1)} collective-permute-done((bf16[144,384]{1,0:T(8,128)(2,1)S(1)}, bf16[144,384]{1,0:T(8,128)(2,1)S(1)}, u32[]{:S(2)}, u32[]{:S(2)}) %collective-permute-start.12) | collective-permute-done | bytes 110624 | tf_op jit(solution)/shard_map/ppermute | solution.py:139
  41.0 0.0 collective-permute-start.13
  41.0 1.3 %collective-permute-done.13.second_ref = bf16[144,384]{1,0:T(8,128)(2,1)S(1)} collective-permute-done((bf16[144,384]{1,0:T(8,128)(2,1)S(1)}, bf16[144,384]{1,0:T(8,128)(2,1)S(1)}, u32[]{:S(2)}, u32[]{:S(2)}) %collective-permute-start.13) | collective-permute-done | bytes 110624 | tf_op jit(solution)/shard_map/ppermute | solution.py:139
  42.3 0.0 collective-permute-done.9.w4
  42.3 0.0 collective-permute-done.10.w5
  42.3 0.0 collective-permute-done.11.w6
  42.3 0.0 copy-done
  42.3 1.2 %shard_map.97 = bf16[128,384]{1,0:T(8,128)(2,1)S(1)} custom-call(bf16[144,384]{1,0:T(8,128)(2,1)S(1)} %collective-permute-done.12.first_ref, bf16[144,384]{1,0:T(8,128)(2,1)S(1)} %collective-permute-done.13.second_ref, bf16[10,96,384]{2,1,0:T(8,128)(2,1)S(1)} %bitcast.8, bf16[5,96,384]{2,1,0:T(8,128)(2,1)S(1)} %collective-permute-done.6.w1, ...), custom_call_target="tpu_custom_call" | custom-call | tf_op jit(solution)/shard_map/pallas_call | solution.py:144
  43.5 3.4 %collective-permute-start.14 = (bf16[128,384]{1,0:T(8,128)(2,1)S(1)}, bf16[128,384]{1,0:T(8,128)(2,1)S(1)}, u32[]{:S(2)}, u32[]{:S(2)}) collective-permute-start(bf16[128,384]{1,0:T(8,128)(2,1)S(1)} %shard_map.97), channel_id=1, source_target_pairs={{0,8},{2,10},{4,12},{6,14},{8,0},{10,2},{12,4},{14,6},{1,9},{3,11}... | collective-permute-start | bytes 294920 | tf_op jit(solution)/shard_map/ppermute | solution.py:139
  47.0 1.0 %shard_map.96 = f32[128,384]{1,0:T(8,128)S(1)} custom-call(bf16[144,768]{1,0:T(8,128)(2,1)S(1)} %get-tuple-element.21.active_ref, f32[128,384]{1,0:T(8,128)S(1)} %get-tuple-element.22.base_ref, bf16[10,96,384]{2,1,0:T(8,128)(2,1)S(1)} %bitcast.9, bf16[5,96,384]{2,1,0:T(8,128)(2,1)S(1)} %collective-permute-done.6.w1, ...), custom_call_target="tpu_custom_call" | custom-call | tf_op jit(solution)/shard_map/pallas_call | solution.py:144
  48.0 2.1 %collective-permute-done.14 = bf16[128,384]{1,0:T(8,128)(2,1)S(1)} collective-permute-done((bf16[128,384]{1,0:T(8,128)(2,1)S(1)}, bf16[128,384]{1,0:T(8,128)(2,1)S(1)}, u32[]{:S(2)}, u32[]{:S(2)}) %collective-permute-start.14) | collective-permute-done | bytes 98336 | tf_op jit(solution)/shard_map/ppermute | solution.py:139
  50.1 0.7 %fusion = bf16[1,128,384]{2,1,0:T(8,128)(2,1)} fusion(f32[128,384]{1,0:T(8,128)S(1)} %shard_map.96, bf16[128,384]{1,0:T(8,128)(2,1)S(1)} %collective-permute-done.14), kind=kLoop, calls=%fused_computation.2 | loop fusion | flops 147456 | bytes 393216 | tf_op jit(solution)/shard_map/broadcast_in_dim | solution.py:513
  (2 shorter events, 0.0 us)
Async XLA Ops:
  0.0 19.8 %copy-start.1 = (bf16[1536,512]{1,0:T(8,128)(2,1)S(1)}, bf16[1536,512]{1,0:T(8,128)(2,1)}, u32[]{:S(2)}) copy-start(bf16[1536,512]{1,0:T(8,128)(2,1)} %query_weight_ref.1) | copy-start | bytes 4718596
  0.0 20.3 %copy-start.2 = (bf16[512,1536]{1,0:T(8,128)(2,1)S(1)}, bf16[512,1536]{1,0:T(8,128)(2,1)}, u32[]{:S(2)}) copy-start(bf16[512,1536]{1,0:T(8,128)(2,1)} %out_weight_ref.1) | copy-start | bytes 4718596
  0.0 20.3 %copy-start.4 = (f32[1536]{0:T(1024)S(1)}, f32[1536]{0:T(1024)}, u32[]{:S(2)}) copy-start(f32[1536]{0:T(1024)} %gain_ref.2) | copy-start | bytes 18436
  0.0 20.3 %copy-start.5 = (f32[1,4,4,32]{3,2,1,0:T(4,128)S(1)}, f32[1,4,4,32]{3,2,1,0:T(4,128)}, u32[]{:S(2)}) copy-start(f32[1,4,4,32]{3,2,1,0:T(4,128)} %bias_ref.1) | copy-start | bytes 6148
  1.7 16.5 %collective-permute-start.6 = (bf16[5,96,384]{2,1,0:T(8,128)(2,1)S(1)}, bf16[5,96,384]{2,1,0:T(8,128)(2,1)S(1)}, u32[]{:S(2)}, u32[]{:S(2)}) collective-permute-start(bf16[5,96,384]{2,1,0:T(8,128)(2,1)S(1)} %get-tuple-element.25), channel_id=1, source_target_pairs={{0,2},{2,0},{4,6},{6,4},{8,10},{10,8},{12,14},{14,12},{1,3},{3,1},... | collective-permute-start | bytes 1105928 | tf_op jit(solution)/shard_map/ppermute | solution.py:139
  4.8 4.7 %collective-permute-start = (bf16[1,48,256]{2,1,0:T(8,128)(2,1)S(1)}, bf16[1,48,256]{2,1,0:T(8,128)(2,1)S(1)}, u32[]{:S(2)}, u32[]{:S(2)}) collective-permute-start(bf16[1,48,256]{2,1,0:T(8,128)(2,1)S(1)} %bitcast.12), channel_id=1, source_target_pairs={{0,8},{2,10},{4,12},{6,14},{8,0},{10,2},{12,4},{14,6},{1,9},{3,11}... | collective-permute-start | bytes 73736 | tf_op jit(solution)/shard_map/ppermute | solution.py:139
  9.5 4.1 %collective-permute-start.1 = (bf16[2,48,256]{2,1,0:T(8,128)(2,1)S(1)}, bf16[2,48,256]{2,1,0:T(8,128)(2,1)S(1)}, u32[]{:S(2)}, u32[]{:S(2)}) collective-permute-start(bf16[2,48,256]{2,1,0:T(8,128)(2,1)S(1)} %shard_map.92.first_ref), channel_id=1, source_target_pairs={{0,4},{2,6},{4,0},{6,2},{8,12},{10,14},{12,8},{14,10},{1,5},{3,7},... | collective-permute-start | bytes 147464 | tf_op jit(solution)/shard_map/ppermute | solution.py:139
  13.6 4.7 %collective-permute-start.3 = (bf16[4,48,256]{2,1,0:T(8,128)(2,1)S(1)}, bf16[4,48,256]{2,1,0:T(8,128)(2,1)S(1)}, u32[]{:S(2)}, u32[]{:S(2)}) collective-permute-start(bf16[4,48,256]{2,1,0:T(8,128)(2,1)S(1)} %shard_map.93.near_ref), channel_id=1, source_target_pairs={{0,2},{2,0},{4,6},{6,4},{8,10},{10,8},{12,14},{14,12},{1,3},{3,1},... | collective-permute-start | bytes 294920 | tf_op jit(solution)/shard_map/ppermute | solution.py:139
  14.1 6.2 %collective-permute-start.2 = (bf16[4,48,256]{2,1,0:T(8,128)(2,1)S(1)}, bf16[4,48,256]{2,1,0:T(8,128)(2,1)S(1)}, u32[]{:S(2)}, u32[]{:S(2)}) collective-permute-start(bf16[4,48,256]{2,1,0:T(8,128)(2,1)S(1)} %shard_map.93.near_ref), channel_id=1, source_target_pairs={{0,1},{1,0},{2,3},{3,2},{4,5},{5,4},{6,7},{7,6},{8,9},{9,8},{10,11... | collective-permute-start | bytes 294920 | tf_op jit(solution)/shard_map/ppermute | solution.py:139
  14.1 11.0 %collective-permute-start.8 = (bf16[5,96,384]{2,1,0:T(8,128)(2,1)S(1)}, bf16[5,96,384]{2,1,0:T(8,128)(2,1)S(1)}, u32[]{:S(2)}, u32[]{:S(2)}) collective-permute-start(bf16[5,96,384]{2,1,0:T(8,128)(2,1)S(1)} %get-tuple-element.25), channel_id=1, source_target_pairs={{0,4},{2,6},{4,0},{6,2},{8,12},{10,14},{12,8},{14,10},{1,5},{3,7},... | collective-permute-start | bytes 1105928 | tf_op jit(solution)/shard_map/ppermute | solution.py:139
  18.3 2.0 %collective-permute-start.4 = (bf16[4,48,256]{2,1,0:T(8,128)(2,1)S(1)}, bf16[4,48,256]{2,1,0:T(8,128)(2,1)S(1)}, u32[]{:S(2)}, u32[]{:S(2)}) collective-permute-start(bf16[4,48,256]{2,1,0:T(8,128)(2,1)S(1)} %collective-permute-done.3.side_ref), channel_id=1, source_target_pairs={{0,1},{1,0},{2,3},{3,2},{4,5},{5,4},{6,7},{7,6},{8,9},{9,8},{10,11... | collective-permute-start | bytes 294920 | tf_op jit(solution)/shard_map/ppermute | solution.py:139
  18.3 11.4 %collective-permute-start.7 = (bf16[5,96,384]{2,1,0:T(8,128)(2,1)S(1)}, bf16[5,96,384]{2,1,0:T(8,128)(2,1)S(1)}, u32[]{:S(2)}, u32[]{:S(2)}) collective-permute-start(bf16[5,96,384]{2,1,0:T(8,128)(2,1)S(1)} %collective-permute-done.6.w1), channel_id=1, source_target_pairs={{0,16},{16,0},{1,17},{17,1},{2,18},{18,2},{3,19},{19,3},{4,20},{20... | collective-permute-start | bytes 1105928 | tf_op jit(solution)/shard_map/ppermute | solution.py:139
  20.2 3.5 %copy-start.3 = (bf16[1,128,1536]{2,1,0:T(8,128)(2,1)S(1)}, bf16[1,128,1536]{2,1,0:T(8,128)(2,1)}, u32[]{:S(2)}) copy-start(bf16[1,128,1536]{2,1,0:T(8,128)(2,1)} %param.9) | copy-start | bytes 1179652
  20.2 3.5 %copy-start.6 = (f32[1536]{0:T(1024)S(1)}, f32[1536]{0:T(1024)}, u32[]{:S(2)}) copy-start(f32[1536]{0:T(1024)} %gain_ref.3) | copy-start | bytes 18436
  20.2 3.5 %copy-start.7 = (f32[384]{0:T(512)S(1)}, f32[384]{0:T(512)}, u32[]{:S(2)}) copy-start(f32[384]{0:T(512)} %dec_bias_ref.1) | copy-start | bytes 4612
  20.2 22.1 %copy-start = (bf16[5,192,384]{2,1,0:T(8,128)(2,1)S(1)}, bf16[5,192,384]{2,1,0:T(8,128)(2,1)}, u32[]{:S(2)}) copy-start(bf16[5,192,384]{2,1,0:T(8,128)(2,1)} %param.16) | copy-start | bytes 2211844
  22.1 1.6 %collective-permute-start.5 = (bf16[80,1536]{1,0:T(8,128)(2,1)S(1)}, bf16[80,1536]{1,0:T(8,128)(2,1)S(1)}, u32[]{:S(2)}, u32[]{:S(2)}) collective-permute-start(bf16[80,1536]{1,0:T(8,128)(2,1)S(1)} %get-tuple-element.20.own_ref), channel_id=1, source_target_pairs={{0,1},{1,0},{2,3},{3,2},{4,5},{5,4},{6,7},{7,6},{8,9},{9,8},{10,11... | collective-permute-start | bytes 737288 | tf_op jit(solution)/shard_map/ppermute | solution.py:139
  25.1 17.2 %collective-permute-start.9 = (bf16[5,96,384]{2,1,0:T(8,128)(2,1)S(1)}, bf16[5,96,384]{2,1,0:T(8,128)(2,1)S(1)}, u32[]{:S(2)}, u32[]{:S(2)}) collective-permute-start(bf16[5,96,384]{2,1,0:T(8,128)(2,1)S(1)} %collective-permute-done.8.w3), channel_id=1, source_target_pairs={{0,16},{16,0},{1,17},{17,1},{2,18},{18,2},{3,19},{19,3},{4,20},{20... | collective-permute-start | bytes 1105928 | tf_op jit(solution)/shard_map/ppermute | solution.py:139
  26.7 15.6 %collective-permute-start.10 = (bf16[5,96,384]{2,1,0:T(8,128)(2,1)S(1)}, bf16[5,96,384]{2,1,0:T(8,128)(2,1)S(1)}, u32[]{:S(2)}, u32[]{:S(2)}) collective-permute-start(bf16[5,96,384]{2,1,0:T(8,128)(2,1)S(1)} %collective-permute-done.8.w3), channel_id=1, source_target_pairs={{0,2},{2,0},{4,6},{6,4},{8,10},{10,8},{12,14},{14,12},{1,3},{3,1},... | collective-permute-start | bytes 1105928 | tf_op jit(solution)/shard_map/ppermute | solution.py:139
  29.7 12.6 %collective-permute-start.11 = (bf16[5,96,384]{2,1,0:T(8,128)(2,1)S(1)}, bf16[5,96,384]{2,1,0:T(8,128)(2,1)S(1)}, u32[]{:S(2)}, u32[]{:S(2)}) collective-permute-start(bf16[5,96,384]{2,1,0:T(8,128)(2,1)S(1)} %collective-permute-done.7.w2), channel_id=1, source_target_pairs={{0,4},{2,6},{4,0},{6,2},{8,12},{10,14},{12,8},{14,10},{1,5},{3,7},... | collective-permute-start | bytes 1105928 | tf_op jit(solution)/shard_map/ppermute | solution.py:139
  31.2 9.7 %collective-permute-start.12 = (bf16[144,384]{1,0:T(8,128)(2,1)S(1)}, bf16[144,384]{1,0:T(8,128)(2,1)S(1)}, u32[]{:S(2)}, u32[]{:S(2)}) collective-permute-start(bf16[144,384]{1,0:T(8,128)(2,1)S(1)} %get-tuple-element.26), channel_id=1, source_target_pairs={{0,8},{2,10},{4,12},{6,14},{8,0},{10,2},{12,4},{14,6},{1,9},{3,11}... | collective-permute-start | bytes 331784 | tf_op jit(solution)/shard_map/ppermute | solution.py:139
  41.0 1.3 %collective-permute-start.13 = (bf16[144,384]{1,0:T(8,128)(2,1)S(1)}, bf16[144,384]{1,0:T(8,128)(2,1)S(1)}, u32[]{:S(2)}, u32[]{:S(2)}) collective-permute-start(bf16[144,384]{1,0:T(8,128)(2,1)S(1)} %collective-permute-done.12.first_ref), channel_id=1, source_target_pairs={{0,1},{1,0},{2,3},{3,2},{4,5},{5,4},{6,7},{7,6},{8,9},{9,8},{10,11... | collective-permute-start | bytes 331784 | tf_op jit(solution)/shard_map/ppermute | solution.py:139
  43.5 6.6 %collective-permute-start.14 = (bf16[128,384]{1,0:T(8,128)(2,1)S(1)}, bf16[128,384]{1,0:T(8,128)(2,1)S(1)}, u32[]{:S(2)}, u32[]{:S(2)}) collective-permute-start(bf16[128,384]{1,0:T(8,128)(2,1)S(1)} %shard_map.97), channel_id=1, source_target_pairs={{0,8},{2,10},{4,12},{6,14},{8,0},{10,2},{12,4},{14,6},{1,9},{3,11}... | collective-permute-start | bytes 294920 | tf_op jit(solution)/shard_map/ppermute | solution.py:139

commit v5 on v4

--- a/solution.py
+++ b/solution.py
@@ -255,7 +255,7 @@
 
 
 def swap_bits(value):
-    return 4 * (value & 1) + (value & 2) + (value & 4) // 4
+    return (value & 1) + 2 * (value & 2) + (value & 4) // 2
 
 
 def attention_kernel(
@@ -476,13 +476,15 @@
     def behind(values_in, gate):
         return lax.optimization_barrier((values_in, gate))[0]
 
-    near = joined(message[None], 4)
-    side = exchange(piece, "seq", 1)
-    near = joined(near, 2)
-    after = exchange(behind(piece, near), "seq", 2)
-    across = exchange(near, "seq", 1)
+    after = exchange(piece, "seq", 2)
+    near = joined(message[None], 1)
+    side = exchange(behind(piece, near), "seq", 1)
+    near = joined(near, 4)
+    across = exchange(near, "seq", 2)
     near_other = exchange(near, "section", 1)
+    after_rest = exchange(behind(after, near), "groups", 1)
     side_rest = exchange(behind(side, near), "groups", 1)
+    across, side = lax.optimization_barrier((across, side))
     across_other = exchange(across, "section", 1)
     queries = jnp.dot(normed, query_weight, preferred_element_type=f32).astype(bf16)
     terms, edges = call(
@@ -491,6 +493,7 @@
         [queries, near, near_other, across, across_other, query_weight, attn_gain, pair_bias, out_weight],
     )
     other = exchange(terms, "section", 1)
+    far = exchange(behind(after, terms), "seq", 1)
     keep, send, base = call(
         activate_kernel,
         [((rows + 16, channels // 2), bf16), ((rows + 16, channels // 4), bf16), ((rows, width), f32)],
@@ -498,10 +501,7 @@
         [pltpu.VMEM((channels // 128, rows + extra, 128), f32) for extra in (0, 16)],
     )
     first = exchange(send, "seq", 4)
-    held = behind(after, send)
-    after_rest = exchange(held, "groups", 1)
-    far = exchange(held, "seq", 1)
-    far_rest = exchange(behind(side_rest, send), "seq", 2)
+    far_rest = exchange(behind(after_rest, send), "seq", 1)
     second = exchange(first, "section", 1)
     weights = [chunks, side, side_rest, after, after_rest, far, far_rest]
     scratch = [pltpu.VMEM((8 * taps, depth // 2, width), bf16)]

time: 50.9 us -> 53.9 us (1.059)
  waiting for transfers between devices: 20.9 us -> 26.5 us
  starting transfers between devices: 22.1 us -> 19.4 us
    ppermute x15, waiting for transfers between devices: 20.9 us -> 26.5 us  [exchange(): return lax.ppermute(values_in, axis, [(i, i ^ mask) for i in range(count)])]
    ppermute x15, starting transfers between devices: 22.1 us -> 19.4 us  [exchange(): return lax.ppermute(values_in, axis, [(i, i ^ mask) for i in range(count)])]
where the time goes in v5:
time: 53.9 us; the launch traced here: 53.8 us
  waiting for transfers between devices  26.5 us (49%)
  starting transfers between devices  19.4 us (36%)
  Pallas kernels  6.61 us (12%)
  other arithmetic  0.67 us (1%)
    ppermute x15, waiting for transfers between devices, exchange(): return lax.ppermute(values_in, axis, [(i, i ^ mask) for i in range(count)])  26.5 us
    ppermute x15, starting transfers between devices, exchange(): return lax.ppermute(values_in, axis, [(i, i ^ mask) for i in range(count)])  19.4 us
    pallas_call x7, Pallas kernels, call(): pl.pallas_call(kernel, out_shape=[jax.ShapeDtypeStruct(shape, kind) for s...  6.61 us
  transfers between devices with their start and end apart: 15, of which 9 were waited for; matrix products, arithmetic and copies ran while one was open for 1% of the time, Pallas kernels for 7%

profile of v5, /device:TPU:0, one launch (start us, length us, event | category | flops | bytes accessed | tf_op | source)
XLA Modules:
  0.0 53.8 jit_solution(351398085516900667)
XLA Ops:
  0.0 0.0 copy-start.1
  0.0 0.0 copy-start.2
  0.0 0.0 copy-start.4
  0.0 0.0 copy-start.5
  0.0 1.7 %shard_map.91 = (bf16[48,256]{1,0:T(8,128)(2,1)S(1)}, bf16[64,1536]{1,0:T(8,128)(2,1)S(1)}, bf16[5,96,384]{2,1,0:T(8,128)(2,1)S(1)}) custom-call(bf16[128,1536]{1,0:T(8,128)(2,1)} %bitcast.10, f32[1536]{0:T(1024)} %gain_ref.2, bf16[1536,256]{1,0:T(8,128)(2,1)} %weight_hbm.1, f32[1,4,4,32]{3,2,1,0:T(4,128)} %bias_ref.1, bf16[10,96,384]{2,1,0:T(8,128)(2,1)} %bitcast.7), custom_call_target="tpu_custom_call" | custom-call | tf_op jit(solution)/shard_map/pallas_call | solution.py:144
  1.7 3.0 %collective-permute-start = (bf16[1,48,256]{2,1,0:T(8,128)(2,1)S(1)}, bf16[1,48,256]{2,1,0:T(8,128)(2,1)S(1)}, u32[]{:S(2)}, u32[]{:S(2)}) collective-permute-start(bf16[1,48,256]{2,1,0:T(8,128)(2,1)S(1)} %bitcast.12), channel_id=1, source_target_pairs={{0,2},{2,0},{4,6},{6,4},{8,10},{10,8},{12,14},{14,12},{1,3},{3,1},... | collective-permute-start | bytes 73736 | tf_op jit(solution)/shard_map/ppermute | solution.py:139
  4.8 1.6 %collective-permute-start.8 = (bf16[5,96,384]{2,1,0:T(8,128)(2,1)S(1)}, bf16[5,96,384]{2,1,0:T(8,128)(2,1)S(1)}, u32[]{:S(2)}, u32[]{:S(2)}) collective-permute-start(bf16[5,96,384]{2,1,0:T(8,128)(2,1)S(1)} %get-tuple-element.23), channel_id=1, source_target_pairs={{0,4},{2,6},{4,0},{6,2},{8,12},{10,14},{12,8},{14,10},{1,5},{3,7},... | collective-permute-start | bytes 1105928 | tf_op jit(solution)/shard_map/ppermute | solution.py:139
  6.3 0.2 collective-permute-done.second_ref
  6.6 2.0 %collective-permute-start.4 = (bf16[5,96,384]{2,1,0:T(8,128)(2,1)S(1)}, bf16[5,96,384]{2,1,0:T(8,128)(2,1)S(1)}, u32[]{:S(2)}, u32[]{:S(2)}) collective-permute-start(bf16[5,96,384]{2,1,0:T(8,128)(2,1)S(1)} %get-tuple-element.23), channel_id=1, source_target_pairs={{0,2},{2,0},{4,6},{6,4},{8,10},{10,8},{12,14},{14,12},{1,3},{3,1},... | collective-permute-start | bytes 1105928 | tf_op jit(solution)/shard_map/ppermute | solution.py:139
  8.6 2.6 %collective-permute-start.1 = (bf16[2,48,256]{2,1,0:T(8,128)(2,1)S(1)}, bf16[2,48,256]{2,1,0:T(8,128)(2,1)S(1)}, u32[]{:S(2)}, u32[]{:S(2)}) collective-permute-start(bf16[2,48,256]{2,1,0:T(8,128)(2,1)S(1)} %shard_map.92.first_ref), channel_id=1, source_target_pairs={{0,8},{2,10},{4,12},{6,14},{8,0},{10,2},{12,4},{14,6},{1,9},{3,11}... | collective-permute-start | bytes 147464 | tf_op jit(solution)/shard_map/ppermute | solution.py:139
  11.2 3.8 %collective-permute-done.1.second_ref = bf16[2,48,256]{2,1,0:T(8,128)(2,1)S(1)} collective-permute-done((bf16[2,48,256]{2,1,0:T(8,128)(2,1)S(1)}, bf16[2,48,256]{2,1,0:T(8,128)(2,1)S(1)}, u32[]{:S(2)}, u32[]{:S(2)}) %collective-permute-start.1) | collective-permute-done | bytes 49184 | tf_op jit(solution)/shard_map/ppermute | solution.py:139
  15.0 3.6 %collective-permute-start.3 = (bf16[4,48,256]{2,1,0:T(8,128)(2,1)S(1)}, bf16[4,48,256]{2,1,0:T(8,128)(2,1)S(1)}, u32[]{:S(2)}, u32[]{:S(2)}) collective-permute-start(bf16[4,48,256]{2,1,0:T(8,128)(2,1)S(1)} %shard_map.93.near_ref), channel_id=1, source_target_pairs={{0,4},{2,6},{4,0},{6,2},{8,12},{10,14},{12,8},{14,10},{1,5},{3,7},... | collective-permute-start | bytes 294920 | tf_op jit(solution)/shard_map/ppermute | solution.py:139
  18.5 0.0 collective-permute-start.2
  18.5 0.0 collective-permute-done.8.w3
  18.5 1.5 %collective-permute-start.9 = (bf16[5,96,384]{2,1,0:T(8,128)(2,1)S(1)}, bf16[5,96,384]{2,1,0:T(8,128)(2,1)S(1)}, u32[]{:S(2)}, u32[]{:S(2)}) collective-permute-start(bf16[5,96,384]{2,1,0:T(8,128)(2,1)S(1)} %collective-permute-done.8.w3), channel_id=1, source_target_pairs={{0,16},{16,0},{1,17},{17,1},{2,18},{18,2},{3,19},{19,3},{4,20},{20... | collective-permute-start | bytes 1105928 | tf_op jit(solution)/shard_map/ppermute | solution.py:139
  20.1 1.1 %collective-permute-done.3.side_ref = bf16[4,48,256]{2,1,0:T(8,128)(2,1)S(1)} collective-permute-done((bf16[4,48,256]{2,1,0:T(8,128)(2,1)S(1)}, bf16[4,48,256]{2,1,0:T(8,128)(2,1)S(1)}, u32[]{:S(2)}, u32[]{:S(2)}) %collective-permute-start.3) | collective-permute-done | bytes 98336 | tf_op jit(solution)/shard_map/ppermute | solution.py:139
  21.1 0.0 collective-permute-done.4.w1
  21.1 0.0 collective-permute-start.5
  21.1 0.0 copy-done.1
  21.1 0.4 convolution_convert_fusion.query_ref
  21.5 0.0 copy-start.3
  21.5 0.0 copy-start.6
  21.6 0.0 copy-start.7
  21.6 0.0 copy-start
  21.6 0.0 collective-permute-done.2.near_other_ref
  21.6 0.8 %collective-permute-done.5.side_other_ref = bf16[4,48,256]{2,1,0:T(8,128)(2,1)S(1)} collective-permute-done((bf16[4,48,256]{2,1,0:T(8,128)(2,1)S(1)}, bf16[4,48,256]{2,1,0:T(8,128)(2,1)S(1)}, u32[]{:S(2)}, u32[]{:S(2)}) %collective-permute-start.5) | collective-permute-done | bytes 98336 | tf_op jit(solution)/shard_map/ppermute | solution.py:139
  22.4 0.0 copy-done.2
  22.4 0.0 copy-done.4
  22.4 0.0 copy-done.5
  22.4 1.8 %shard_map.94 = (bf16[80,1536]{1,0:T(8,128)(2,1)S(1)}, f32[8,1536]{1,0:T(8,128)S(1)}) custom-call(bf16[64,512]{1,0:T(8,128)(2,1)S(1)} %convolution_convert_fusion.query_ref, bf16[4,48,256]{2,1,0:T(8,128)(2,1)S(1)} %shard_map.93.near_ref, bf16[4,48,256]{2,1,0:T(8,128)(2,1)S(1)} %collective-permute-done.2.near_other_ref, ...), custom_call_target="tpu_custom_call" | custom-call | tf_op jit(solution)/shard_map/pallas_call | solution.py:144
  24.3 0.2 collective-permute-start.6
  24.5 1.5 %collective-permute-start.7 = (bf16[5,96,384]{2,1,0:T(8,128)(2,1)S(1)}, bf16[5,96,384]{2,1,0:T(8,128)(2,1)S(1)}, u32[]{:S(2)}, u32[]{:S(2)}) collective-permute-start(bf16[5,96,384]{2,1,0:T(8,128)(2,1)S(1)} %collective-permute-done.4.w1), channel_id=1, source_target_pairs={{0,16},{16,0},{1,17},{17,1},{2,18},{18,2},{3,19},{19,3},{4,20},{20... | collective-permute-start | bytes 1105928 | tf_op jit(solution)/shard_map/ppermute | solution.py:139
  26.0 0.5 collective-permute-start.10
  26.6 0.0 collective-permute-done.6.other_ref
  26.6 0.0 copy-done.3
  26.6 0.0 copy-done.6
  26.6 0.0 copy-done.7
  26.6 0.7 %shard_map.95 = (bf16[144,768]{1,0:T(8,128)(2,1)S(1)}, bf16[144,384]{1,0:T(8,128)(2,1)S(1)}, f32[128,384]{1,0:T(8,128)S(1)}) custom-call(bf16[128,1536]{1,0:T(8,128)(2,1)S(1)} %bitcast.11, f32[8,1536]{1,0:T(8,128)S(1)} %get-tuple-element.25.edge_ref, bf16[80,1536]{1,0:T(8,128)(2,1)S(1)} %get-tuple-element.26.own_ref, ...), custom_call_target="tpu_custom_call" | custom-call | tf_op jit(solution)/shard_map/pallas_call | solution.py:144
  27.3 2.6 %collective-permute-done.9.w4 = bf16[5,96,384]{2,1,0:T(8,128)(2,1)S(1)} collective-permute-done((bf16[5,96,384]{2,1,0:T(8,128)(2,1)S(1)}, bf16[5,96,384]{2,1,0:T(8,128)(2,1)S(1)}, u32[]{:S(2)}, u32[]{:S(2)}) %collective-permute-start.9) | collective-permute-done | bytes 368672 | tf_op jit(solution)/shard_map/ppermute | solution.py:139
  29.9 0.5 collective-permute-start.11
  30.5 0.4 collective-permute-start.12
  30.8 6.9 %collective-permute-done.12.first_ref = bf16[144,384]{1,0:T(8,128)(2,1)S(1)} collective-permute-done((bf16[144,384]{1,0:T(8,128)(2,1)S(1)}, bf16[144,384]{1,0:T(8,128)(2,1)S(1)}, u32[]{:S(2)}, u32[]{:S(2)}) %collective-permute-start.12) | collective-permute-done | bytes 110624 | tf_op jit(solution)/shard_map/ppermute | solution.py:139
  37.7 0.0 collective-permute-start.13
  37.8 0.0 collective-permute-done.7.w2
  37.8 0.0 collective-permute-done.10.w5
  37.8 1.3 %collective-permute-done.13.second_ref = bf16[144,384]{1,0:T(8,128)(2,1)S(1)} collective-permute-done((bf16[144,384]{1,0:T(8,128)(2,1)S(1)}, bf16[144,384]{1,0:T(8,128)(2,1)S(1)}, u32[]{:S(2)}, u32[]{:S(2)}) %collective-permute-start.13) | collective-permute-done | bytes 110624 | tf_op jit(solution)/shard_map/ppermute | solution.py:139
  39.1 5.4 %collective-permute-done.11.w6 = bf16[5,96,384]{2,1,0:T(8,128)(2,1)S(1)} collective-permute-done((bf16[5,96,384]{2,1,0:T(8,128)(2,1)S(1)}, bf16[5,96,384]{2,1,0:T(8,128)(2,1)S(1)}, u32[]{:S(2)}, u32[]{:S(2)}) %collective-permute-start.11) | collective-permute-done | bytes 368672 | tf_op jit(solution)/shard_map/ppermute | solution.py:139
  44.5 0.0 copy-done
  44.5 1.2 %shard_map.97 = bf16[128,384]{1,0:T(8,128)(2,1)S(1)} custom-call(bf16[144,384]{1,0:T(8,128)(2,1)S(1)} %collective-permute-done.12.first_ref, bf16[144,384]{1,0:T(8,128)(2,1)S(1)} %collective-permute-done.13.second_ref, bf16[10,96,384]{2,1,0:T(8,128)(2,1)S(1)} %bitcast.8, bf16[5,96,384]{2,1,0:T(8,128)(2,1)S(1)} %collective-permute-done.4.w1, ...), custom_call_target="tpu_custom_call" | custom-call | tf_op jit(solution)/shard_map/pallas_call | solution.py:144
  45.7 2.0 %collective-permute-start.14 = (bf16[128,384]{1,0:T(8,128)(2,1)S(1)}, bf16[128,384]{1,0:T(8,128)(2,1)S(1)}, u32[]{:S(2)}, u32[]{:S(2)}) collective-permute-start(bf16[128,384]{1,0:T(8,128)(2,1)S(1)} %shard_map.97), channel_id=1, source_target_pairs={{0,8},{2,10},{4,12},{6,14},{8,0},{10,2},{12,4},{14,6},{1,9},{3,11}... | collective-permute-start | bytes 294920 | tf_op jit(solution)/shard_map/ppermute | solution.py:139
  47.7 1.1 %shard_map.96 = f32[128,384]{1,0:T(8,128)S(1)} custom-call(bf16[144,768]{1,0:T(8,128)(2,1)S(1)} %get-tuple-element.27.active_ref, f32[128,384]{1,0:T(8,128)S(1)} %get-tuple-element.28.base_ref, bf16[10,96,384]{2,1,0:T(8,128)(2,1)S(1)} %bitcast.9, bf16[5,96,384]{2,1,0:T(8,128)(2,1)S(1)} %collective-permute-done.4.w1, ...), custom_call_target="tpu_custom_call" | custom-call | tf_op jit(solution)/shard_map/pallas_call | solution.py:144
  48.8 4.4 %collective-permute-done.14 = bf16[128,384]{1,0:T(8,128)(2,1)S(1)} collective-permute-done((bf16[128,384]{1,0:T(8,128)(2,1)S(1)}, bf16[128,384]{1,0:T(8,128)(2,1)S(1)}, u32[]{:S(2)}, u32[]{:S(2)}) %collective-permute-start.14) | collective-permute-done | bytes 98336 | tf_op jit(solution)/shard_map/ppermute | solution.py:139
  53.1 0.7 %fusion = bf16[1,128,384]{2,1,0:T(8,128)(2,1)} fusion(f32[128,384]{1,0:T(8,128)S(1)} %shard_map.96, bf16[128,384]{1,0:T(8,128)(2,1)S(1)} %collective-permute-done.14), kind=kLoop, calls=%fused_computation.2 | loop fusion | flops 147456 | bytes 393216 | tf_op jit(solution)/shard_map/broadcast_in_dim | solution.py:513
  (2 shorter events, 0.0 us)
Async XLA Ops:
  0.0 21.1 %copy-start.1 = (bf16[1536,512]{1,0:T(8,128)(2,1)S(1)}, bf16[1536,512]{1,0:T(8,128)(2,1)}, u32[]{:S(2)}) copy-start(bf16[1536,512]{1,0:T(8,128)(2,1)} %query_weight_ref.1) | copy-start | bytes 4718596
  0.0 22.4 %copy-start.2 = (bf16[512,1536]{1,0:T(8,128)(2,1)S(1)}, bf16[512,1536]{1,0:T(8,128)(2,1)}, u32[]{:S(2)}) copy-start(bf16[512,1536]{1,0:T(8,128)(2,1)} %out_weight_ref.1) | copy-start | bytes 4718596
  0.0 22.4 %copy-start.4 = (f32[1536]{0:T(1024)S(1)}, f32[1536]{0:T(1024)}, u32[]{:S(2)}) copy-start(f32[1536]{0:T(1024)} %gain_ref.2) | copy-start | bytes 18436
  0.0 22.4 %copy-start.5 = (f32[1,4,4,32]{3,2,1,0:T(4,128)S(1)}, f32[1,4,4,32]{3,2,1,0:T(4,128)}, u32[]{:S(2)}) copy-start(f32[1,4,4,32]{3,2,1,0:T(4,128)} %bias_ref.1) | copy-start | bytes 6148
  1.7 4.8 %collective-permute-start = (bf16[1,48,256]{2,1,0:T(8,128)(2,1)S(1)}, bf16[1,48,256]{2,1,0:T(8,128)(2,1)S(1)}, u32[]{:S(2)}, u32[]{:S(2)}) collective-permute-start(bf16[1,48,256]{2,1,0:T(8,128)(2,1)S(1)} %bitcast.12), channel_id=1, source_target_pairs={{0,2},{2,0},{4,6},{6,4},{8,10},{10,8},{12,14},{14,12},{1,3},{3,1},... | collective-permute-start | bytes 73736 | tf_op jit(solution)/shard_map/ppermute | solution.py:139
  4.8 13.8 %collective-permute-start.8 = (bf16[5,96,384]{2,1,0:T(8,128)(2,1)S(1)}, bf16[5,96,384]{2,1,0:T(8,128)(2,1)S(1)}, u32[]{:S(2)}, u32[]{:S(2)}) collective-permute-start(bf16[5,96,384]{2,1,0:T(8,128)(2,1)S(1)} %get-tuple-element.23), channel_id=1, source_target_pairs={{0,4},{2,6},{4,0},{6,2},{8,12},{10,14},{12,8},{14,10},{1,5},{3,7},... | collective-permute-start | bytes 1105928 | tf_op jit(solution)/shard_map/ppermute | solution.py:139
  6.6 14.6 %collective-permute-start.4 = (bf16[5,96,384]{2,1,0:T(8,128)(2,1)S(1)}, bf16[5,96,384]{2,1,0:T(8,128)(2,1)S(1)}, u32[]{:S(2)}, u32[]{:S(2)}) collective-permute-start(bf16[5,96,384]{2,1,0:T(8,128)(2,1)S(1)} %get-tuple-element.23), channel_id=1, source_target_pairs={{0,2},{2,0},{4,6},{6,4},{8,10},{10,8},{12,14},{14,12},{1,3},{3,1},... | collective-permute-start | bytes 1105928 | tf_op jit(solution)/shard_map/ppermute | solution.py:139
  8.6 6.4 %collective-permute-start.1 = (bf16[2,48,256]{2,1,0:T(8,128)(2,1)S(1)}, bf16[2,48,256]{2,1,0:T(8,128)(2,1)S(1)}, u32[]{:S(2)}, u32[]{:S(2)}) collective-permute-start(bf16[2,48,256]{2,1,0:T(8,128)(2,1)S(1)} %shard_map.92.first_ref), channel_id=1, source_target_pairs={{0,8},{2,10},{4,12},{6,14},{8,0},{10,2},{12,4},{14,6},{1,9},{3,11}... | collective-permute-start | bytes 147464 | tf_op jit(solution)/shard_map/ppermute | solution.py:139
  15.0 6.2 %collective-permute-start.3 = (bf16[4,48,256]{2,1,0:T(8,128)(2,1)S(1)}, bf16[4,48,256]{2,1,0:T(8,128)(2,1)S(1)}, u32[]{:S(2)}, u32[]{:S(2)}) collective-permute-start(bf16[4,48,256]{2,1,0:T(8,128)(2,1)S(1)} %shard_map.93.near_ref), channel_id=1, source_target_pairs={{0,4},{2,6},{4,0},{6,2},{8,12},{10,14},{12,8},{14,10},{1,5},{3,7},... | collective-permute-start | bytes 294920 | tf_op jit(solution)/shard_map/ppermute | solution.py:139
  18.5 3.0 %collective-permute-start.2 = (bf16[4,48,256]{2,1,0:T(8,128)(2,1)S(1)}, bf16[4,48,256]{2,1,0:T(8,128)(2,1)S(1)}, u32[]{:S(2)}, u32[]{:S(2)}) collective-permute-start(bf16[4,48,256]{2,1,0:T(8,128)(2,1)S(1)} %shard_map.93.near_ref), channel_id=1, source_target_pairs={{0,1},{1,0},{2,3},{3,2},{4,5},{5,4},{6,7},{7,6},{8,9},{9,8},{10,11... | collective-permute-start | bytes 294920 | tf_op jit(solution)/shard_map/ppermute | solution.py:139
  18.5 11.4 %collective-permute-start.9 = (bf16[5,96,384]{2,1,0:T(8,128)(2,1)S(1)}, bf16[5,96,384]{2,1,0:T(8,128)(2,1)S(1)}, u32[]{:S(2)}, u32[]{:S(2)}) collective-permute-start(bf16[5,96,384]{2,1,0:T(8,128)(2,1)S(1)} %collective-permute-done.8.w3), channel_id=1, source_target_pairs={{0,16},{16,0},{1,17},{17,1},{2,18},{18,2},{3,19},{19,3},{4,20},{20... | collective-permute-start | bytes 1105928 | tf_op jit(solution)/shard_map/ppermute | solution.py:139
  21.1 1.3 %collective-permute-start.5 = (bf16[4,48,256]{2,1,0:T(8,128)(2,1)S(1)}, bf16[4,48,256]{2,1,0:T(8,128)(2,1)S(1)}, u32[]{:S(2)}, u32[]{:S(2)}) collective-permute-start(bf16[4,48,256]{2,1,0:T(8,128)(2,1)S(1)} %collective-permute-done.3.side_ref), channel_id=1, source_target_pairs={{0,1},{1,0},{2,3},{3,2},{4,5},{5,4},{6,7},{7,6},{8,9},{9,8},{10,11... | collective-permute-start | bytes 294920 | tf_op jit(solution)/shard_map/ppermute | solution.py:139
  21.5 5.0 %copy-start.3 = (bf16[1,128,1536]{2,1,0:T(8,128)(2,1)S(1)}, bf16[1,128,1536]{2,1,0:T(8,128)(2,1)}, u32[]{:S(2)}) copy-start(bf16[1,128,1536]{2,1,0:T(8,128)(2,1)} %param.9) | copy-start | bytes 1179652
  21.5 5.0 %copy-start.6 = (f32[1536]{0:T(1024)S(1)}, f32[1536]{0:T(1024)}, u32[]{:S(2)}) copy-start(f32[1536]{0:T(1024)} %gain_ref.3) | copy-start | bytes 18436
  21.6 5.0 %copy-start.7 = (f32[384]{0:T(512)S(1)}, f32[384]{0:T(512)}, u32[]{:S(2)}) copy-start(f32[384]{0:T(512)} %dec_bias_ref.1) | copy-start | bytes 4612
  21.6 22.9 %copy-start = (bf16[5,192,384]{2,1,0:T(8,128)(2,1)S(1)}, bf16[5,192,384]{2,1,0:T(8,128)(2,1)}, u32[]{:S(2)}) copy-start(bf16[5,192,384]{2,1,0:T(8,128)(2,1)} %param.16) | copy-start | bytes 2211844
  24.3 2.3 %collective-permute-start.6 = (bf16[80,1536]{1,0:T(8,128)(2,1)S(1)}, bf16[80,1536]{1,0:T(8,128)(2,1)S(1)}, u32[]{:S(2)}, u32[]{:S(2)}) collective-permute-start(bf16[80,1536]{1,0:T(8,128)(2,1)S(1)} %get-tuple-element.26.own_ref), channel_id=1, source_target_pairs={{0,1},{1,0},{2,3},{3,2},{4,5},{5,4},{6,7},{7,6},{8,9},{9,8},{10,11... | collective-permute-start | bytes 737288 | tf_op jit(solution)/shard_map/ppermute | solution.py:139
  24.5 13.3 %collective-permute-start.7 = (bf16[5,96,384]{2,1,0:T(8,128)(2,1)S(1)}, bf16[5,96,384]{2,1,0:T(8,128)(2,1)S(1)}, u32[]{:S(2)}, u32[]{:S(2)}) collective-permute-start(bf16[5,96,384]{2,1,0:T(8,128)(2,1)S(1)} %collective-permute-done.4.w1), channel_id=1, source_target_pairs={{0,16},{16,0},{1,17},{17,1},{2,18},{18,2},{3,19},{19,3},{4,20},{20... | collective-permute-start | bytes 1105928 | tf_op jit(solution)/shard_map/ppermute | solution.py:139
  26.0 11.7 %collective-permute-start.10 = (bf16[5,96,384]{2,1,0:T(8,128)(2,1)S(1)}, bf16[5,96,384]{2,1,0:T(8,128)(2,1)S(1)}, u32[]{:S(2)}, u32[]{:S(2)}) collective-permute-start(bf16[5,96,384]{2,1,0:T(8,128)(2,1)S(1)} %collective-permute-done.8.w3), channel_id=1, source_target_pairs={{0,2},{2,0},{4,6},{6,4},{8,10},{10,8},{12,14},{14,12},{1,3},{3,1},... | collective-permute-start | bytes 1105928 | tf_op jit(solution)/shard_map/ppermute | solution.py:139
  29.9 14.6 %collective-permute-start.11 = (bf16[5,96,384]{2,1,0:T(8,128)(2,1)S(1)}, bf16[5,96,384]{2,1,0:T(8,128)(2,1)S(1)}, u32[]{:S(2)}, u32[]{:S(2)}) collective-permute-start(bf16[5,96,384]{2,1,0:T(8,128)(2,1)S(1)} %collective-permute-done.9.w4), channel_id=1, source_target_pairs={{0,2},{2,0},{4,6},{6,4},{8,10},{10,8},{12,14},{14,12},{1,3},{3,1},... | collective-permute-start | bytes 1105928 | tf_op jit(solution)/shard_map/ppermute | solution.py:139
  30.5 7.3 %collective-permute-start.12 = (bf16[144,384]{1,0:T(8,128)(2,1)S(1)}, bf16[144,384]{1,0:T(8,128)(2,1)S(1)}, u32[]{:S(2)}, u32[]{:S(2)}) collective-permute-start(bf16[144,384]{1,0:T(8,128)(2,1)S(1)} %get-tuple-element.33), channel_id=1, source_target_pairs={{0,8},{2,10},{4,12},{6,14},{8,0},{10,2},{12,4},{14,6},{1,9},{3,11}... | collective-permute-start | bytes 331784 | tf_op jit(solution)/shard_map/ppermute | solution.py:139
  37.7 1.3 %collective-permute-start.13 = (bf16[144,384]{1,0:T(8,128)(2,1)S(1)}, bf16[144,384]{1,0:T(8,128)(2,1)S(1)}, u32[]{:S(2)}, u32[]{:S(2)}) collective-permute-start(bf16[144,384]{1,0:T(8,128)(2,1)S(1)} %collective-permute-done.12.first_ref), channel_id=1, source_target_pairs={{0,1},{1,0},{2,3},{3,2},{4,5},{5,4},{6,7},{7,6},{8,9},{9,8},{10,11... | collective-permute-start | bytes 331784 | tf_op jit(solution)/shard_map/ppermute | solution.py:139
  45.7 7.4 %collective-permute-start.14 = (bf16[128,384]{1,0:T(8,128)(2,1)S(1)}, bf16[128,384]{1,0:T(8,128)(2,1)S(1)}, u32[]{:S(2)}, u32[]{:S(2)}) collective-permute-start(bf16[128,384]{1,0:T(8,128)(2,1)S(1)} %shard_map.97), channel_id=1, source_target_pairs={{0,8},{2,10},{4,12},{6,14},{8,0},{10,2},{12,4},{14,6},{1,9},{3,11}... | collective-permute-start | bytes 294920 | tf_op jit(solution)/shard_map/ppermute | solution.py:139

commit v6 on v4

--- a/solution.py
+++ b/solution.py
@@ -254,8 +254,12 @@
     out_ref[count:] = second_ref[...]
 
 
-def swap_bits(value):
-    return 4 * (value & 1) + (value & 2) + (value & 4) // 4
+def slot_of(distance):
+    return distance // 2 + 4 * (distance & 1)
+
+
+def distance_of(slot):
+    return 2 * (slot & 3) + slot // 4
 
 
 def attention_kernel(
@@ -274,8 +278,8 @@
     me = lax.axis_index("seq")
     section = lax.axis_index("section")
     count = lax.axis_size("seq")
-    low_slot = swap_bits(me ^ jnp.maximum(me - 1, 0))
-    high_slot = swap_bits(me ^ jnp.minimum(me + 1, count - 1))
+    low_slot = slot_of(me ^ jnp.maximum(me - 1, 0))
+    high_slot = slot_of(me ^ jnp.minimum(me + 1, count - 1))
 
     def block_of(slot, near, side):
         return jnp.where(
@@ -315,7 +319,7 @@
     cell = lax.broadcasted_iota(jnp.int32, (32, 512), 0)
     column = lax.broadcasted_iota(jnp.int32, (32, 512), 1)
     inner = 2 * (((column >> 5) & 1) ^ section) + ((column & 31) >> 4)
-    wanted = 4 * (swap_bits(column >> 6) ^ me) + inner
+    wanted = 4 * (distance_of(column >> 6) ^ me) + inner
     spread = jnp.where(cell == wanted, 1.0, 0.0).astype(jnp.bfloat16)
     bias = jnp.zeros((24, 512), jnp.float32)
     for n, term in enumerate(split_three(own_bias(bias_ref))):
@@ -476,13 +480,14 @@
     def behind(values_in, gate):
         return lax.optimization_barrier((values_in, gate))[0]
 
-    near = joined(message[None], 4)
+    near = joined(message[None], 2)
     side = exchange(piece, "seq", 1)
-    near = joined(near, 2)
     after = exchange(behind(piece, near), "seq", 2)
+    received, side = lax.optimization_barrier((exchange(near, "seq", 4), side))
+    near = call(join_kernel, [((4, MSG, 256), bf16)], [near, received])[0]
     across = exchange(near, "seq", 1)
     near_other = exchange(near, "section", 1)
-    side_rest = exchange(behind(side, near), "groups", 1)
+    side_rest = exchange(side, "groups", 1)
     across_other = exchange(across, "section", 1)
     queries = jnp.dot(normed, query_weight, preferred_element_type=f32).astype(bf16)
     terms, edges = call(
@@ -490,7 +495,11 @@
         [((ROWS, channels), bf16), ((8, channels), f32)],
         [queries, near, near_other, across, across_other, query_weight, attn_gain, pair_bias, out_weight],
     )
+    terms, after = lax.optimization_barrier((terms, after))
     other = exchange(terms, "section", 1)
+    after_rest = exchange(after, "groups", 1)
+    far = exchange(after, "seq", 1)
+    far_rest = exchange(behind(side_rest, terms), "seq", 2)
     keep, send, base = call(
         activate_kernel,
         [((rows + 16, channels // 2), bf16), ((rows + 16, channels // 4), bf16), ((rows, width), f32)],
@@ -498,10 +507,7 @@
         [pltpu.VMEM((channels // 128, rows + extra, 128), f32) for extra in (0, 16)],
     )
     first = exchange(send, "seq", 4)
-    held = behind(after, send)
-    after_rest = exchange(held, "groups", 1)
-    far = exchange(held, "seq", 1)
-    far_rest = exchange(behind(side_rest, send), "seq", 2)
+    first, far_rest = lax.optimization_barrier((first, far_rest))
     second = exchange(first, "section", 1)
     weights = [chunks, side, side_rest, after, after_rest, far, far_rest]
     scratch = [pltpu.VMEM((8 * taps, depth // 2, width), bf16)]

time: 50.9 us -> 47 us (0.923)
  the two profiles are of different devices: /device:TPU:0 before, /device:TPU:2 now
where the time goes in v6:
time: 47 us; the launch traced here: 46.9 us
  waiting for transfers between devices  22.6 us (48%)
  starting transfers between devices  16.5 us (35%)
  Pallas kernels  6.58 us (14%)
  other arithmetic  0.66 us (1%)
    ppermute x15, waiting for transfers between devices, exchange(): return lax.ppermute(values_in, axis, [(i, i ^ mask) for i in range(count)])  22.6 us
    ppermute x15, starting transfers between devices, exchange(): return lax.ppermute(values_in, axis, [(i, i ^ mask) for i in range(count)])  16.5 us
    pallas_call x7, Pallas kernels, call(): pl.pallas_call(kernel, out_shape=[jax.ShapeDtypeStruct(shape, kind) for s...  6.58 us
  transfers between devices with their start and end apart: 15, of which 11 were waited for; matrix products, arithmetic and copies ran while one was open for 1% of the time, Pallas kernels for 8%

profile of v6, /device:TPU:2, one launch (start us, length us, event | category | flops | bytes accessed | tf_op | source)
XLA Modules:
  0.0 46.9 jit_solution(11594735106238205189)
XLA Ops:
  0.0 0.0 copy-start.1
  0.0 0.0 copy-start.2
  0.0 0.0 copy-start.4
  0.0 0.0 copy-start.5
  0.0 1.7 %shard_map.91 = (bf16[48,256]{1,0:T(8,128)(2,1)S(1)}, bf16[64,1536]{1,0:T(8,128)(2,1)S(1)}, bf16[5,96,384]{2,1,0:T(8,128)(2,1)S(1)}) custom-call(bf16[128,1536]{1,0:T(8,128)(2,1)} %bitcast.10, f32[1536]{0:T(1024)} %gain_ref.2, bf16[1536,256]{1,0:T(8,128)(2,1)} %weight_hbm.1, f32[1,4,4,32]{3,2,1,0:T(4,128)} %bias_ref.1, bf16[10,96,384]{2,1,0:T(8,128)(2,1)} %bitcast.7), custom_call_target="tpu_custom_call" | custom-call | tf_op jit(solution)/shard_map/pallas_call | solution.py:144
  1.8 0.1 collective-permute-start.2
  1.8 2.1 %collective-permute-start = (bf16[1,48,256]{2,1,0:T(8,128)(2,1)S(1)}, bf16[1,48,256]{2,1,0:T(8,128)(2,1)S(1)}, u32[]{:S(2)}, u32[]{:S(2)}) collective-permute-start(bf16[1,48,256]{2,1,0:T(8,128)(2,1)S(1)} %bitcast.12), channel_id=1, source_target_pairs={{0,4},{2,6},{4,0},{6,2},{8,12},{10,14},{12,8},{14,10},{1,5},{3,7},... | collective-permute-start | bytes 73736 | tf_op jit(solution)/shard_map/ppermute | solution.py:139
  3.9 1.8 %collective-permute-done.second_ref = bf16[1,48,256]{2,1,0:T(8,128)(2,1)S(1)} collective-permute-done((bf16[1,48,256]{2,1,0:T(8,128)(2,1)S(1)}, bf16[1,48,256]{2,1,0:T(8,128)(2,1)S(1)}, u32[]{:S(2)}, u32[]{:S(2)}) %collective-permute-start) | collective-permute-done | bytes 24608 | tf_op jit(solution)/shard_map/ppermute | solution.py:139
  5.7 3.0 %collective-permute-start.1 = (bf16[2,48,256]{2,1,0:T(8,128)(2,1)S(1)}, bf16[2,48,256]{2,1,0:T(8,128)(2,1)S(1)}, u32[]{:S(2)}, u32[]{:S(2)}) collective-permute-start(bf16[2,48,256]{2,1,0:T(8,128)(2,1)S(1)} %shard_map.92.first_ref), channel_id=1, source_target_pairs={{0,8},{2,10},{4,12},{6,14},{8,0},{10,2},{12,4},{14,6},{1,9},{3,11}... | collective-permute-start | bytes 147464 | tf_op jit(solution)/shard_map/ppermute | solution.py:139
  8.8 2.1 %collective-permute-done.1.second_ref = bf16[2,48,256]{2,1,0:T(8,128)(2,1)S(1)} collective-permute-done((bf16[2,48,256]{2,1,0:T(8,128)(2,1)S(1)}, bf16[2,48,256]{2,1,0:T(8,128)(2,1)S(1)}, u32[]{:S(2)}, u32[]{:S(2)}) %collective-permute-start.1) | collective-permute-done | bytes 49184 | tf_op jit(solution)/shard_map/ppermute | solution.py:139
  10.8 1.3 %collective-permute-done.2.w1 = bf16[5,96,384]{2,1,0:T(8,128)(2,1)S(1)} collective-permute-done((bf16[5,96,384]{2,1,0:T(8,128)(2,1)S(1)}, bf16[5,96,384]{2,1,0:T(8,128)(2,1)S(1)}, u32[]{:S(2)}, u32[]{:S(2)}) %collective-permute-start.2) | collective-permute-done | bytes 368672 | tf_op jit(solution)/shard_map/ppermute | solution.py:139
  12.2 0.6 %collective-permute-start.4 = (bf16[4,48,256]{2,1,0:T(8,128)(2,1)S(1)}, bf16[4,48,256]{2,1,0:T(8,128)(2,1)S(1)}, u32[]{:S(2)}, u32[]{:S(2)}) collective-permute-start(bf16[4,48,256]{2,1,0:T(8,128)(2,1)S(1)} %shard_map.93.near_ref), channel_id=1, source_target_pairs={{0,2},{2,0},{4,6},{6,4},{8,10},{10,8},{12,14},{14,12},{1,3},{3,1},... | collective-permute-start | bytes 294920 | tf_op jit(solution)/shard_map/ppermute | solution.py:139
  12.8 1.6 %collective-permute-start.6 = (bf16[5,96,384]{2,1,0:T(8,128)(2,1)S(1)}, bf16[5,96,384]{2,1,0:T(8,128)(2,1)S(1)}, u32[]{:S(2)}, u32[]{:S(2)}) collective-permute-start(bf16[5,96,384]{2,1,0:T(8,128)(2,1)S(1)} %get-tuple-element.27), channel_id=1, source_target_pairs={{0,4},{2,6},{4,0},{6,2},{8,12},{10,14},{12,8},{14,10},{1,5},{3,7},... | collective-permute-start | bytes 1105928 | tf_op jit(solution)/shard_map/ppermute | solution.py:139
  14.3 1.5 %collective-permute-start.8 = (bf16[5,96,384]{2,1,0:T(8,128)(2,1)S(1)}, bf16[5,96,384]{2,1,0:T(8,128)(2,1)S(1)}, u32[]{:S(2)}, u32[]{:S(2)}) collective-permute-start(bf16[5,96,384]{2,1,0:T(8,128)(2,1)S(1)} %collective-permute-done.2.w1), channel_id=1, source_target_pairs={{0,16},{16,0},{1,17},{17,1},{2,18},{18,2},{3,19},{19,3},{4,20},{20... | collective-permute-start | bytes 1105928 | tf_op jit(solution)/shard_map/ppermute | solution.py:139
  15.9 0.0 collective-permute-start.3
  15.9 1.0 %collective-permute-done.4.side_ref = bf16[4,48,256]{2,1,0:T(8,128)(2,1)S(1)} collective-permute-done((bf16[4,48,256]{2,1,0:T(8,128)(2,1)S(1)}, bf16[4,48,256]{2,1,0:T(8,128)(2,1)S(1)}, u32[]{:S(2)}, u32[]{:S(2)}) %collective-permute-start.4) | collective-permute-done | bytes 98336 | tf_op jit(solution)/shard_map/ppermute | solution.py:139
  16.8 0.0 collective-permute-start.5
  16.8 0.0 copy-done.1
  16.8 0.4 convolution_convert_fusion.query_ref
  17.2 0.0 copy-start.3
  17.2 0.0 copy-start.6
  17.3 0.0 copy-start.7
  17.3 0.0 copy-start
  17.3 0.0 collective-permute-done.3.near_other_ref
  17.3 0.8 %collective-permute-done.5.side_other_ref = bf16[4,48,256]{2,1,0:T(8,128)(2,1)S(1)} collective-permute-done((bf16[4,48,256]{2,1,0:T(8,128)(2,1)S(1)}, bf16[4,48,256]{2,1,0:T(8,128)(2,1)S(1)}, u32[]{:S(2)}, u32[]{:S(2)}) %collective-permute-start.5) | collective-permute-done | bytes 98336 | tf_op jit(solution)/shard_map/ppermute | solution.py:139
  18.1 0.0 copy-done.2
  18.1 0.0 copy-done.4
  18.1 0.0 copy-done.5
  18.2 1.8 %shard_map.94 = (bf16[80,1536]{1,0:T(8,128)(2,1)S(1)}, f32[8,1536]{1,0:T(8,128)S(1)}) custom-call(bf16[64,512]{1,0:T(8,128)(2,1)S(1)} %convolution_convert_fusion.query_ref, bf16[4,48,256]{2,1,0:T(8,128)(2,1)S(1)} %shard_map.93.near_ref, bf16[4,48,256]{2,1,0:T(8,128)(2,1)S(1)} %collective-permute-done.3.near_other_ref, ...), custom_call_target="tpu_custom_call" | custom-call | tf_op jit(solution)/shard_map/pallas_call | solution.py:144
  20.0 2.0 %collective-permute-done.6.w3 = bf16[5,96,384]{2,1,0:T(8,128)(2,1)S(1)} collective-permute-done((bf16[5,96,384]{2,1,0:T(8,128)(2,1)S(1)}, bf16[5,96,384]{2,1,0:T(8,128)(2,1)S(1)}, u32[]{:S(2)}, u32[]{:S(2)}) %collective-permute-start.6) | collective-permute-done | bytes 368672 | tf_op jit(solution)/shard_map/ppermute | solution.py:139
  22.0 1.2 %collective-permute-done.8.w2 = bf16[5,96,384]{2,1,0:T(8,128)(2,1)S(1)} collective-permute-done((bf16[5,96,384]{2,1,0:T(8,128)(2,1)S(1)}, bf16[5,96,384]{2,1,0:T(8,128)(2,1)S(1)}, u32[]{:S(2)}, u32[]{:S(2)}) %collective-permute-start.8) | collective-permute-done | bytes 368672 | tf_op jit(solution)/shard_map/ppermute | solution.py:139
  23.2 0.5 %collective-permute-start.12 = (bf16[5,96,384]{2,1,0:T(8,128)(2,1)S(1)}, bf16[5,96,384]{2,1,0:T(8,128)(2,1)S(1)}, u32[]{:S(2)}, u32[]{:S(2)}) collective-permute-start(bf16[5,96,384]{2,1,0:T(8,128)(2,1)S(1)} %collective-permute-done.8.w2), channel_id=1, source_target_pairs={{0,4},{2,6},{4,0},{6,2},{8,12},{10,14},{12,8},{14,10},{1,5},{3,7},... | collective-permute-start | bytes 1105928 | tf_op jit(solution)/shard_map/ppermute | solution.py:139
  23.8 0.0 collective-permute-start.7
  23.8 1.4 %collective-permute-start.10 = (bf16[5,96,384]{2,1,0:T(8,128)(2,1)S(1)}, bf16[5,96,384]{2,1,0:T(8,128)(2,1)S(1)}, u32[]{:S(2)}, u32[]{:S(2)}) collective-permute-start(bf16[5,96,384]{2,1,0:T(8,128)(2,1)S(1)} %collective-permute-done.6.w3), channel_id=1, source_target_pairs={{0,2},{2,0},{4,6},{6,4},{8,10},{10,8},{12,14},{14,12},{1,3},{3,1},... | collective-permute-start | bytes 1105928 | tf_op jit(solution)/shard_map/ppermute | solution.py:139
  25.2 1.5 %collective-permute-start.9 = (bf16[5,96,384]{2,1,0:T(8,128)(2,1)S(1)}, bf16[5,96,384]{2,1,0:T(8,128)(2,1)S(1)}, u32[]{:S(2)}, u32[]{:S(2)}) collective-permute-start(bf16[5,96,384]{2,1,0:T(8,128)(2,1)S(1)} %collective-permute-done.6.w3), channel_id=1, source_target_pairs={{0,16},{16,0},{1,17},{17,1},{2,18},{18,2},{3,19},{19,3},{4,20},{20... | collective-permute-start | bytes 1105928 | tf_op jit(solution)/shard_map/ppermute | solution.py:139
  26.7 0.0 collective-permute-done.7.other_ref
  26.7 0.0 copy-done.3
  26.7 0.0 copy-done.6
  26.7 0.0 copy-done.7
  26.7 0.7 %shard_map.95 = (bf16[144,768]{1,0:T(8,128)(2,1)S(1)}, bf16[144,384]{1,0:T(8,128)(2,1)S(1)}, f32[128,384]{1,0:T(8,128)S(1)}) custom-call(bf16[128,1536]{1,0:T(8,128)(2,1)S(1)} %bitcast.11, f32[8,1536]{1,0:T(8,128)S(1)} %get-tuple-element.25.edge_ref, bf16[80,1536]{1,0:T(8,128)(2,1)S(1)} %get-tuple-element.28.own_ref, ...), custom_call_target="tpu_custom_call" | custom-call | tf_op jit(solution)/shard_map/pallas_call | solution.py:144
  27.5 2.7 %collective-permute-start.11 = (bf16[144,384]{1,0:T(8,128)(2,1)S(1)}, bf16[144,384]{1,0:T(8,128)(2,1)S(1)}, u32[]{:S(2)}, u32[]{:S(2)}) collective-permute-start(bf16[144,384]{1,0:T(8,128)(2,1)S(1)} %get-tuple-element.33), channel_id=1, source_target_pairs={{0,8},{2,10},{4,12},{6,14},{8,0},{10,2},{12,4},{14,6},{1,9},{3,11}... | collective-permute-start | bytes 331784 | tf_op jit(solution)/shard_map/ppermute | solution.py:139
  30.1 5.6 %collective-permute-done.11.first_ref = bf16[144,384]{1,0:T(8,128)(2,1)S(1)} collective-permute-done((bf16[144,384]{1,0:T(8,128)(2,1)S(1)}, bf16[144,384]{1,0:T(8,128)(2,1)S(1)}, u32[]{:S(2)}, u32[]{:S(2)}) %collective-permute-start.11) | collective-permute-done | bytes 110624 | tf_op jit(solution)/shard_map/ppermute | solution.py:139
  35.8 0.0 collective-permute-done.12.w6
  35.8 0.0 collective-permute-start.13
  35.8 0.0 collective-permute-done.10.w5
  35.8 0.1 collective-permute-done.9.w4
  35.9 1.2 %collective-permute-done.13.second_ref = bf16[144,384]{1,0:T(8,128)(2,1)S(1)} collective-permute-done((bf16[144,384]{1,0:T(8,128)(2,1)S(1)}, bf16[144,384]{1,0:T(8,128)(2,1)S(1)}, u32[]{:S(2)}, u32[]{:S(2)}) %collective-permute-start.13) | collective-permute-done | bytes 110624 | tf_op jit(solution)/shard_map/ppermute | solution.py:139
  37.1 0.0 copy-done
  37.1 1.2 %shard_map.97 = bf16[128,384]{1,0:T(8,128)(2,1)S(1)} custom-call(bf16[144,384]{1,0:T(8,128)(2,1)S(1)} %collective-permute-done.11.first_ref, bf16[144,384]{1,0:T(8,128)(2,1)S(1)} %collective-permute-done.13.second_ref, bf16[10,96,384]{2,1,0:T(8,128)(2,1)S(1)} %bitcast.8, bf16[5,96,384]{2,1,0:T(8,128)(2,1)S(1)} %collective-permute-done.2.w1, ...), custom_call_target="tpu_custom_call" | custom-call | tf_op jit(solution)/shard_map/pallas_call | solution.py:144
  38.3 1.5 %collective-permute-start.14 = (bf16[128,384]{1,0:T(8,128)(2,1)S(1)}, bf16[128,384]{1,0:T(8,128)(2,1)S(1)}, u32[]{:S(2)}, u32[]{:S(2)}) collective-permute-start(bf16[128,384]{1,0:T(8,128)(2,1)S(1)} %shard_map.97), channel_id=1, source_target_pairs={{0,8},{2,10},{4,12},{6,14},{8,0},{10,2},{12,4},{14,6},{1,9},{3,11}... | collective-permute-start | bytes 294920 | tf_op jit(solution)/shard_map/ppermute | solution.py:139
  39.8 1.0 %shard_map.96 = f32[128,384]{1,0:T(8,128)S(1)} custom-call(bf16[144,768]{1,0:T(8,128)(2,1)S(1)} %get-tuple-element.29.active_ref, f32[128,384]{1,0:T(8,128)S(1)} %get-tuple-element.30.base_ref, bf16[10,96,384]{2,1,0:T(8,128)(2,1)S(1)} %bitcast.9, bf16[5,96,384]{2,1,0:T(8,128)(2,1)S(1)} %collective-permute-done.2.w1, ...), custom_call_target="tpu_custom_call" | custom-call | tf_op jit(solution)/shard_map/pallas_call | solution.py:144
  40.8 5.4 %collective-permute-done.14 = bf16[128,384]{1,0:T(8,128)(2,1)S(1)} collective-permute-done((bf16[128,384]{1,0:T(8,128)(2,1)S(1)}, bf16[128,384]{1,0:T(8,128)(2,1)S(1)}, u32[]{:S(2)}, u32[]{:S(2)}) %collective-permute-start.14) | collective-permute-done | bytes 98336 | tf_op jit(solution)/shard_map/ppermute | solution.py:139
  46.2 0.7 %fusion = bf16[1,128,384]{2,1,0:T(8,128)(2,1)} fusion(f32[128,384]{1,0:T(8,128)S(1)} %shard_map.96, bf16[128,384]{1,0:T(8,128)(2,1)S(1)} %collective-permute-done.14), kind=kLoop, calls=%fused_computation.2 | loop fusion | flops 147456 | bytes 393216 | tf_op jit(solution)/shard_map/broadcast_in_dim | solution.py:519
  (2 shorter events, 0.0 us)
Async XLA Ops:
  0.0 16.8 %copy-start.1 = (bf16[1536,512]{1,0:T(8,128)(2,1)S(1)}, bf16[1536,512]{1,0:T(8,128)(2,1)}, u32[]{:S(2)}) copy-start(bf16[1536,512]{1,0:T(8,128)(2,1)} %query_weight_ref.1) | copy-start | bytes 4718596
  0.0 18.1 %copy-start.2 = (bf16[512,1536]{1,0:T(8,128)(2,1)S(1)}, bf16[512,1536]{1,0:T(8,128)(2,1)}, u32[]{:S(2)}) copy-start(bf16[512,1536]{1,0:T(8,128)(2,1)} %out_weight_ref.1) | copy-start | bytes 4718596
  0.0 18.1 %copy-start.4 = (f32[1536]{0:T(1024)S(1)}, f32[1536]{0:T(1024)}, u32[]{:S(2)}) copy-start(f32[1536]{0:T(1024)} %gain_ref.2) | copy-start | bytes 18436
  0.0 18.1 %copy-start.5 = (f32[1,4,4,32]{3,2,1,0:T(4,128)S(1)}, f32[1,4,4,32]{3,2,1,0:T(4,128)}, u32[]{:S(2)}) copy-start(f32[1,4,4,32]{3,2,1,0:T(4,128)} %bias_ref.1) | copy-start | bytes 6148
  1.8 10.4 %collective-permute-start.2 = (bf16[5,96,384]{2,1,0:T(8,128)(2,1)S(1)}, bf16[5,96,384]{2,1,0:T(8,128)(2,1)S(1)}, u32[]{:S(2)}, u32[]{:S(2)}) collective-permute-start(bf16[5,96,384]{2,1,0:T(8,128)(2,1)S(1)} %get-tuple-element.27), channel_id=1, source_target_pairs={{0,2},{2,0},{4,6},{6,4},{8,10},{10,8},{12,14},{14,12},{1,3},{3,1},... | collective-permute-start | bytes 1105928 | tf_op jit(solution)/shard_map/ppermute | solution.py:139
  1.8 3.9 %collective-permute-start = (bf16[1,48,256]{2,1,0:T(8,128)(2,1)S(1)}, bf16[1,48,256]{2,1,0:T(8,128)(2,1)S(1)}, u32[]{:S(2)}, u32[]{:S(2)}) collective-permute-start(bf16[1,48,256]{2,1,0:T(8,128)(2,1)S(1)} %bitcast.12), channel_id=1, source_target_pairs={{0,4},{2,6},{4,0},{6,2},{8,12},{10,14},{12,8},{14,10},{1,5},{3,7},... | collective-permute-start | bytes 73736 | tf_op jit(solution)/shard_map/ppermute | solution.py:139
  5.7 5.1 %collective-permute-start.1 = (bf16[2,48,256]{2,1,0:T(8,128)(2,1)S(1)}, bf16[2,48,256]{2,1,0:T(8,128)(2,1)S(1)}, u32[]{:S(2)}, u32[]{:S(2)}) collective-permute-start(bf16[2,48,256]{2,1,0:T(8,128)(2,1)S(1)} %shard_map.92.first_ref), channel_id=1, source_target_pairs={{0,8},{2,10},{4,12},{6,14},{8,0},{10,2},{12,4},{14,6},{1,9},{3,11}... | collective-permute-start | bytes 147464 | tf_op jit(solution)/shard_map/ppermute | solution.py:139
  12.2 4.7 %collective-permute-start.4 = (bf16[4,48,256]{2,1,0:T(8,128)(2,1)S(1)}, bf16[4,48,256]{2,1,0:T(8,128)(2,1)S(1)}, u32[]{:S(2)}, u32[]{:S(2)}) collective-permute-start(bf16[4,48,256]{2,1,0:T(8,128)(2,1)S(1)} %shard_map.93.near_ref), channel_id=1, source_target_pairs={{0,2},{2,0},{4,6},{6,4},{8,10},{10,8},{12,14},{14,12},{1,3},{3,1},... | collective-permute-start | bytes 294920 | tf_op jit(solution)/shard_map/ppermute | solution.py:139
  12.8 9.3 %collective-permute-start.6 = (bf16[5,96,384]{2,1,0:T(8,128)(2,1)S(1)}, bf16[5,96,384]{2,1,0:T(8,128)(2,1)S(1)}, u32[]{:S(2)}, u32[]{:S(2)}) collective-permute-start(bf16[5,96,384]{2,1,0:T(8,128)(2,1)S(1)} %get-tuple-element.27), channel_id=1, source_target_pairs={{0,4},{2,6},{4,0},{6,2},{8,12},{10,14},{12,8},{14,10},{1,5},{3,7},... | collective-permute-start | bytes 1105928 | tf_op jit(solution)/shard_map/ppermute | solution.py:139
  14.3 8.9 %collective-permute-start.8 = (bf16[5,96,384]{2,1,0:T(8,128)(2,1)S(1)}, bf16[5,96,384]{2,1,0:T(8,128)(2,1)S(1)}, u32[]{:S(2)}, u32[]{:S(2)}) collective-permute-start(bf16[5,96,384]{2,1,0:T(8,128)(2,1)S(1)} %collective-permute-done.2.w1), channel_id=1, source_target_pairs={{0,16},{16,0},{1,17},{17,1},{2,18},{18,2},{3,19},{19,3},{4,20},{20... | collective-permute-start | bytes 1105928 | tf_op jit(solution)/shard_map/ppermute | solution.py:139
  15.9 1.4 %collective-permute-start.3 = (bf16[4,48,256]{2,1,0:T(8,128)(2,1)S(1)}, bf16[4,48,256]{2,1,0:T(8,128)(2,1)S(1)}, u32[]{:S(2)}, u32[]{:S(2)}) collective-permute-start(bf16[4,48,256]{2,1,0:T(8,128)(2,1)S(1)} %shard_map.93.near_ref), channel_id=1, source_target_pairs={{0,1},{1,0},{2,3},{3,2},{4,5},{5,4},{6,7},{7,6},{8,9},{9,8},{10,11... | collective-permute-start | bytes 294920 | tf_op jit(solution)/shard_map/ppermute | solution.py:139
  16.8 1.3 %collective-permute-start.5 = (bf16[4,48,256]{2,1,0:T(8,128)(2,1)S(1)}, bf16[4,48,256]{2,1,0:T(8,128)(2,1)S(1)}, u32[]{:S(2)}, u32[]{:S(2)}) collective-permute-start(bf16[4,48,256]{2,1,0:T(8,128)(2,1)S(1)} %collective-permute-done.4.side_ref), channel_id=1, source_target_pairs={{0,1},{1,0},{2,3},{3,2},{4,5},{5,4},{6,7},{7,6},{8,9},{9,8},{10,11... | collective-permute-start | bytes 294920 | tf_op jit(solution)/shard_map/ppermute | solution.py:139
  17.2 9.5 %copy-start.3 = (bf16[1,128,1536]{2,1,0:T(8,128)(2,1)S(1)}, bf16[1,128,1536]{2,1,0:T(8,128)(2,1)}, u32[]{:S(2)}) copy-start(bf16[1,128,1536]{2,1,0:T(8,128)(2,1)} %param.9) | copy-start | bytes 1179652
  17.2 9.5 %copy-start.6 = (f32[1536]{0:T(1024)S(1)}, f32[1536]{0:T(1024)}, u32[]{:S(2)}) copy-start(f32[1536]{0:T(1024)} %gain_ref.3) | copy-start | bytes 18436
  17.3 9.4 %copy-start.7 = (f32[384]{0:T(512)S(1)}, f32[384]{0:T(512)}, u32[]{:S(2)}) copy-start(f32[384]{0:T(512)} %dec_bias_ref.1) | copy-start | bytes 4612
  17.3 19.8 %copy-start = (bf16[5,192,384]{2,1,0:T(8,128)(2,1)S(1)}, bf16[5,192,384]{2,1,0:T(8,128)(2,1)}, u32[]{:S(2)}) copy-start(bf16[5,192,384]{2,1,0:T(8,128)(2,1)} %param.16) | copy-start | bytes 2211844
  23.2 12.5 %collective-permute-start.12 = (bf16[5,96,384]{2,1,0:T(8,128)(2,1)S(1)}, bf16[5,96,384]{2,1,0:T(8,128)(2,1)S(1)}, u32[]{:S(2)}, u32[]{:S(2)}) collective-permute-start(bf16[5,96,384]{2,1,0:T(8,128)(2,1)S(1)} %collective-permute-done.8.w2), channel_id=1, source_target_pairs={{0,4},{2,6},{4,0},{6,2},{8,12},{10,14},{12,8},{14,10},{1,5},{3,7},... | collective-permute-start | bytes 1105928 | tf_op jit(solution)/shard_map/ppermute | solution.py:139
  23.8 2.9 %collective-permute-start.7 = (bf16[80,1536]{1,0:T(8,128)(2,1)S(1)}, bf16[80,1536]{1,0:T(8,128)(2,1)S(1)}, u32[]{:S(2)}, u32[]{:S(2)}) collective-permute-start(bf16[80,1536]{1,0:T(8,128)(2,1)S(1)} %get-tuple-element.28.own_ref), channel_id=1, source_target_pairs={{0,1},{1,0},{2,3},{3,2},{4,5},{5,4},{6,7},{7,6},{8,9},{9,8},{10,11... | collective-permute-start | bytes 737288 | tf_op jit(solution)/shard_map/ppermute | solution.py:139
  23.8 12.0 %collective-permute-start.10 = (bf16[5,96,384]{2,1,0:T(8,128)(2,1)S(1)}, bf16[5,96,384]{2,1,0:T(8,128)(2,1)S(1)}, u32[]{:S(2)}, u32[]{:S(2)}) collective-permute-start(bf16[5,96,384]{2,1,0:T(8,128)(2,1)S(1)} %collective-permute-done.6.w3), channel_id=1, source_target_pairs={{0,2},{2,0},{4,6},{6,4},{8,10},{10,8},{12,14},{14,12},{1,3},{3,1},... | collective-permute-start | bytes 1105928 | tf_op jit(solution)/shard_map/ppermute | solution.py:139
  25.2 10.7 %collective-permute-start.9 = (bf16[5,96,384]{2,1,0:T(8,128)(2,1)S(1)}, bf16[5,96,384]{2,1,0:T(8,128)(2,1)S(1)}, u32[]{:S(2)}, u32[]{:S(2)}) collective-permute-start(bf16[5,96,384]{2,1,0:T(8,128)(2,1)S(1)} %collective-permute-done.6.w3), channel_id=1, source_target_pairs={{0,16},{16,0},{1,17},{17,1},{2,18},{18,2},{3,19},{19,3},{4,20},{20... | collective-permute-start | bytes 1105928 | tf_op jit(solution)/shard_map/ppermute | solution.py:139
  27.5 8.3 %collective-permute-start.11 = (bf16[144,384]{1,0:T(8,128)(2,1)S(1)}, bf16[144,384]{1,0:T(8,128)(2,1)S(1)}, u32[]{:S(2)}, u32[]{:S(2)}) collective-permute-start(bf16[144,384]{1,0:T(8,128)(2,1)S(1)} %get-tuple-element.33), channel_id=1, source_target_pairs={{0,8},{2,10},{4,12},{6,14},{8,0},{10,2},{12,4},{14,6},{1,9},{3,11}... | collective-permute-start | bytes 331784 | tf_op jit(solution)/shard_map/ppermute | solution.py:139
  35.8 1.3 %collective-permute-start.13 = (bf16[144,384]{1,0:T(8,128)(2,1)S(1)}, bf16[144,384]{1,0:T(8,128)(2,1)S(1)}, u32[]{:S(2)}, u32[]{:S(2)}) collective-permute-start(bf16[144,384]{1,0:T(8,128)(2,1)S(1)} %collective-permute-done.11.first_ref), channel_id=1, source_target_pairs={{0,1},{1,0},{2,3},{3,2},{4,5},{5,4},{6,7},{7,6},{8,9},{9,8},{10,11... | collective-permute-start | bytes 331784 | tf_op jit(solution)/shard_map/ppermute | solution.py:139
  38.3 7.9 %collective-permute-start.14 = (bf16[128,384]{1,0:T(8,128)(2,1)S(1)}, bf16[128,384]{1,0:T(8,128)(2,1)S(1)}, u32[]{:S(2)}, u32[]{:S(2)}) collective-permute-start(bf16[128,384]{1,0:T(8,128)(2,1)S(1)} %shard_map.97), channel_id=1, source_target_pairs={{0,8},{2,10},{4,12},{6,14},{8,0},{10,2},{12,4},{14,6},{1,9},{3,11}... | collective-permute-start | bytes 294920 | tf_op jit(solution)/shard_map/ppermute | solution.py:139

commit v7 on v6

--- a/solution.py
+++ b/solution.py
@@ -483,10 +483,10 @@
     near = joined(message[None], 2)
     side = exchange(piece, "seq", 1)
     after = exchange(behind(piece, near), "seq", 2)
-    received, side = lax.optimization_barrier((exchange(near, "seq", 4), side))
-    near = call(join_kernel, [((4, MSG, 256), bf16)], [near, received])[0]
+    near = joined(near, 4)
     across = exchange(near, "seq", 1)
-    near_other = exchange(near, "section", 1)
+    held, side = lax.optimization_barrier((near, side))
+    near_other = exchange(held, "section", 1)
     side_rest = exchange(side, "groups", 1)
     across_other = exchange(across, "section", 1)
     queries = jnp.dot(normed, query_weight, preferred_element_type=f32).astype(bf16)
@@ -507,7 +507,7 @@
         [pltpu.VMEM((channels // 128, rows + extra, 128), f32) for extra in (0, 16)],
     )
     first = exchange(send, "seq", 4)
-    first, far_rest = lax.optimization_barrier((first, far_rest))
+    first, far, far_rest = lax.optimization_barrier((first, far, far_rest))
     second = exchange(first, "section", 1)
     weights = [chunks, side, side_rest, after, after_rest, far, far_rest]
     scratch = [pltpu.VMEM((8 * taps, depth // 2, width), bf16)]

time: 47 us -> 45.1 us (0.960)
  the two profiles are of different devices: /device:TPU:2 before, /device:TPU:25 now
where the time goes in v7:
time: 45.1 us; the launch traced here: 44.9 us
  waiting for transfers between devices  22.3 us (49%)
  starting transfers between devices  14.8 us (33%)
  Pallas kernels  6.58 us (15%)
  other arithmetic  0.66 us (1%)
    ppermute x15, waiting for transfers between devices, exchange(): return lax.ppermute(values_in, axis, [(i, i ^ mask) for i in range(count)])  22.3 us
    ppermute x15, starting transfers between devices, exchange(): return lax.ppermute(values_in, axis, [(i, i ^ mask) for i in range(count)])  14.8 us
    pallas_call x7, Pallas kernels, call(): pl.pallas_call(kernel, out_shape=[jax.ShapeDtypeStruct(shape, kind) for s...  6.58 us
  transfers between devices with their start and end apart: 15, of which 10 were waited for; matrix products, arithmetic and copies ran while one was open for 1% of the time, Pallas kernels for 8%

profile of v7, /device:TPU:25, one launch (start us, length us, event | category | flops | bytes accessed | tf_op | source)
XLA Modules:
  0.0 44.9 jit_solution(6041272040618330078)
XLA Ops:
  0.0 0.0 copy-start.1
  0.0 0.0 copy-start.2
  0.0 0.0 copy-start.4
  0.0 0.0 copy-start.5
  0.0 1.7 %shard_map.91 = (bf16[48,256]{1,0:T(8,128)(2,1)S(1)}, bf16[64,1536]{1,0:T(8,128)(2,1)S(1)}, bf16[5,96,384]{2,1,0:T(8,128)(2,1)S(1)}) custom-call(bf16[128,1536]{1,0:T(8,128)(2,1)} %bitcast.10, f32[1536]{0:T(1024)} %gain_ref.2, bf16[1536,256]{1,0:T(8,128)(2,1)} %weight_hbm.1, f32[1,4,4,32]{3,2,1,0:T(4,128)} %bias_ref.1, bf16[10,96,384]{2,1,0:T(8,128)(2,1)} %bitcast.7), custom_call_target="tpu_custom_call" | custom-call | tf_op jit(solution)/shard_map/pallas_call | solution.py:144
  1.8 1.3 %collective-permute-start.2 = (bf16[5,96,384]{2,1,0:T(8,128)(2,1)S(1)}, bf16[5,96,384]{2,1,0:T(8,128)(2,1)S(1)}, u32[]{:S(2)}, u32[]{:S(2)}) collective-permute-start(bf16[5,96,384]{2,1,0:T(8,128)(2,1)S(1)} %get-tuple-element.28), channel_id=1, source_target_pairs={{0,2},{2,0},{4,6},{6,4},{8,10},{10,8},{12,14},{14,12},{1,3},{3,1},... | collective-permute-start | bytes 1105928 | tf_op jit(solution)/shard_map/ppermute | solution.py:139
  3.0 0.2 collective-permute-start
  3.2 2.8 %collective-permute-done.second_ref = bf16[1,48,256]{2,1,0:T(8,128)(2,1)S(1)} collective-permute-done((bf16[1,48,256]{2,1,0:T(8,128)(2,1)S(1)}, bf16[1,48,256]{2,1,0:T(8,128)(2,1)S(1)}, u32[]{:S(2)}, u32[]{:S(2)}) %collective-permute-start) | collective-permute-done | bytes 24608 | tf_op jit(solution)/shard_map/ppermute | solution.py:139
  6.0 0.1 collective-permute-start.1
  6.1 4.2 %collective-permute-done.1.second_ref = bf16[2,48,256]{2,1,0:T(8,128)(2,1)S(1)} collective-permute-done((bf16[2,48,256]{2,1,0:T(8,128)(2,1)S(1)}, bf16[2,48,256]{2,1,0:T(8,128)(2,1)S(1)}, u32[]{:S(2)}, u32[]{:S(2)}) %collective-permute-start.1) | collective-permute-done | bytes 49184 | tf_op jit(solution)/shard_map/ppermute | solution.py:139
  10.3 0.1 collective-permute-start.4
  10.4 0.1 collective-permute-start.6
  10.4 0.8 %collective-permute-done.2.w1 = bf16[5,96,384]{2,1,0:T(8,128)(2,1)S(1)} collective-permute-done((bf16[5,96,384]{2,1,0:T(8,128)(2,1)S(1)}, bf16[5,96,384]{2,1,0:T(8,128)(2,1)S(1)}, u32[]{:S(2)}, u32[]{:S(2)}) %collective-permute-start.2) | collective-permute-done | bytes 368672 | tf_op jit(solution)/shard_map/ppermute | solution.py:139
  11.3 1.2 %collective-permute-start.8 = (bf16[5,96,384]{2,1,0:T(8,128)(2,1)S(1)}, bf16[5,96,384]{2,1,0:T(8,128)(2,1)S(1)}, u32[]{:S(2)}, u32[]{:S(2)}) collective-permute-start(bf16[5,96,384]{2,1,0:T(8,128)(2,1)S(1)} %collective-permute-done.2.w1), channel_id=1, source_target_pairs={{0,16},{16,0},{1,17},{17,1},{2,18},{18,2},{3,19},{19,3},{4,20},{20... | collective-permute-start | bytes 1105928 | tf_op jit(solution)/shard_map/ppermute | solution.py:139
  12.5 1.3 %collective-permute-done.4.side_ref = bf16[4,48,256]{2,1,0:T(8,128)(2,1)S(1)} collective-permute-done((bf16[4,48,256]{2,1,0:T(8,128)(2,1)S(1)}, bf16[4,48,256]{2,1,0:T(8,128)(2,1)S(1)}, u32[]{:S(2)}, u32[]{:S(2)}) %collective-permute-start.4) | collective-permute-done | bytes 98336 | tf_op jit(solution)/shard_map/ppermute | solution.py:139
  13.8 4.1 %collective-permute-start.5 = (bf16[4,48,256]{2,1,0:T(8,128)(2,1)S(1)}, bf16[4,48,256]{2,1,0:T(8,128)(2,1)S(1)}, u32[]{:S(2)}, u32[]{:S(2)}) collective-permute-start(bf16[4,48,256]{2,1,0:T(8,128)(2,1)S(1)} %collective-permute-done.4.side_ref), channel_id=1, source_target_pairs={{0,1},{1,0},{2,3},{3,2},{4,5},{5,4},{6,7},{7,6},{8,9},{9,8},{10,11... | collective-permute-start | bytes 294920 | tf_op jit(solution)/shard_map/ppermute | solution.py:139
  17.9 0.0 collective-permute-start.3
  17.9 0.0 copy-done.1
  17.9 0.4 convolution_convert_fusion.query_ref
  18.3 0.0 copy-start.3
  18.3 0.0 copy-start.6
  18.3 0.0 copy-start.7
  18.3 0.0 copy-start
  18.4 0.5 %collective-permute-done.5.side_other_ref = bf16[4,48,256]{2,1,0:T(8,128)(2,1)S(1)} collective-permute-done((bf16[4,48,256]{2,1,0:T(8,128)(2,1)S(1)}, bf16[4,48,256]{2,1,0:T(8,128)(2,1)S(1)}, u32[]{:S(2)}, u32[]{:S(2)}) %collective-permute-start.5) | collective-permute-done | bytes 98336 | tf_op jit(solution)/shard_map/ppermute | solution.py:139
  18.9 0.4 collective-permute-done.3.near_other_ref
  19.2 0.0 copy-done.2
  19.2 0.0 copy-done.4
  19.2 0.0 copy-done.5
  19.2 1.8 %shard_map.94 = (bf16[80,1536]{1,0:T(8,128)(2,1)S(1)}, f32[8,1536]{1,0:T(8,128)S(1)}) custom-call(bf16[64,512]{1,0:T(8,128)(2,1)S(1)} %convolution_convert_fusion.query_ref, bf16[4,48,256]{2,1,0:T(8,128)(2,1)S(1)} %shard_map.93.near_ref, bf16[4,48,256]{2,1,0:T(8,128)(2,1)S(1)} %collective-permute-done.3.near_other_ref, ...), custom_call_target="tpu_custom_call" | custom-call | tf_op jit(solution)/shard_map/pallas_call | solution.py:144
  21.1 0.0 collective-permute-done.6.w3
  21.1 0.3 collective-permute-start.11
  21.4 0.0 collective-permute-done.8.w2
  21.4 0.2 collective-permute-start.12
  21.6 1.8 %collective-permute-start.7 = (bf16[80,1536]{1,0:T(8,128)(2,1)S(1)}, bf16[80,1536]{1,0:T(8,128)(2,1)S(1)}, u32[]{:S(2)}, u32[]{:S(2)}) collective-permute-start(bf16[80,1536]{1,0:T(8,128)(2,1)S(1)} %get-tuple-element.29.own_ref), channel_id=1, source_target_pairs={{0,1},{1,0},{2,3},{3,2},{4,5},{5,4},{6,7},{7,6},{8,9},{9,8},{10,11... | collective-permute-start | bytes 737288 | tf_op jit(solution)/shard_map/ppermute | solution.py:139
  23.4 1.2 %collective-permute-start.9 = (bf16[5,96,384]{2,1,0:T(8,128)(2,1)S(1)}, bf16[5,96,384]{2,1,0:T(8,128)(2,1)S(1)}, u32[]{:S(2)}, u32[]{:S(2)}) collective-permute-start(bf16[5,96,384]{2,1,0:T(8,128)(2,1)S(1)} %collective-permute-done.6.w3), channel_id=1, source_target_pairs={{0,16},{16,0},{1,17},{17,1},{2,18},{18,2},{3,19},{19,3},{4,20},{20... | collective-permute-start | bytes 1105928 | tf_op jit(solution)/shard_map/ppermute | solution.py:139
  24.6 0.0 collective-permute-done.7.other_ref
  24.6 0.0 copy-done.3
  24.6 0.0 copy-done.6
  24.6 0.0 copy-done.7
  24.6 0.7 %shard_map.95 = (bf16[144,768]{1,0:T(8,128)(2,1)S(1)}, bf16[144,384]{1,0:T(8,128)(2,1)S(1)}, f32[128,384]{1,0:T(8,128)S(1)}) custom-call(bf16[128,1536]{1,0:T(8,128)(2,1)S(1)} %bitcast.11, f32[8,1536]{1,0:T(8,128)S(1)} %get-tuple-element.26.edge_ref, bf16[80,1536]{1,0:T(8,128)(2,1)S(1)} %get-tuple-element.29.own_ref, ...), custom_call_target="tpu_custom_call" | custom-call | tf_op jit(solution)/shard_map/pallas_call | solution.py:144
  25.4 0.1 collective-permute-start.10
  25.5 5.8 %collective-permute-done.10.first_ref = bf16[144,384]{1,0:T(8,128)(2,1)S(1)} collective-permute-done((bf16[144,384]{1,0:T(8,128)(2,1)S(1)}, bf16[144,384]{1,0:T(8,128)(2,1)S(1)}, u32[]{:S(2)}, u32[]{:S(2)}) %collective-permute-start.10) | collective-permute-done | bytes 110624 | tf_op jit(solution)/shard_map/ppermute | solution.py:139
  31.2 0.0 collective-permute-done.11.w5
  31.2 0.4 collective-permute-done.12.w6
  31.7 3.1 %collective-permute-start.13 = (bf16[144,384]{1,0:T(8,128)(2,1)S(1)}, bf16[144,384]{1,0:T(8,128)(2,1)S(1)}, u32[]{:S(2)}, u32[]{:S(2)}) collective-permute-start(bf16[144,384]{1,0:T(8,128)(2,1)S(1)} %collective-permute-done.10.first_ref), channel_id=1, source_target_pairs={{0,1},{1,0},{2,3},{3,2},{4,5},{5,4},{6,7},{7,6},{8,9},{9,8},{10,11... | collective-permute-start | bytes 331784 | tf_op jit(solution)/shard_map/ppermute | solution.py:139
  34.8 0.0 collective-permute-done.9.w4
  34.8 1.0 %collective-permute-done.13.second_ref = bf16[144,384]{1,0:T(8,128)(2,1)S(1)} collective-permute-done((bf16[144,384]{1,0:T(8,128)(2,1)S(1)}, bf16[144,384]{1,0:T(8,128)(2,1)S(1)}, u32[]{:S(2)}, u32[]{:S(2)}) %collective-permute-start.13) | collective-permute-done | bytes 110624 | tf_op jit(solution)/shard_map/ppermute | solution.py:139
  35.7 0.0 copy-done
  35.7 1.2 %shard_map.97 = bf16[128,384]{1,0:T(8,128)(2,1)S(1)} custom-call(bf16[144,384]{1,0:T(8,128)(2,1)S(1)} %collective-permute-done.10.first_ref, bf16[144,384]{1,0:T(8,128)(2,1)S(1)} %collective-permute-done.13.second_ref, bf16[10,96,384]{2,1,0:T(8,128)(2,1)S(1)} %bitcast.8, bf16[5,96,384]{2,1,0:T(8,128)(2,1)S(1)} %collective-permute-done.2.w1, ...), custom_call_target="tpu_custom_call" | custom-call | tf_op jit(solution)/shard_map/pallas_call | solution.py:144
  37.0 1.1 %collective-permute-start.14 = (bf16[128,384]{1,0:T(8,128)(2,1)S(1)}, bf16[128,384]{1,0:T(8,128)(2,1)S(1)}, u32[]{:S(2)}, u32[]{:S(2)}) collective-permute-start(bf16[128,384]{1,0:T(8,128)(2,1)S(1)} %shard_map.97), channel_id=1, source_target_pairs={{0,8},{2,10},{4,12},{6,14},{8,0},{10,2},{12,4},{14,6},{1,9},{3,11}... | collective-permute-start | bytes 294920 | tf_op jit(solution)/shard_map/ppermute | solution.py:139
  38.1 1.0 %shard_map.96 = f32[128,384]{1,0:T(8,128)S(1)} custom-call(bf16[144,768]{1,0:T(8,128)(2,1)S(1)} %get-tuple-element.30.active_ref, f32[128,384]{1,0:T(8,128)S(1)} %get-tuple-element.31.base_ref, bf16[10,96,384]{2,1,0:T(8,128)(2,1)S(1)} %bitcast.9, bf16[5,96,384]{2,1,0:T(8,128)(2,1)S(1)} %collective-permute-done.2.w1, ...), custom_call_target="tpu_custom_call" | custom-call | tf_op jit(solution)/shard_map/pallas_call | solution.py:144
  39.1 5.1 %collective-permute-done.14 = bf16[128,384]{1,0:T(8,128)(2,1)S(1)} collective-permute-done((bf16[128,384]{1,0:T(8,128)(2,1)S(1)}, bf16[128,384]{1,0:T(8,128)(2,1)S(1)}, u32[]{:S(2)}, u32[]{:S(2)}) %collective-permute-start.14) | collective-permute-done | bytes 98336 | tf_op jit(solution)/shard_map/ppermute | solution.py:139
  44.3 0.7 %fusion = bf16[1,128,384]{2,1,0:T(8,128)(2,1)} fusion(f32[128,384]{1,0:T(8,128)S(1)} %shard_map.96, bf16[128,384]{1,0:T(8,128)(2,1)S(1)} %collective-permute-done.14), kind=kLoop, calls=%fused_computation.2 | loop fusion | flops 147456 | bytes 393216 | tf_op jit(solution)/shard_map/broadcast_in_dim | solution.py:519
  (2 shorter events, 0.0 us)
Async XLA Ops:
  0.0 17.9 %copy-start.1 = (bf16[1536,512]{1,0:T(8,128)(2,1)S(1)}, bf16[1536,512]{1,0:T(8,128)(2,1)}, u32[]{:S(2)}) copy-start(bf16[1536,512]{1,0:T(8,128)(2,1)} %query_weight_ref.1) | copy-start | bytes 4718596
  0.0 19.2 %copy-start.2 = (bf16[512,1536]{1,0:T(8,128)(2,1)S(1)}, bf16[512,1536]{1,0:T(8,128)(2,1)}, u32[]{:S(2)}) copy-start(bf16[512,1536]{1,0:T(8,128)(2,1)} %out_weight_ref.1) | copy-start | bytes 4718596
  0.0 19.2 %copy-start.4 = (f32[1536]{0:T(1024)S(1)}, f32[1536]{0:T(1024)}, u32[]{:S(2)}) copy-start(f32[1536]{0:T(1024)} %gain_ref.2) | copy-start | bytes 18436
  0.0 19.2 %copy-start.5 = (f32[1,4,4,32]{3,2,1,0:T(4,128)S(1)}, f32[1,4,4,32]{3,2,1,0:T(4,128)}, u32[]{:S(2)}) copy-start(f32[1,4,4,32]{3,2,1,0:T(4,128)} %bias_ref.1) | copy-start | bytes 6148
  1.8 9.5 %collective-permute-start.2 = (bf16[5,96,384]{2,1,0:T(8,128)(2,1)S(1)}, bf16[5,96,384]{2,1,0:T(8,128)(2,1)S(1)}, u32[]{:S(2)}, u32[]{:S(2)}) collective-permute-start(bf16[5,96,384]{2,1,0:T(8,128)(2,1)S(1)} %get-tuple-element.28), channel_id=1, source_target_pairs={{0,2},{2,0},{4,6},{6,4},{8,10},{10,8},{12,14},{14,12},{1,3},{3,1},... | collective-permute-start | bytes 1105928 | tf_op jit(solution)/shard_map/ppermute | solution.py:139
  3.0 3.0 %collective-permute-start = (bf16[1,48,256]{2,1,0:T(8,128)(2,1)S(1)}, bf16[1,48,256]{2,1,0:T(8,128)(2,1)S(1)}, u32[]{:S(2)}, u32[]{:S(2)}) collective-permute-start(bf16[1,48,256]{2,1,0:T(8,128)(2,1)S(1)} %bitcast.12), channel_id=1, source_target_pairs={{0,4},{2,6},{4,0},{6,2},{8,12},{10,14},{12,8},{14,10},{1,5},{3,7},... | collective-permute-start | bytes 73736 | tf_op jit(solution)/shard_map/ppermute | solution.py:139
  6.0 4.3 %collective-permute-start.1 = (bf16[2,48,256]{2,1,0:T(8,128)(2,1)S(1)}, bf16[2,48,256]{2,1,0:T(8,128)(2,1)S(1)}, u32[]{:S(2)}, u32[]{:S(2)}) collective-permute-start(bf16[2,48,256]{2,1,0:T(8,128)(2,1)S(1)} %shard_map.92.first_ref), channel_id=1, source_target_pairs={{0,8},{2,10},{4,12},{6,14},{8,0},{10,2},{12,4},{14,6},{1,9},{3,11}... | collective-permute-start | bytes 147464 | tf_op jit(solution)/shard_map/ppermute | solution.py:139
  10.3 3.5 %collective-permute-start.4 = (bf16[4,48,256]{2,1,0:T(8,128)(2,1)S(1)}, bf16[4,48,256]{2,1,0:T(8,128)(2,1)S(1)}, u32[]{:S(2)}, u32[]{:S(2)}) collective-permute-start(bf16[4,48,256]{2,1,0:T(8,128)(2,1)S(1)} %shard_map.93.near_ref), channel_id=1, source_target_pairs={{0,2},{2,0},{4,6},{6,4},{8,10},{10,8},{12,14},{14,12},{1,3},{3,1},... | collective-permute-start | bytes 294920 | tf_op jit(solution)/shard_map/ppermute | solution.py:139
  10.4 10.7 %collective-permute-start.6 = (bf16[5,96,384]{2,1,0:T(8,128)(2,1)S(1)}, bf16[5,96,384]{2,1,0:T(8,128)(2,1)S(1)}, u32[]{:S(2)}, u32[]{:S(2)}) collective-permute-start(bf16[5,96,384]{2,1,0:T(8,128)(2,1)S(1)} %get-tuple-element.28), channel_id=1, source_target_pairs={{0,4},{2,6},{4,0},{6,2},{8,12},{10,14},{12,8},{14,10},{1,5},{3,7},... | collective-permute-start | bytes 1105928 | tf_op jit(solution)/shard_map/ppermute | solution.py:139
  11.3 10.1 %collective-permute-start.8 = (bf16[5,96,384]{2,1,0:T(8,128)(2,1)S(1)}, bf16[5,96,384]{2,1,0:T(8,128)(2,1)S(1)}, u32[]{:S(2)}, u32[]{:S(2)}) collective-permute-start(bf16[5,96,384]{2,1,0:T(8,128)(2,1)S(1)} %collective-permute-done.2.w1), channel_id=1, source_target_pairs={{0,16},{16,0},{1,17},{17,1},{2,18},{18,2},{3,19},{19,3},{4,20},{20... | collective-permute-start | bytes 1105928 | tf_op jit(solution)/shard_map/ppermute | solution.py:139
  13.8 5.1 %collective-permute-start.5 = (bf16[4,48,256]{2,1,0:T(8,128)(2,1)S(1)}, bf16[4,48,256]{2,1,0:T(8,128)(2,1)S(1)}, u32[]{:S(2)}, u32[]{:S(2)}) collective-permute-start(bf16[4,48,256]{2,1,0:T(8,128)(2,1)S(1)} %collective-permute-done.4.side_ref), channel_id=1, source_target_pairs={{0,1},{1,0},{2,3},{3,2},{4,5},{5,4},{6,7},{7,6},{8,9},{9,8},{10,11... | collective-permute-start | bytes 294920 | tf_op jit(solution)/shard_map/ppermute | solution.py:139
  17.9 1.3 %collective-permute-start.3 = (bf16[4,48,256]{2,1,0:T(8,128)(2,1)S(1)}, bf16[4,48,256]{2,1,0:T(8,128)(2,1)S(1)}, u32[]{:S(2)}, u32[]{:S(2)}) collective-permute-start(bf16[4,48,256]{2,1,0:T(8,128)(2,1)S(1)} %shard_map.93.near_ref), channel_id=1, source_target_pairs={{0,1},{1,0},{2,3},{3,2},{4,5},{5,4},{6,7},{7,6},{8,9},{9,8},{10,11... | collective-permute-start | bytes 294920 | tf_op jit(solution)/shard_map/ppermute | solution.py:139
  18.3 6.3 %copy-start.3 = (bf16[1,128,1536]{2,1,0:T(8,128)(2,1)S(1)}, bf16[1,128,1536]{2,1,0:T(8,128)(2,1)}, u32[]{:S(2)}) copy-start(bf16[1,128,1536]{2,1,0:T(8,128)(2,1)} %param.9) | copy-start | bytes 1179652
  18.3 6.3 %copy-start.6 = (f32[1536]{0:T(1024)S(1)}, f32[1536]{0:T(1024)}, u32[]{:S(2)}) copy-start(f32[1536]{0:T(1024)} %gain_ref.3) | copy-start | bytes 18436
  18.3 6.3 %copy-start.7 = (f32[384]{0:T(512)S(1)}, f32[384]{0:T(512)}, u32[]{:S(2)}) copy-start(f32[384]{0:T(512)} %dec_bias_ref.1) | copy-start | bytes 4612
  18.3 17.4 %copy-start = (bf16[5,192,384]{2,1,0:T(8,128)(2,1)S(1)}, bf16[5,192,384]{2,1,0:T(8,128)(2,1)}, u32[]{:S(2)}) copy-start(bf16[5,192,384]{2,1,0:T(8,128)(2,1)} %param.16) | copy-start | bytes 2211844
  21.1 10.1 %collective-permute-start.11 = (bf16[5,96,384]{2,1,0:T(8,128)(2,1)S(1)}, bf16[5,96,384]{2,1,0:T(8,128)(2,1)S(1)}, u32[]{:S(2)}, u32[]{:S(2)}) collective-permute-start(bf16[5,96,384]{2,1,0:T(8,128)(2,1)S(1)} %collective-permute-done.6.w3), channel_id=1, source_target_pairs={{0,2},{2,0},{4,6},{6,4},{8,10},{10,8},{12,14},{14,12},{1,3},{3,1},... | collective-permute-start | bytes 1105928 | tf_op jit(solution)/shard_map/ppermute | solution.py:139
  21.4 10.3 %collective-permute-start.12 = (bf16[5,96,384]{2,1,0:T(8,128)(2,1)S(1)}, bf16[5,96,384]{2,1,0:T(8,128)(2,1)S(1)}, u32[]{:S(2)}, u32[]{:S(2)}) collective-permute-start(bf16[5,96,384]{2,1,0:T(8,128)(2,1)S(1)} %collective-permute-done.8.w2), channel_id=1, source_target_pairs={{0,4},{2,6},{4,0},{6,2},{8,12},{10,14},{12,8},{14,10},{1,5},{3,7},... | collective-permute-start | bytes 1105928 | tf_op jit(solution)/shard_map/ppermute | solution.py:139
  21.6 3.1 %collective-permute-start.7 = (bf16[80,1536]{1,0:T(8,128)(2,1)S(1)}, bf16[80,1536]{1,0:T(8,128)(2,1)S(1)}, u32[]{:S(2)}, u32[]{:S(2)}) collective-permute-start(bf16[80,1536]{1,0:T(8,128)(2,1)S(1)} %get-tuple-element.29.own_ref), channel_id=1, source_target_pairs={{0,1},{1,0},{2,3},{3,2},{4,5},{5,4},{6,7},{7,6},{8,9},{9,8},{10,11... | collective-permute-start | bytes 737288 | tf_op jit(solution)/shard_map/ppermute | solution.py:139
  23.4 11.4 %collective-permute-start.9 = (bf16[5,96,384]{2,1,0:T(8,128)(2,1)S(1)}, bf16[5,96,384]{2,1,0:T(8,128)(2,1)S(1)}, u32[]{:S(2)}, u32[]{:S(2)}) collective-permute-start(bf16[5,96,384]{2,1,0:T(8,128)(2,1)S(1)} %collective-permute-done.6.w3), channel_id=1, source_target_pairs={{0,16},{16,0},{1,17},{17,1},{2,18},{18,2},{3,19},{19,3},{4,20},{20... | collective-permute-start | bytes 1105928 | tf_op jit(solution)/shard_map/ppermute | solution.py:139
  25.4 5.8 %collective-permute-start.10 = (bf16[144,384]{1,0:T(8,128)(2,1)S(1)}, bf16[144,384]{1,0:T(8,128)(2,1)S(1)}, u32[]{:S(2)}, u32[]{:S(2)}) collective-permute-start(bf16[144,384]{1,0:T(8,128)(2,1)S(1)} %get-tuple-element.34), channel_id=1, source_target_pairs={{0,8},{2,10},{4,12},{6,14},{8,0},{10,2},{12,4},{14,6},{1,9},{3,11}... | collective-permute-start | bytes 331784 | tf_op jit(solution)/shard_map/ppermute | solution.py:139
  31.7 4.1 %collective-permute-start.13 = (bf16[144,384]{1,0:T(8,128)(2,1)S(1)}, bf16[144,384]{1,0:T(8,128)(2,1)S(1)}, u32[]{:S(2)}, u32[]{:S(2)}) collective-permute-start(bf16[144,384]{1,0:T(8,128)(2,1)S(1)} %collective-permute-done.10.first_ref), channel_id=1, source_target_pairs={{0,1},{1,0},{2,3},{3,2},{4,5},{5,4},{6,7},{7,6},{8,9},{9,8},{10,11... | collective-permute-start | bytes 331784 | tf_op jit(solution)/shard_map/ppermute | solution.py:139
  37.0 7.3 %collective-permute-start.14 = (bf16[128,384]{1,0:T(8,128)(2,1)S(1)}, bf16[128,384]{1,0:T(8,128)(2,1)S(1)}, u32[]{:S(2)}, u32[]{:S(2)}) collective-permute-start(bf16[128,384]{1,0:T(8,128)(2,1)S(1)} %shard_map.97), channel_id=1, source_target_pairs={{0,8},{2,10},{4,12},{6,14},{8,0},{10,2},{12,4},{14,6},{1,9},{3,11}... | collective-permute-start | bytes 294920 | tf_op jit(solution)/shard_map/ppermute | solution.py:139

commit v8 on v7

--- a/solution.py
+++ b/solution.py
@@ -433,11 +433,14 @@
     load_weight(w0, (w1, w2, w3, w4, w5, w6), weight)
     section = lax.axis_index("section")
     first, second = first_ref[...], second_ref[...]
-    near, far = 4 * section, 4 * (1 - section)
+    active = jnp.where(
+        section == 0,
+        jnp.concatenate([first, second], axis=1),
+        jnp.concatenate([second, first], axis=1),
+    )
     out_ref[...] = shifted_sum(
         [
-            jnp.dot(first, tap_weight(weight, t, near, 4), preferred_element_type=jnp.float32)
-            + jnp.dot(second, tap_weight(weight, t, far, 4), preferred_element_type=jnp.float32)
+            jnp.dot(active, tap_weight(weight, t, 0, 8), preferred_element_type=jnp.float32)
             for t in range(KW)
         ]
     ).astype(jnp.bfloat16)

time: 45.1 us -> 44.9 us (level)
  no operation moved by 1% of the time
where the time goes in v8:
time: 44.9 us; the launch traced here: 44.7 us
  waiting for transfers between devices  22.3 us (50%)
  starting transfers between devices  14.8 us (33%)
  Pallas kernels  6.39 us (14%)
  other arithmetic  0.66 us (1%)
    ppermute x15, waiting for transfers between devices, exchange(): return lax.ppermute(values_in, axis, [(i, i ^ mask) for i in range(count)])  22.3 us
    ppermute x15, starting transfers between devices, exchange(): return lax.ppermute(values_in, axis, [(i, i ^ mask) for i in range(count)])  14.8 us
    pallas_call x7, Pallas kernels, call(): pl.pallas_call(kernel, out_shape=[jax.ShapeDtypeStruct(shape, kind) for s...  6.39 us
  transfers between devices with their start and end apart: 15, of which 10 were waited for; matrix products, arithmetic and copies ran while one was open for 1% of the time, Pallas kernels for 8%

profile of v8, /device:TPU:25, one launch (start us, length us, event | category | flops | bytes accessed | tf_op | source)
XLA Modules:
  0.0 44.7 jit_solution(3798995876541811368)
XLA Ops:
  0.0 0.0 copy-start.1
  0.0 0.0 copy-start.2
  0.0 0.0 copy-start.4
  0.0 0.0 copy-start.5
  0.0 1.7 %shard_map.91 = (bf16[48,256]{1,0:T(8,128)(2,1)S(1)}, bf16[64,1536]{1,0:T(8,128)(2,1)S(1)}, bf16[5,96,384]{2,1,0:T(8,128)(2,1)S(1)}) custom-call(bf16[128,1536]{1,0:T(8,128)(2,1)} %bitcast.10, f32[1536]{0:T(1024)} %gain_ref.2, bf16[1536,256]{1,0:T(8,128)(2,1)} %weight_hbm.1, f32[1,4,4,32]{3,2,1,0:T(4,128)} %bias_ref.1, bf16[10,96,384]{2,1,0:T(8,128)(2,1)} %bitcast.7), custom_call_target="tpu_custom_call" | custom-call | tf_op jit(solution)/shard_map/pallas_call | solution.py:144
  1.8 1.3 %collective-permute-start.2 = (bf16[5,96,384]{2,1,0:T(8,128)(2,1)S(1)}, bf16[5,96,384]{2,1,0:T(8,128)(2,1)S(1)}, u32[]{:S(2)}, u32[]{:S(2)}) collective-permute-start(bf16[5,96,384]{2,1,0:T(8,128)(2,1)S(1)} %get-tuple-element.28), channel_id=1, source_target_pairs={{0,2},{2,0},{4,6},{6,4},{8,10},{10,8},{12,14},{14,12},{1,3},{3,1},... | collective-permute-start | bytes 1105928 | tf_op jit(solution)/shard_map/ppermute | solution.py:139
  3.0 0.2 collective-permute-start
  3.2 2.8 %collective-permute-done.second_ref = bf16[1,48,256]{2,1,0:T(8,128)(2,1)S(1)} collective-permute-done((bf16[1,48,256]{2,1,0:T(8,128)(2,1)S(1)}, bf16[1,48,256]{2,1,0:T(8,128)(2,1)S(1)}, u32[]{:S(2)}, u32[]{:S(2)}) %collective-permute-start) | collective-permute-done | bytes 24608 | tf_op jit(solution)/shard_map/ppermute | solution.py:139
  6.0 0.1 collective-permute-start.1
  6.1 4.2 %collective-permute-done.1.second_ref = bf16[2,48,256]{2,1,0:T(8,128)(2,1)S(1)} collective-permute-done((bf16[2,48,256]{2,1,0:T(8,128)(2,1)S(1)}, bf16[2,48,256]{2,1,0:T(8,128)(2,1)S(1)}, u32[]{:S(2)}, u32[]{:S(2)}) %collective-permute-start.1) | collective-permute-done | bytes 49184 | tf_op jit(solution)/shard_map/ppermute | solution.py:139
  10.3 0.1 collective-permute-start.4
  10.4 0.1 collective-permute-start.6
  10.4 0.8 %collective-permute-done.2.w1 = bf16[5,96,384]{2,1,0:T(8,128)(2,1)S(1)} collective-permute-done((bf16[5,96,384]{2,1,0:T(8,128)(2,1)S(1)}, bf16[5,96,384]{2,1,0:T(8,128)(2,1)S(1)}, u32[]{:S(2)}, u32[]{:S(2)}) %collective-permute-start.2) | collective-permute-done | bytes 368672 | tf_op jit(solution)/shard_map/ppermute | solution.py:139
  11.3 1.2 %collective-permute-start.8 = (bf16[5,96,384]{2,1,0:T(8,128)(2,1)S(1)}, bf16[5,96,384]{2,1,0:T(8,128)(2,1)S(1)}, u32[]{:S(2)}, u32[]{:S(2)}) collective-permute-start(bf16[5,96,384]{2,1,0:T(8,128)(2,1)S(1)} %collective-permute-done.2.w1), channel_id=1, source_target_pairs={{0,16},{16,0},{1,17},{17,1},{2,18},{18,2},{3,19},{19,3},{4,20},{20... | collective-permute-start | bytes 1105928 | tf_op jit(solution)/shard_map/ppermute | solution.py:139
  12.5 1.3 %collective-permute-done.4.side_ref = bf16[4,48,256]{2,1,0:T(8,128)(2,1)S(1)} collective-permute-done((bf16[4,48,256]{2,1,0:T(8,128)(2,1)S(1)}, bf16[4,48,256]{2,1,0:T(8,128)(2,1)S(1)}, u32[]{:S(2)}, u32[]{:S(2)}) %collective-permute-start.4) | collective-permute-done | bytes 98336 | tf_op jit(solution)/shard_map/ppermute | solution.py:139
  13.8 4.1 %collective-permute-start.5 = (bf16[4,48,256]{2,1,0:T(8,128)(2,1)S(1)}, bf16[4,48,256]{2,1,0:T(8,128)(2,1)S(1)}, u32[]{:S(2)}, u32[]{:S(2)}) collective-permute-start(bf16[4,48,256]{2,1,0:T(8,128)(2,1)S(1)} %collective-permute-done.4.side_ref), channel_id=1, source_target_pairs={{0,1},{1,0},{2,3},{3,2},{4,5},{5,4},{6,7},{7,6},{8,9},{9,8},{10,11... | collective-permute-start | bytes 294920 | tf_op jit(solution)/shard_map/ppermute | solution.py:139
  17.9 0.0 collective-permute-start.3
  17.9 0.0 copy-done.1
  17.9 0.4 convolution_convert_fusion.query_ref
  18.3 0.0 copy-start.3
  18.3 0.0 copy-start.6
  18.3 0.0 copy-start.7
  18.3 0.0 copy-start
  18.4 0.5 %collective-permute-done.5.side_other_ref = bf16[4,48,256]{2,1,0:T(8,128)(2,1)S(1)} collective-permute-done((bf16[4,48,256]{2,1,0:T(8,128)(2,1)S(1)}, bf16[4,48,256]{2,1,0:T(8,128)(2,1)S(1)}, u32[]{:S(2)}, u32[]{:S(2)}) %collective-permute-start.5) | collective-permute-done | bytes 98336 | tf_op jit(solution)/shard_map/ppermute | solution.py:139
  18.9 0.4 collective-permute-done.3.near_other_ref
  19.2 0.0 copy-done.2
  19.2 0.0 copy-done.4
  19.2 0.0 copy-done.5
  19.2 1.8 %shard_map.94 = (bf16[80,1536]{1,0:T(8,128)(2,1)S(1)}, f32[8,1536]{1,0:T(8,128)S(1)}) custom-call(bf16[64,512]{1,0:T(8,128)(2,1)S(1)} %convolution_convert_fusion.query_ref, bf16[4,48,256]{2,1,0:T(8,128)(2,1)S(1)} %shard_map.93.near_ref, bf16[4,48,256]{2,1,0:T(8,128)(2,1)S(1)} %collective-permute-done.3.near_other_ref, ...), custom_call_target="tpu_custom_call" | custom-call | tf_op jit(solution)/shard_map/pallas_call | solution.py:144
  21.1 0.0 collective-permute-done.6.w3
  21.1 0.3 collective-permute-start.11
  21.4 0.0 collective-permute-done.8.w2
  21.4 0.2 collective-permute-start.12
  21.6 1.8 %collective-permute-start.7 = (bf16[80,1536]{1,0:T(8,128)(2,1)S(1)}, bf16[80,1536]{1,0:T(8,128)(2,1)S(1)}, u32[]{:S(2)}, u32[]{:S(2)}) collective-permute-start(bf16[80,1536]{1,0:T(8,128)(2,1)S(1)} %get-tuple-element.29.own_ref), channel_id=1, source_target_pairs={{0,1},{1,0},{2,3},{3,2},{4,5},{5,4},{6,7},{7,6},{8,9},{9,8},{10,11... | collective-permute-start | bytes 737288 | tf_op jit(solution)/shard_map/ppermute | solution.py:139
  23.4 1.2 %collective-permute-start.9 = (bf16[5,96,384]{2,1,0:T(8,128)(2,1)S(1)}, bf16[5,96,384]{2,1,0:T(8,128)(2,1)S(1)}, u32[]{:S(2)}, u32[]{:S(2)}) collective-permute-start(bf16[5,96,384]{2,1,0:T(8,128)(2,1)S(1)} %collective-permute-done.6.w3), channel_id=1, source_target_pairs={{0,16},{16,0},{1,17},{17,1},{2,18},{18,2},{3,19},{19,3},{4,20},{20... | collective-permute-start | bytes 1105928 | tf_op jit(solution)/shard_map/ppermute | solution.py:139
  24.6 0.0 collective-permute-done.7.other_ref
  24.6 0.0 copy-done.3
  24.6 0.0 copy-done.6
  24.6 0.0 copy-done.7
  24.6 0.7 %shard_map.95 = (bf16[144,768]{1,0:T(8,128)(2,1)S(1)}, bf16[144,384]{1,0:T(8,128)(2,1)S(1)}, f32[128,384]{1,0:T(8,128)S(1)}) custom-call(bf16[128,1536]{1,0:T(8,128)(2,1)S(1)} %bitcast.11, f32[8,1536]{1,0:T(8,128)S(1)} %get-tuple-element.26.edge_ref, bf16[80,1536]{1,0:T(8,128)(2,1)S(1)} %get-tuple-element.29.own_ref, ...), custom_call_target="tpu_custom_call" | custom-call | tf_op jit(solution)/shard_map/pallas_call | solution.py:144
  25.4 0.1 collective-permute-start.10
  25.5 5.8 %collective-permute-done.10.first_ref = bf16[144,384]{1,0:T(8,128)(2,1)S(1)} collective-permute-done((bf16[144,384]{1,0:T(8,128)(2,1)S(1)}, bf16[144,384]{1,0:T(8,128)(2,1)S(1)}, u32[]{:S(2)}, u32[]{:S(2)}) %collective-permute-start.10) | collective-permute-done | bytes 110624 | tf_op jit(solution)/shard_map/ppermute | solution.py:139
  31.2 0.0 collective-permute-done.11.w5
  31.2 0.4 collective-permute-done.12.w6
  31.7 3.1 %collective-permute-start.13 = (bf16[144,384]{1,0:T(8,128)(2,1)S(1)}, bf16[144,384]{1,0:T(8,128)(2,1)S(1)}, u32[]{:S(2)}, u32[]{:S(2)}) collective-permute-start(bf16[144,384]{1,0:T(8,128)(2,1)S(1)} %collective-permute-done.10.first_ref), channel_id=1, source_target_pairs={{0,1},{1,0},{2,3},{3,2},{4,5},{5,4},{6,7},{7,6},{8,9},{9,8},{10,11... | collective-permute-start | bytes 331784 | tf_op jit(solution)/shard_map/ppermute | solution.py:139
  34.8 0.0 collective-permute-done.9.w4
  34.8 1.0 %collective-permute-done.13.second_ref = bf16[144,384]{1,0:T(8,128)(2,1)S(1)} collective-permute-done((bf16[144,384]{1,0:T(8,128)(2,1)S(1)}, bf16[144,384]{1,0:T(8,128)(2,1)S(1)}, u32[]{:S(2)}, u32[]{:S(2)}) %collective-permute-start.13) | collective-permute-done | bytes 110624 | tf_op jit(solution)/shard_map/ppermute | solution.py:139
  35.7 0.0 copy-done
  35.7 1.0 %shard_map.97 = bf16[128,384]{1,0:T(8,128)(2,1)S(1)} custom-call(bf16[144,384]{1,0:T(8,128)(2,1)S(1)} %collective-permute-done.10.first_ref, bf16[144,384]{1,0:T(8,128)(2,1)S(1)} %collective-permute-done.13.second_ref, bf16[10,96,384]{2,1,0:T(8,128)(2,1)S(1)} %bitcast.8, bf16[5,96,384]{2,1,0:T(8,128)(2,1)S(1)} %collective-permute-done.2.w1, ...), custom_call_target="tpu_custom_call" | custom-call | tf_op jit(solution)/shard_map/pallas_call | solution.py:144
  36.8 1.1 %collective-permute-start.14 = (bf16[128,384]{1,0:T(8,128)(2,1)S(1)}, bf16[128,384]{1,0:T(8,128)(2,1)S(1)}, u32[]{:S(2)}, u32[]{:S(2)}) collective-permute-start(bf16[128,384]{1,0:T(8,128)(2,1)S(1)} %shard_map.97), channel_id=1, source_target_pairs={{0,8},{2,10},{4,12},{6,14},{8,0},{10,2},{12,4},{14,6},{1,9},{3,11}... | collective-permute-start | bytes 294920 | tf_op jit(solution)/shard_map/ppermute | solution.py:139
  37.9 1.0 %shard_map.96 = f32[128,384]{1,0:T(8,128)S(1)} custom-call(bf16[144,768]{1,0:T(8,128)(2,1)S(1)} %get-tuple-element.30.active_ref, f32[128,384]{1,0:T(8,128)S(1)} %get-tuple-element.31.base_ref, bf16[10,96,384]{2,1,0:T(8,128)(2,1)S(1)} %bitcast.9, bf16[5,96,384]{2,1,0:T(8,128)(2,1)S(1)} %collective-permute-done.2.w1, ...), custom_call_target="tpu_custom_call" | custom-call | tf_op jit(solution)/shard_map/pallas_call | solution.py:144
  38.9 5.1 %collective-permute-done.14 = bf16[128,384]{1,0:T(8,128)(2,1)S(1)} collective-permute-done((bf16[128,384]{1,0:T(8,128)(2,1)S(1)}, bf16[128,384]{1,0:T(8,128)(2,1)S(1)}, u32[]{:S(2)}, u32[]{:S(2)}) %collective-permute-start.14) | collective-permute-done | bytes 98336 | tf_op jit(solution)/shard_map/ppermute | solution.py:139
  44.1 0.7 %fusion = bf16[1,128,384]{2,1,0:T(8,128)(2,1)} fusion(f32[128,384]{1,0:T(8,128)S(1)} %shard_map.96, bf16[128,384]{1,0:T(8,128)(2,1)S(1)} %collective-permute-done.14), kind=kLoop, calls=%fused_computation.2 | loop fusion | flops 147456 | bytes 393216 | tf_op jit(solution)/shard_map/broadcast_in_dim | solution.py:522
  (2 shorter events, 0.0 us)
Async XLA Ops:
  0.0 17.9 %copy-start.1 = (bf16[1536,512]{1,0:T(8,128)(2,1)S(1)}, bf16[1536,512]{1,0:T(8,128)(2,1)}, u32[]{:S(2)}) copy-start(bf16[1536,512]{1,0:T(8,128)(2,1)} %query_weight_ref.1) | copy-start | bytes 4718596
  0.0 19.2 %copy-start.2 = (bf16[512,1536]{1,0:T(8,128)(2,1)S(1)}, bf16[512,1536]{1,0:T(8,128)(2,1)}, u32[]{:S(2)}) copy-start(bf16[512,1536]{1,0:T(8,128)(2,1)} %out_weight_ref.1) | copy-start | bytes 4718596
  0.0 19.2 %copy-start.4 = (f32[1536]{0:T(1024)S(1)}, f32[1536]{0:T(1024)}, u32[]{:S(2)}) copy-start(f32[1536]{0:T(1024)} %gain_ref.2) | copy-start | bytes 18436
  0.0 19.2 %copy-start.5 = (f32[1,4,4,32]{3,2,1,0:T(4,128)S(1)}, f32[1,4,4,32]{3,2,1,0:T(4,128)}, u32[]{:S(2)}) copy-start(f32[1,4,4,32]{3,2,1,0:T(4,128)} %bias_ref.1) | copy-start | bytes 6148
  1.8 9.5 %collective-permute-start.2 = (bf16[5,96,384]{2,1,0:T(8,128)(2,1)S(1)}, bf16[5,96,384]{2,1,0:T(8,128)(2,1)S(1)}, u32[]{:S(2)}, u32[]{:S(2)}) collective-permute-start(bf16[5,96,384]{2,1,0:T(8,128)(2,1)S(1)} %get-tuple-element.28), channel_id=1, source_target_pairs={{0,2},{2,0},{4,6},{6,4},{8,10},{10,8},{12,14},{14,12},{1,3},{3,1},... | collective-permute-start | bytes 1105928 | tf_op jit(solution)/shard_map/ppermute | solution.py:139
  3.0 3.0 %collective-permute-start = (bf16[1,48,256]{2,1,0:T(8,128)(2,1)S(1)}, bf16[1,48,256]{2,1,0:T(8,128)(2,1)S(1)}, u32[]{:S(2)}, u32[]{:S(2)}) collective-permute-start(bf16[1,48,256]{2,1,0:T(8,128)(2,1)S(1)} %bitcast.12), channel_id=1, source_target_pairs={{0,4},{2,6},{4,0},{6,2},{8,12},{10,14},{12,8},{14,10},{1,5},{3,7},... | collective-permute-start | bytes 73736 | tf_op jit(solution)/shard_map/ppermute | solution.py:139
  6.0 4.3 %collective-permute-start.1 = (bf16[2,48,256]{2,1,0:T(8,128)(2,1)S(1)}, bf16[2,48,256]{2,1,0:T(8,128)(2,1)S(1)}, u32[]{:S(2)}, u32[]{:S(2)}) collective-permute-start(bf16[2,48,256]{2,1,0:T(8,128)(2,1)S(1)} %shard_map.92.first_ref), channel_id=1, source_target_pairs={{0,8},{2,10},{4,12},{6,14},{8,0},{10,2},{12,4},{14,6},{1,9},{3,11}... | collective-permute-start | bytes 147464 | tf_op jit(solution)/shard_map/ppermute | solution.py:139
  10.3 3.5 %collective-permute-start.4 = (bf16[4,48,256]{2,1,0:T(8,128)(2,1)S(1)}, bf16[4,48,256]{2,1,0:T(8,128)(2,1)S(1)}, u32[]{:S(2)}, u32[]{:S(2)}) collective-permute-start(bf16[4,48,256]{2,1,0:T(8,128)(2,1)S(1)} %shard_map.93.near_ref), channel_id=1, source_target_pairs={{0,2},{2,0},{4,6},{6,4},{8,10},{10,8},{12,14},{14,12},{1,3},{3,1},... | collective-permute-start | bytes 294920 | tf_op jit(solution)/shard_map/ppermute | solution.py:139
  10.4 10.7 %collective-permute-start.6 = (bf16[5,96,384]{2,1,0:T(8,128)(2,1)S(1)}, bf16[5,96,384]{2,1,0:T(8,128)(2,1)S(1)}, u32[]{:S(2)}, u32[]{:S(2)}) collective-permute-start(bf16[5,96,384]{2,1,0:T(8,128)(2,1)S(1)} %get-tuple-element.28), channel_id=1, source_target_pairs={{0,4},{2,6},{4,0},{6,2},{8,12},{10,14},{12,8},{14,10},{1,5},{3,7},... | collective-permute-start | bytes 1105928 | tf_op jit(solution)/shard_map/ppermute | solution.py:139
  11.3 10.1 %collective-permute-start.8 = (bf16[5,96,384]{2,1,0:T(8,128)(2,1)S(1)}, bf16[5,96,384]{2,1,0:T(8,128)(2,1)S(1)}, u32[]{:S(2)}, u32[]{:S(2)}) collective-permute-start(bf16[5,96,384]{2,1,0:T(8,128)(2,1)S(1)} %collective-permute-done.2.w1), channel_id=1, source_target_pairs={{0,16},{16,0},{1,17},{17,1},{2,18},{18,2},{3,19},{19,3},{4,20},{20... | collective-permute-start | bytes 1105928 | tf_op jit(solution)/shard_map/ppermute | solution.py:139
  13.8 5.1 %collective-permute-start.5 = (bf16[4,48,256]{2,1,0:T(8,128)(2,1)S(1)}, bf16[4,48,256]{2,1,0:T(8,128)(2,1)S(1)}, u32[]{:S(2)}, u32[]{:S(2)}) collective-permute-start(bf16[4,48,256]{2,1,0:T(8,128)(2,1)S(1)} %collective-permute-done.4.side_ref), channel_id=1, source_target_pairs={{0,1},{1,0},{2,3},{3,2},{4,5},{5,4},{6,7},{7,6},{8,9},{9,8},{10,11... | collective-permute-start | bytes 294920 | tf_op jit(solution)/shard_map/ppermute | solution.py:139
  17.9 1.3 %collective-permute-start.3 = (bf16[4,48,256]{2,1,0:T(8,128)(2,1)S(1)}, bf16[4,48,256]{2,1,0:T(8,128)(2,1)S(1)}, u32[]{:S(2)}, u32[]{:S(2)}) collective-permute-start(bf16[4,48,256]{2,1,0:T(8,128)(2,1)S(1)} %shard_map.93.near_ref), channel_id=1, source_target_pairs={{0,1},{1,0},{2,3},{3,2},{4,5},{5,4},{6,7},{7,6},{8,9},{9,8},{10,11... | collective-permute-start | bytes 294920 | tf_op jit(solution)/shard_map/ppermute | solution.py:139
  18.3 6.3 %copy-start.3 = (bf16[1,128,1536]{2,1,0:T(8,128)(2,1)S(1)}, bf16[1,128,1536]{2,1,0:T(8,128)(2,1)}, u32[]{:S(2)}) copy-start(bf16[1,128,1536]{2,1,0:T(8,128)(2,1)} %param.9) | copy-start | bytes 1179652
  18.3 6.3 %copy-start.6 = (f32[1536]{0:T(1024)S(1)}, f32[1536]{0:T(1024)}, u32[]{:S(2)}) copy-start(f32[1536]{0:T(1024)} %gain_ref.3) | copy-start | bytes 18436
  18.3 6.3 %copy-start.7 = (f32[384]{0:T(512)S(1)}, f32[384]{0:T(512)}, u32[]{:S(2)}) copy-start(f32[384]{0:T(512)} %dec_bias_ref.1) | copy-start | bytes 4612
  18.3 17.4 %copy-start = (bf16[5,192,384]{2,1,0:T(8,128)(2,1)S(1)}, bf16[5,192,384]{2,1,0:T(8,128)(2,1)}, u32[]{:S(2)}) copy-start(bf16[5,192,384]{2,1,0:T(8,128)(2,1)} %param.16) | copy-start | bytes 2211844
  21.1 10.1 %collective-permute-start.11 = (bf16[5,96,384]{2,1,0:T(8,128)(2,1)S(1)}, bf16[5,96,384]{2,1,0:T(8,128)(2,1)S(1)}, u32[]{:S(2)}, u32[]{:S(2)}) collective-permute-start(bf16[5,96,384]{2,1,0:T(8,128)(2,1)S(1)} %collective-permute-done.6.w3), channel_id=1, source_target_pairs={{0,2},{2,0},{4,6},{6,4},{8,10},{10,8},{12,14},{14,12},{1,3},{3,1},... | collective-permute-start | bytes 1105928 | tf_op jit(solution)/shard_map/ppermute | solution.py:139
  21.4 10.3 %collective-permute-start.12 = (bf16[5,96,384]{2,1,0:T(8,128)(2,1)S(1)}, bf16[5,96,384]{2,1,0:T(8,128)(2,1)S(1)}, u32[]{:S(2)}, u32[]{:S(2)}) collective-permute-start(bf16[5,96,384]{2,1,0:T(8,128)(2,1)S(1)} %collective-permute-done.8.w2), channel_id=1, source_target_pairs={{0,4},{2,6},{4,0},{6,2},{8,12},{10,14},{12,8},{14,10},{1,5},{3,7},... | collective-permute-start | bytes 1105928 | tf_op jit(solution)/shard_map/ppermute | solution.py:139
  21.6 3.1 %collective-permute-start.7 = (bf16[80,1536]{1,0:T(8,128)(2,1)S(1)}, bf16[80,1536]{1,0:T(8,128)(2,1)S(1)}, u32[]{:S(2)}, u32[]{:S(2)}) collective-permute-start(bf16[80,1536]{1,0:T(8,128)(2,1)S(1)} %get-tuple-element.29.own_ref), channel_id=1, source_target_pairs={{0,1},{1,0},{2,3},{3,2},{4,5},{5,4},{6,7},{7,6},{8,9},{9,8},{10,11... | collective-permute-start | bytes 737288 | tf_op jit(solution)/shard_map/ppermute | solution.py:139
  23.4 11.4 %collective-permute-start.9 = (bf16[5,96,384]{2,1,0:T(8,128)(2,1)S(1)}, bf16[5,96,384]{2,1,0:T(8,128)(2,1)S(1)}, u32[]{:S(2)}, u32[]{:S(2)}) collective-permute-start(bf16[5,96,384]{2,1,0:T(8,128)(2,1)S(1)} %collective-permute-done.6.w3), channel_id=1, source_target_pairs={{0,16},{16,0},{1,17},{17,1},{2,18},{18,2},{3,19},{19,3},{4,20},{20... | collective-permute-start | bytes 1105928 | tf_op jit(solution)/shard_map/ppermute | solution.py:139
  25.4 5.8 %collective-permute-start.10 = (bf16[144,384]{1,0:T(8,128)(2,1)S(1)}, bf16[144,384]{1,0:T(8,128)(2,1)S(1)}, u32[]{:S(2)}, u32[]{:S(2)}) collective-permute-start(bf16[144,384]{1,0:T(8,128)(2,1)S(1)} %get-tuple-element.34), channel_id=1, source_target_pairs={{0,8},{2,10},{4,12},{6,14},{8,0},{10,2},{12,4},{14,6},{1,9},{3,11}... | collective-permute-start | bytes 331784 | tf_op jit(solution)/shard_map/ppermute | solution.py:139
  31.7 4.1 %collective-permute-start.13 = (bf16[144,384]{1,0:T(8,128)(2,1)S(1)}, bf16[144,384]{1,0:T(8,128)(2,1)S(1)}, u32[]{:S(2)}, u32[]{:S(2)}) collective-permute-start(bf16[144,384]{1,0:T(8,128)(2,1)S(1)} %collective-permute-done.10.first_ref), channel_id=1, source_target_pairs={{0,1},{1,0},{2,3},{3,2},{4,5},{5,4},{6,7},{7,6},{8,9},{9,8},{10,11... | collective-permute-start | bytes 331784 | tf_op jit(solution)/shard_map/ppermute | solution.py:139
  36.8 7.3 %collective-permute-start.14 = (bf16[128,384]{1,0:T(8,128)(2,1)S(1)}, bf16[128,384]{1,0:T(8,128)(2,1)S(1)}, u32[]{:S(2)}, u32[]{:S(2)}) collective-permute-start(bf16[128,384]{1,0:T(8,128)(2,1)S(1)} %shard_map.97), channel_id=1, source_target_pairs={{0,8},{2,10},{4,12},{6,14},{8,0},{10,2},{12,4},{14,6},{1,9},{3,11}... | collective-permute-start | bytes 294920 | tf_op jit(solution)/shard_map/ppermute | solution.py:139

commit v9 on v8

--- a/solution.py
+++ b/solution.py
@@ -372,8 +372,8 @@
     odd = rounded(attended + odd)
     put_rows(wide, 0, even)
     put_rows(wide, 1, odd)
-    put_rows(active, 8, gelu(normalize(even, gain)))
-    put_rows(active, 9, gelu(normalize(odd, gain)))
+    put_rows(active, 2, gelu(normalize(even, gain)))
+    put_rows(active, 3, gelu(normalize(odd, gain)))
     edges = edge_ref[0:4, :]
     low = rounded(jnp.maximum(edges[0:1], edges[1:2]) + projected[64:65])
     high = rounded(jnp.maximum(edges[2:3], edges[3:4]) + projected[65:66])
@@ -381,11 +381,11 @@
     halo = gelu(normalize(joined, gain))
     above = jnp.where(me > 0, halo[0:2], 0.0)
     below = jnp.where(me < lax.axis_size("seq") - 1, halo[2:4], 0.0)
-    zeros = jnp.zeros((6, 128), jnp.float32)
+    zeros = jnp.zeros((4, 128), jnp.float32)
     for k in range(12):
         columns = slice(128 * k, 128 * k + 128)
-        active[k, 0:8, :] = jnp.concatenate([zeros, above[:, columns]], axis=0)
-        active[k, 136:144, :] = jnp.concatenate([below[:, columns], zeros], axis=0)
+        active[k, 0:2, :] = above[:, columns]
+        active[k, 130:136, :] = jnp.concatenate([below[:, columns], zeros], axis=0)
     for k in range(6):
         keep_ref[:, 128 * k : 128 * k + 128] = active[upper * 6 + k].astype(jnp.bfloat16)
     for k in range(3):
@@ -412,9 +412,9 @@
 
 
 def shifted_sum(products):
-    total = products[0][6:134]
+    total = products[0][0:128]
     for tap in range(1, KW):
-        total = total + products[tap][6 + tap : 134 + tap]
+        total = total + products[tap][tap : 128 + tap]
     return total
 
 
@@ -505,9 +505,9 @@
     far_rest = exchange(behind(side_rest, terms), "seq", 2)
     keep, send, base = call(
         activate_kernel,
-        [((rows + 16, channels // 2), bf16), ((rows + 16, channels // 4), bf16), ((rows, width), f32)],
+        [((rows + 8, channels // 2), bf16), ((rows + 8, channels // 4), bf16), ((rows, width), f32)],
         [skip, edges, terms, other, dec_gain, dec_bias],
-        [pltpu.VMEM((channels // 128, rows + extra, 128), f32) for extra in (0, 16)],
+        [pltpu.VMEM((channels // 128, rows + extra, 128), f32) for extra in (0, 8)],
     )
     first = exchange(send, "seq", 4)
     first, far, far_rest = lax.optimization_barrier((first, far, far_rest))

time: 44.9 us -> 44.6 us (level)
  the two profiles are of different devices: /device:TPU:25 before, /device:TPU:0 now
where the time goes in v9:
time: 44.6 us; the launch traced here: 43.8 us
  starting transfers between devices  22 us (49%)
  waiting for transfers between devices  14.2 us (32%)
  Pallas kernels  6.36 us (14%)
  other arithmetic  0.67 us (2%)
    ppermute x15, starting transfers between devices, exchange(): return lax.ppermute(values_in, axis, [(i, i ^ mask) for i in range(count)])  22 us
    ppermute x15, waiting for transfers between devices, exchange(): return lax.ppermute(values_in, axis, [(i, i ^ mask) for i in range(count)])  14.2 us
    pallas_call x7, Pallas kernels, call(): pl.pallas_call(kernel, out_shape=[jax.ShapeDtypeStruct(shape, kind) for s...  6.36 us
  transfers between devices with their start and end apart: 15, of which 11 were waited for; matrix products, arithmetic and copies ran while one was open for 1% of the time, Pallas kernels for 8%

profile of v9, /device:TPU:0, one launch (start us, length us, event | category | flops | bytes accessed | tf_op | source)
XLA Modules:
  0.0 43.8 jit_solution(17880950842579828307)
XLA Ops:
  0.0 0.0 copy-start.1
  0.0 0.0 copy-start.2
  0.0 0.0 copy-start.4
  0.0 0.0 copy-start.5
  0.0 1.7 %shard_map.91 = (bf16[48,256]{1,0:T(8,128)(2,1)S(1)}, bf16[64,1536]{1,0:T(8,128)(2,1)S(1)}, bf16[5,96,384]{2,1,0:T(8,128)(2,1)S(1)}) custom-call(bf16[128,1536]{1,0:T(8,128)(2,1)} %bitcast.10, f32[1536]{0:T(1024)} %gain_ref.2, bf16[1536,256]{1,0:T(8,128)(2,1)} %weight_hbm.1, f32[1,4,4,32]{3,2,1,0:T(4,128)} %bias_ref.1, bf16[10,96,384]{2,1,0:T(8,128)(2,1)} %bitcast.7), custom_call_target="tpu_custom_call" | custom-call | tf_op jit(solution)/shard_map/pallas_call | solution.py:144
  1.7 3.0 %collective-permute-start.2 = (bf16[5,96,384]{2,1,0:T(8,128)(2,1)S(1)}, bf16[5,96,384]{2,1,0:T(8,128)(2,1)S(1)}, u32[]{:S(2)}, u32[]{:S(2)}) collective-permute-start(bf16[5,96,384]{2,1,0:T(8,128)(2,1)S(1)} %get-tuple-element.28), channel_id=1, source_target_pairs={{0,2},{2,0},{4,6},{6,4},{8,10},{10,8},{12,14},{14,12},{1,3},{3,1},... | collective-permute-start | bytes 1105928 | tf_op jit(solution)/shard_map/ppermute | solution.py:139
  4.8 1.6 %collective-permute-start = (bf16[1,48,256]{2,1,0:T(8,128)(2,1)S(1)}, bf16[1,48,256]{2,1,0:T(8,128)(2,1)S(1)}, u32[]{:S(2)}, u32[]{:S(2)}) collective-permute-start(bf16[1,48,256]{2,1,0:T(8,128)(2,1)S(1)} %bitcast.12), channel_id=1, source_target_pairs={{0,4},{2,6},{4,0},{6,2},{8,12},{10,14},{12,8},{14,10},{1,5},{3,7},... | collective-permute-start | bytes 73736 | tf_op jit(solution)/shard_map/ppermute | solution.py:139
  6.3 2.3 %collective-permute-done.second_ref = bf16[1,48,256]{2,1,0:T(8,128)(2,1)S(1)} collective-permute-done((bf16[1,48,256]{2,1,0:T(8,128)(2,1)S(1)}, bf16[1,48,256]{2,1,0:T(8,128)(2,1)S(1)}, u32[]{:S(2)}, u32[]{:S(2)}) %collective-permute-start) | collective-permute-done | bytes 24608 | tf_op jit(solution)/shard_map/ppermute | solution.py:139
  8.6 2.6 %collective-permute-start.1 = (bf16[2,48,256]{2,1,0:T(8,128)(2,1)S(1)}, bf16[2,48,256]{2,1,0:T(8,128)(2,1)S(1)}, u32[]{:S(2)}, u32[]{:S(2)}) collective-permute-start(bf16[2,48,256]{2,1,0:T(8,128)(2,1)S(1)} %shard_map.92.first_ref), channel_id=1, source_target_pairs={{0,8},{2,10},{4,12},{6,14},{8,0},{10,2},{12,4},{14,6},{1,9},{3,11}... | collective-permute-start | bytes 147464 | tf_op jit(solution)/shard_map/ppermute | solution.py:139
  11.2 2.4 %collective-permute-done.1.second_ref = bf16[2,48,256]{2,1,0:T(8,128)(2,1)S(1)} collective-permute-done((bf16[2,48,256]{2,1,0:T(8,128)(2,1)S(1)}, bf16[2,48,256]{2,1,0:T(8,128)(2,1)S(1)}, u32[]{:S(2)}, u32[]{:S(2)}) %collective-permute-start.1) | collective-permute-done | bytes 49184 | tf_op jit(solution)/shard_map/ppermute | solution.py:139
  13.6 0.3 collective-permute-start.4
  13.9 1.9 %collective-permute-start.6 = (bf16[5,96,384]{2,1,0:T(8,128)(2,1)S(1)}, bf16[5,96,384]{2,1,0:T(8,128)(2,1)S(1)}, u32[]{:S(2)}, u32[]{:S(2)}) collective-permute-start(bf16[5,96,384]{2,1,0:T(8,128)(2,1)S(1)} %get-tuple-element.28), channel_id=1, source_target_pairs={{0,4},{2,6},{4,0},{6,2},{8,12},{10,14},{12,8},{14,10},{1,5},{3,7},... | collective-permute-start | bytes 1105928 | tf_op jit(solution)/shard_map/ppermute | solution.py:139
  15.8 0.0 collective-permute-done.2.w1
  15.8 1.5 %collective-permute-start.8 = (bf16[5,96,384]{2,1,0:T(8,128)(2,1)S(1)}, bf16[5,96,384]{2,1,0:T(8,128)(2,1)S(1)}, u32[]{:S(2)}, u32[]{:S(2)}) collective-permute-start(bf16[5,96,384]{2,1,0:T(8,128)(2,1)S(1)} %collective-permute-done.2.w1), channel_id=1, source_target_pairs={{0,16},{16,0},{1,17},{17,1},{2,18},{18,2},{3,19},{19,3},{4,20},{20... | collective-permute-start | bytes 1105928 | tf_op jit(solution)/shard_map/ppermute | solution.py:139
  17.3 1.0 %collective-permute-done.4.side_ref = bf16[4,48,256]{2,1,0:T(8,128)(2,1)S(1)} collective-permute-done((bf16[4,48,256]{2,1,0:T(8,128)(2,1)S(1)}, bf16[4,48,256]{2,1,0:T(8,128)(2,1)S(1)}, u32[]{:S(2)}, u32[]{:S(2)}) %collective-permute-start.4) | collective-permute-done | bytes 98336 | tf_op jit(solution)/shard_map/ppermute | solution.py:139
  18.3 0.0 collective-permute-start.5
  18.3 0.5 %collective-permute-start.3 = (bf16[4,48,256]{2,1,0:T(8,128)(2,1)S(1)}, bf16[4,48,256]{2,1,0:T(8,128)(2,1)S(1)}, u32[]{:S(2)}, u32[]{:S(2)}) collective-permute-start(bf16[4,48,256]{2,1,0:T(8,128)(2,1)S(1)} %shard_map.93.near_ref), channel_id=1, source_target_pairs={{0,1},{1,0},{2,3},{3,2},{4,5},{5,4},{6,7},{7,6},{8,9},{9,8},{10,11... | collective-permute-start | bytes 294920 | tf_op jit(solution)/shard_map/ppermute | solution.py:139
  18.8 0.0 copy-done.1
  18.8 0.4 convolution_convert_fusion.query_ref
  19.2 0.0 copy-start.3
  19.2 0.0 copy-start.6
  19.2 0.0 copy-start.7
  19.2 0.0 copy-start
  19.2 0.4 collective-permute-done.5.side_other_ref
  19.6 0.2 collective-permute-done.3.near_other_ref
  19.7 0.0 copy-done.2
  19.7 0.0 copy-done.4
  19.7 0.0 copy-done.5
  19.7 1.8 %shard_map.94 = (bf16[80,1536]{1,0:T(8,128)(2,1)S(1)}, f32[8,1536]{1,0:T(8,128)S(1)}) custom-call(bf16[64,512]{1,0:T(8,128)(2,1)S(1)} %convolution_convert_fusion.query_ref, bf16[4,48,256]{2,1,0:T(8,128)(2,1)S(1)} %shard_map.93.near_ref, bf16[4,48,256]{2,1,0:T(8,128)(2,1)S(1)} %collective-permute-done.3.near_other_ref, ...), custom_call_target="tpu_custom_call" | custom-call | tf_op jit(solution)/shard_map/pallas_call | solution.py:144
  21.6 0.2 collective-permute-done.6.w3
  21.8 1.7 %collective-permute-start.11 = (bf16[5,96,384]{2,1,0:T(8,128)(2,1)S(1)}, bf16[5,96,384]{2,1,0:T(8,128)(2,1)S(1)}, u32[]{:S(2)}, u32[]{:S(2)}) collective-permute-start(bf16[5,96,384]{2,1,0:T(8,128)(2,1)S(1)} %collective-permute-done.6.w3), channel_id=1, source_target_pairs={{0,2},{2,0},{4,6},{6,4},{8,10},{10,8},{12,14},{14,12},{1,3},{3,1},... | collective-permute-start | bytes 1105928 | tf_op jit(solution)/shard_map/ppermute | solution.py:139
  23.4 0.0 collective-permute-done.8.w2
  23.5 1.6 %collective-permute-start.12 = (bf16[5,96,384]{2,1,0:T(8,128)(2,1)S(1)}, bf16[5,96,384]{2,1,0:T(8,128)(2,1)S(1)}, u32[]{:S(2)}, u32[]{:S(2)}) collective-permute-start(bf16[5,96,384]{2,1,0:T(8,128)(2,1)S(1)} %collective-permute-done.8.w2), channel_id=1, source_target_pairs={{0,4},{2,6},{4,0},{6,2},{8,12},{10,14},{12,8},{14,10},{1,5},{3,7},... | collective-permute-start | bytes 1105928 | tf_op jit(solution)/shard_map/ppermute | solution.py:139
  25.0 0.0 collective-permute-start.7
  25.0 1.5 %collective-permute-start.9 = (bf16[5,96,384]{2,1,0:T(8,128)(2,1)S(1)}, bf16[5,96,384]{2,1,0:T(8,128)(2,1)S(1)}, u32[]{:S(2)}, u32[]{:S(2)}) collective-permute-start(bf16[5,96,384]{2,1,0:T(8,128)(2,1)S(1)} %collective-permute-done.6.w3), channel_id=1, source_target_pairs={{0,16},{16,0},{1,17},{17,1},{2,18},{18,2},{3,19},{19,3},{4,20},{20... | collective-permute-start | bytes 1105928 | tf_op jit(solution)/shard_map/ppermute | solution.py:139
  26.6 0.0 collective-permute-done.7.other_ref
  26.6 0.0 copy-done.3
  26.6 0.0 copy-done.6
  26.6 0.0 copy-done.7
  26.6 0.7 %shard_map.95 = (bf16[136,768]{1,0:T(8,128)(2,1)S(1)}, bf16[136,384]{1,0:T(8,128)(2,1)S(1)}, f32[128,384]{1,0:T(8,128)S(1)}) custom-call(bf16[128,1536]{1,0:T(8,128)(2,1)S(1)} %bitcast.11, f32[8,1536]{1,0:T(8,128)S(1)} %get-tuple-element.26.edge_ref, bf16[80,1536]{1,0:T(8,128)(2,1)S(1)} %get-tuple-element.29.own_ref, ...), custom_call_target="tpu_custom_call" | custom-call | tf_op jit(solution)/shard_map/pallas_call | solution.py:144
  27.3 3.1 %collective-permute-start.10 = (bf16[136,384]{1,0:T(8,128)(2,1)S(1)}, bf16[136,384]{1,0:T(8,128)(2,1)S(1)}, u32[]{:S(2)}, u32[]{:S(2)}) collective-permute-start(bf16[136,384]{1,0:T(8,128)(2,1)S(1)} %get-tuple-element.34), channel_id=1, source_target_pairs={{0,8},{2,10},{4,12},{6,14},{8,0},{10,2},{12,4},{14,6},{1,9},{3,11}... | collective-permute-start | bytes 313352 | tf_op jit(solution)/shard_map/ppermute | solution.py:139
  30.4 4.0 %collective-permute-done.10.first_ref = bf16[136,384]{1,0:T(8,128)(2,1)S(1)} collective-permute-done((bf16[136,384]{1,0:T(8,128)(2,1)S(1)}, bf16[136,384]{1,0:T(8,128)(2,1)S(1)}, u32[]{:S(2)}, u32[]{:S(2)}) %collective-permute-start.10) | collective-permute-done | bytes 104480 | tf_op jit(solution)/shard_map/ppermute | solution.py:139
  34.4 0.0 collective-permute-done.11.w5
  34.4 0.6 %collective-permute-done.12.w6 = bf16[5,96,384]{2,1,0:T(8,128)(2,1)S(1)} collective-permute-done((bf16[5,96,384]{2,1,0:T(8,128)(2,1)S(1)}, bf16[5,96,384]{2,1,0:T(8,128)(2,1)S(1)}, u32[]{:S(2)}, u32[]{:S(2)}) %collective-permute-start.12) | collective-permute-done | bytes 368672 | tf_op jit(solution)/shard_map/ppermute | solution.py:139
  35.0 0.0 collective-permute-start.13
  35.0 1.0 %collective-permute-done.9.w4 = bf16[5,96,384]{2,1,0:T(8,128)(2,1)S(1)} collective-permute-done((bf16[5,96,384]{2,1,0:T(8,128)(2,1)S(1)}, bf16[5,96,384]{2,1,0:T(8,128)(2,1)S(1)}, u32[]{:S(2)}, u32[]{:S(2)}) %collective-permute-start.9) | collective-permute-done | bytes 368672 | tf_op jit(solution)/shard_map/ppermute | solution.py:139
  36.0 0.3 collective-permute-done.13.second_ref
  36.3 0.0 copy-done
  36.3 1.0 %shard_map.97 = bf16[128,384]{1,0:T(8,128)(2,1)S(1)} custom-call(bf16[136,384]{1,0:T(8,128)(2,1)S(1)} %collective-permute-done.10.first_ref, bf16[136,384]{1,0:T(8,128)(2,1)S(1)} %collective-permute-done.13.second_ref, bf16[10,96,384]{2,1,0:T(8,128)(2,1)S(1)} %bitcast.8, bf16[5,96,384]{2,1,0:T(8,128)(2,1)S(1)} %collective-permute-done.2.w1, ...), custom_call_target="tpu_custom_call" | custom-call | tf_op jit(solution)/shard_map/pallas_call | solution.py:144
  37.3 2.8 %collective-permute-start.14 = (bf16[128,384]{1,0:T(8,128)(2,1)S(1)}, bf16[128,384]{1,0:T(8,128)(2,1)S(1)}, u32[]{:S(2)}, u32[]{:S(2)}) collective-permute-start(bf16[128,384]{1,0:T(8,128)(2,1)S(1)} %shard_map.97), channel_id=1, source_target_pairs={{0,8},{2,10},{4,12},{6,14},{8,0},{10,2},{12,4},{14,6},{1,9},{3,11}... | collective-permute-start | bytes 294920 | tf_op jit(solution)/shard_map/ppermute | solution.py:139
  40.1 1.0 %shard_map.96 = f32[128,384]{1,0:T(8,128)S(1)} custom-call(bf16[136,768]{1,0:T(8,128)(2,1)S(1)} %get-tuple-element.30.active_ref, f32[128,384]{1,0:T(8,128)S(1)} %get-tuple-element.31.base_ref, bf16[10,96,384]{2,1,0:T(8,128)(2,1)S(1)} %bitcast.9, bf16[5,96,384]{2,1,0:T(8,128)(2,1)S(1)} %collective-permute-done.2.w1, ...), custom_call_target="tpu_custom_call" | custom-call | tf_op jit(solution)/shard_map/pallas_call | solution.py:144
  41.2 2.0 %collective-permute-done.14 = bf16[128,384]{1,0:T(8,128)(2,1)S(1)} collective-permute-done((bf16[128,384]{1,0:T(8,128)(2,1)S(1)}, bf16[128,384]{1,0:T(8,128)(2,1)S(1)}, u32[]{:S(2)}, u32[]{:S(2)}) %collective-permute-start.14) | collective-permute-done | bytes 98336 | tf_op jit(solution)/shard_map/ppermute | solution.py:139
  43.1 0.7 %fusion = bf16[1,128,384]{2,1,0:T(8,128)(2,1)} fusion(f32[128,384]{1,0:T(8,128)S(1)} %shard_map.96, bf16[128,384]{1,0:T(8,128)(2,1)S(1)} %collective-permute-done.14), kind=kLoop, calls=%fused_computation.2 | loop fusion | flops 147456 | bytes 393216 | tf_op jit(solution)/shard_map/broadcast_in_dim | solution.py:522
  (2 shorter events, 0.0 us)
Async XLA Ops:
  0.0 18.8 %copy-start.1 = (bf16[1536,512]{1,0:T(8,128)(2,1)S(1)}, bf16[1536,512]{1,0:T(8,128)(2,1)}, u32[]{:S(2)}) copy-start(bf16[1536,512]{1,0:T(8,128)(2,1)} %query_weight_ref.1) | copy-start | bytes 4718596
  0.0 19.7 %copy-start.2 = (bf16[512,1536]{1,0:T(8,128)(2,1)S(1)}, bf16[512,1536]{1,0:T(8,128)(2,1)}, u32[]{:S(2)}) copy-start(bf16[512,1536]{1,0:T(8,128)(2,1)} %out_weight_ref.1) | copy-start | bytes 4718596
  0.0 19.7 %copy-start.4 = (f32[1536]{0:T(1024)S(1)}, f32[1536]{0:T(1024)}, u32[]{:S(2)}) copy-start(f32[1536]{0:T(1024)} %gain_ref.2) | copy-start | bytes 18436
  0.0 19.7 %copy-start.5 = (f32[1,4,4,32]{3,2,1,0:T(4,128)S(1)}, f32[1,4,4,32]{3,2,1,0:T(4,128)}, u32[]{:S(2)}) copy-start(f32[1,4,4,32]{3,2,1,0:T(4,128)} %bias_ref.1) | copy-start | bytes 6148
  1.7 14.0 %collective-permute-start.2 = (bf16[5,96,384]{2,1,0:T(8,128)(2,1)S(1)}, bf16[5,96,384]{2,1,0:T(8,128)(2,1)S(1)}, u32[]{:S(2)}, u32[]{:S(2)}) collective-permute-start(bf16[5,96,384]{2,1,0:T(8,128)(2,1)S(1)} %get-tuple-element.28), channel_id=1, source_target_pairs={{0,2},{2,0},{4,6},{6,4},{8,10},{10,8},{12,14},{14,12},{1,3},{3,1},... | collective-permute-start | bytes 1105928 | tf_op jit(solution)/shard_map/ppermute | solution.py:139
  4.8 3.8 %collective-permute-start = (bf16[1,48,256]{2,1,0:T(8,128)(2,1)S(1)}, bf16[1,48,256]{2,1,0:T(8,128)(2,1)S(1)}, u32[]{:S(2)}, u32[]{:S(2)}) collective-permute-start(bf16[1,48,256]{2,1,0:T(8,128)(2,1)S(1)} %bitcast.12), channel_id=1, source_target_pairs={{0,4},{2,6},{4,0},{6,2},{8,12},{10,14},{12,8},{14,10},{1,5},{3,7},... | collective-permute-start | bytes 73736 | tf_op jit(solution)/shard_map/ppermute | solution.py:139
  8.6 5.0 %collective-permute-start.1 = (bf16[2,48,256]{2,1,0:T(8,128)(2,1)S(1)}, bf16[2,48,256]{2,1,0:T(8,128)(2,1)S(1)}, u32[]{:S(2)}, u32[]{:S(2)}) collective-permute-start(bf16[2,48,256]{2,1,0:T(8,128)(2,1)S(1)} %shard_map.92.first_ref), channel_id=1, source_target_pairs={{0,8},{2,10},{4,12},{6,14},{8,0},{10,2},{12,4},{14,6},{1,9},{3,11}... | collective-permute-start | bytes 147464 | tf_op jit(solution)/shard_map/ppermute | solution.py:139
  13.6 4.7 %collective-permute-start.4 = (bf16[4,48,256]{2,1,0:T(8,128)(2,1)S(1)}, bf16[4,48,256]{2,1,0:T(8,128)(2,1)S(1)}, u32[]{:S(2)}, u32[]{:S(2)}) collective-permute-start(bf16[4,48,256]{2,1,0:T(8,128)(2,1)S(1)} %shard_map.93.near_ref), channel_id=1, source_target_pairs={{0,2},{2,0},{4,6},{6,4},{8,10},{10,8},{12,14},{14,12},{1,3},{3,1},... | collective-permute-start | bytes 294920 | tf_op jit(solution)/shard_map/ppermute | solution.py:139
  13.9 7.9 %collective-permute-start.6 = (bf16[5,96,384]{2,1,0:T(8,128)(2,1)S(1)}, bf16[5,96,384]{2,1,0:T(8,128)(2,1)S(1)}, u32[]{:S(2)}, u32[]{:S(2)}) collective-permute-start(bf16[5,96,384]{2,1,0:T(8,128)(2,1)S(1)} %get-tuple-element.28), channel_id=1, source_target_pairs={{0,4},{2,6},{4,0},{6,2},{8,12},{10,14},{12,8},{14,10},{1,5},{3,7},... | collective-permute-start | bytes 1105928 | tf_op jit(solution)/shard_map/ppermute | solution.py:139
  15.8 7.7 %collective-permute-start.8 = (bf16[5,96,384]{2,1,0:T(8,128)(2,1)S(1)}, bf16[5,96,384]{2,1,0:T(8,128)(2,1)S(1)}, u32[]{:S(2)}, u32[]{:S(2)}) collective-permute-start(bf16[5,96,384]{2,1,0:T(8,128)(2,1)S(1)} %collective-permute-done.2.w1), channel_id=1, source_target_pairs={{0,16},{16,0},{1,17},{17,1},{2,18},{18,2},{3,19},{19,3},{4,20},{20... | collective-permute-start | bytes 1105928 | tf_op jit(solution)/shard_map/ppermute | solution.py:139
  18.3 1.3 %collective-permute-start.5 = (bf16[4,48,256]{2,1,0:T(8,128)(2,1)S(1)}, bf16[4,48,256]{2,1,0:T(8,128)(2,1)S(1)}, u32[]{:S(2)}, u32[]{:S(2)}) collective-permute-start(bf16[4,48,256]{2,1,0:T(8,128)(2,1)S(1)} %collective-permute-done.4.side_ref), channel_id=1, source_target_pairs={{0,1},{1,0},{2,3},{3,2},{4,5},{5,4},{6,7},{7,6},{8,9},{9,8},{10,11... | collective-permute-start | bytes 294920 | tf_op jit(solution)/shard_map/ppermute | solution.py:139
  18.3 1.5 %collective-permute-start.3 = (bf16[4,48,256]{2,1,0:T(8,128)(2,1)S(1)}, bf16[4,48,256]{2,1,0:T(8,128)(2,1)S(1)}, u32[]{:S(2)}, u32[]{:S(2)}) collective-permute-start(bf16[4,48,256]{2,1,0:T(8,128)(2,1)S(1)} %shard_map.93.near_ref), channel_id=1, source_target_pairs={{0,1},{1,0},{2,3},{3,2},{4,5},{5,4},{6,7},{7,6},{8,9},{9,8},{10,11... | collective-permute-start | bytes 294920 | tf_op jit(solution)/shard_map/ppermute | solution.py:139
  19.2 7.4 %copy-start.3 = (bf16[1,128,1536]{2,1,0:T(8,128)(2,1)S(1)}, bf16[1,128,1536]{2,1,0:T(8,128)(2,1)}, u32[]{:S(2)}) copy-start(bf16[1,128,1536]{2,1,0:T(8,128)(2,1)} %param.9) | copy-start | bytes 1179652
  19.2 7.4 %copy-start.6 = (f32[1536]{0:T(1024)S(1)}, f32[1536]{0:T(1024)}, u32[]{:S(2)}) copy-start(f32[1536]{0:T(1024)} %gain_ref.3) | copy-start | bytes 18436
  19.2 7.4 %copy-start.7 = (f32[384]{0:T(512)S(1)}, f32[384]{0:T(512)}, u32[]{:S(2)}) copy-start(f32[384]{0:T(512)} %dec_bias_ref.1) | copy-start | bytes 4612
  19.2 17.1 %copy-start = (bf16[5,192,384]{2,1,0:T(8,128)(2,1)S(1)}, bf16[5,192,384]{2,1,0:T(8,128)(2,1)}, u32[]{:S(2)}) copy-start(bf16[5,192,384]{2,1,0:T(8,128)(2,1)} %param.16) | copy-start | bytes 2211844
  21.8 12.6 %collective-permute-start.11 = (bf16[5,96,384]{2,1,0:T(8,128)(2,1)S(1)}, bf16[5,96,384]{2,1,0:T(8,128)(2,1)S(1)}, u32[]{:S(2)}, u32[]{:S(2)}) collective-permute-start(bf16[5,96,384]{2,1,0:T(8,128)(2,1)S(1)} %collective-permute-done.6.w3), channel_id=1, source_target_pairs={{0,2},{2,0},{4,6},{6,4},{8,10},{10,8},{12,14},{14,12},{1,3},{3,1},... | collective-permute-start | bytes 1105928 | tf_op jit(solution)/shard_map/ppermute | solution.py:139
  23.5 11.5 %collective-permute-start.12 = (bf16[5,96,384]{2,1,0:T(8,128)(2,1)S(1)}, bf16[5,96,384]{2,1,0:T(8,128)(2,1)S(1)}, u32[]{:S(2)}, u32[]{:S(2)}) collective-permute-start(bf16[5,96,384]{2,1,0:T(8,128)(2,1)S(1)} %collective-permute-done.8.w2), channel_id=1, source_target_pairs={{0,4},{2,6},{4,0},{6,2},{8,12},{10,14},{12,8},{14,10},{1,5},{3,7},... | collective-permute-start | bytes 1105928 | tf_op jit(solution)/shard_map/ppermute | solution.py:139
  25.0 1.5 %collective-permute-start.7 = (bf16[80,1536]{1,0:T(8,128)(2,1)S(1)}, bf16[80,1536]{1,0:T(8,128)(2,1)S(1)}, u32[]{:S(2)}, u32[]{:S(2)}) collective-permute-start(bf16[80,1536]{1,0:T(8,128)(2,1)S(1)} %get-tuple-element.29.own_ref), channel_id=1, source_target_pairs={{0,1},{1,0},{2,3},{3,2},{4,5},{5,4},{6,7},{7,6},{8,9},{9,8},{10,11... | collective-permute-start | bytes 737288 | tf_op jit(solution)/shard_map/ppermute | solution.py:139
  25.0 11.0 %collective-permute-start.9 = (bf16[5,96,384]{2,1,0:T(8,128)(2,1)S(1)}, bf16[5,96,384]{2,1,0:T(8,128)(2,1)S(1)}, u32[]{:S(2)}, u32[]{:S(2)}) collective-permute-start(bf16[5,96,384]{2,1,0:T(8,128)(2,1)S(1)} %collective-permute-done.6.w3), channel_id=1, source_target_pairs={{0,16},{16,0},{1,17},{17,1},{2,18},{18,2},{3,19},{19,3},{4,20},{20... | collective-permute-start | bytes 1105928 | tf_op jit(solution)/shard_map/ppermute | solution.py:139
  27.3 7.1 %collective-permute-start.10 = (bf16[136,384]{1,0:T(8,128)(2,1)S(1)}, bf16[136,384]{1,0:T(8,128)(2,1)S(1)}, u32[]{:S(2)}, u32[]{:S(2)}) collective-permute-start(bf16[136,384]{1,0:T(8,128)(2,1)S(1)} %get-tuple-element.34), channel_id=1, source_target_pairs={{0,8},{2,10},{4,12},{6,14},{8,0},{10,2},{12,4},{14,6},{1,9},{3,11}... | collective-permute-start | bytes 313352 | tf_op jit(solution)/shard_map/ppermute | solution.py:139
  35.0 1.3 %collective-permute-start.13 = (bf16[136,384]{1,0:T(8,128)(2,1)S(1)}, bf16[136,384]{1,0:T(8,128)(2,1)S(1)}, u32[]{:S(2)}, u32[]{:S(2)}) collective-permute-start(bf16[136,384]{1,0:T(8,128)(2,1)S(1)} %collective-permute-done.10.first_ref), channel_id=1, source_target_pairs={{0,1},{1,0},{2,3},{3,2},{4,5},{5,4},{6,7},{7,6},{8,9},{9,8},{10,11... | collective-permute-start | bytes 313352 | tf_op jit(solution)/shard_map/ppermute | solution.py:139
  37.3 5.8 %collective-permute-start.14 = (bf16[128,384]{1,0:T(8,128)(2,1)S(1)}, bf16[128,384]{1,0:T(8,128)(2,1)S(1)}, u32[]{:S(2)}, u32[]{:S(2)}) collective-permute-start(bf16[128,384]{1,0:T(8,128)(2,1)S(1)} %shard_map.97), channel_id=1, source_target_pairs={{0,8},{2,10},{4,12},{6,14},{8,0},{10,2},{12,4},{14,6},{1,9},{3,11}... | collective-permute-start | bytes 294920 | tf_op jit(solution)/shard_map/ppermute | solution.py:139

commit v10 on v8

--- a/solution.py
+++ b/solution.py
@@ -252,6 +252,10 @@
     count = first_ref.shape[0]
     out_ref[0:count] = first_ref[...]
     out_ref[count:] = second_ref[...]
+
+
+def add_kernel(own_ref, partial_ref, out_ref):
+    out_ref[...] = (own_ref[...] + partial_ref[...].astype(jnp.float32)).astype(jnp.bfloat16)
 
 
 def slot_of(distance):
@@ -518,8 +522,8 @@
     (partial,) = call(
         partner_kernel, [((rows, width), bf16)], [first, second] + weights, scratch
     )
-    decoded = own + exchange(partial, "seq", 4).astype(f32)
-    return decoded.astype(bf16)[None]
+    (decoded,) = call(add_kernel, [((rows, width), bf16)], [own, exchange(partial, "seq", 4)])
+    return decoded[None]
 
 
 def solution(mesh):

time: 44.9 us -> 44.9 us (level)
  Pallas kernels: 6.39 us -> 7.05 us
  other arithmetic: 0.66 us -> 0 us
    pallas_call x7 -> x8, Pallas kernels: 6.39 us -> 7.05 us  [call(): pl.pallas_call(kernel, out_shape=[jax.ShapeDtypeStruct(shape, kind) for s...]
    broadcast_in_dim x1 -> x0, other arithmetic: 0.66 us -> none  [split_body(): return decoded.astype(bf16)[None]]
where the time goes in v10:
time: 44.9 us; the launch traced here: 44.7 us
  waiting for transfers between devices  22.3 us (50%)
  starting transfers between devices  14.8 us (33%)
  Pallas kernels  7.05 us (16%)
    ppermute x15, waiting for transfers between devices, exchange(): return lax.ppermute(values_in, axis, [(i, i ^ mask) for i in range(count)])  22.3 us
    ppermute x15, starting transfers between devices, exchange(): return lax.ppermute(values_in, axis, [(i, i ^ mask) for i in range(count)])  14.8 us
    pallas_call x8, Pallas kernels, call(): pl.pallas_call(kernel, out_shape=[jax.ShapeDtypeStruct(shape, kind) for s...  7.05 us
  transfers between devices with their start and end apart: 15, of which 10 were waited for; matrix products, arithmetic and copies ran while one was open for 1% of the time, Pallas kernels for 8%

profile of v10, /device:TPU:25, one launch (start us, length us, event | category | flops | bytes accessed | tf_op | source)
XLA Modules:
  0.0 44.7 jit_solution(13369969898114845421)
XLA Ops:
  0.0 0.0 copy-start.1
  0.0 0.0 copy-start.2
  0.0 0.0 copy-start.4
  0.0 0.0 copy-start.5
  0.0 1.7 %shard_map.91 = (bf16[48,256]{1,0:T(8,128)(2,1)S(1)}, bf16[64,1536]{1,0:T(8,128)(2,1)S(1)}, bf16[5,96,384]{2,1,0:T(8,128)(2,1)S(1)}) custom-call(bf16[128,1536]{1,0:T(8,128)(2,1)} %bitcast.9, f32[1536]{0:T(1024)} %gain_ref.2, bf16[1536,256]{1,0:T(8,128)(2,1)} %weight_hbm.1, f32[1,4,4,32]{3,2,1,0:T(4,128)} %bias_ref.1, bf16[10,96,384]{2,1,0:T(8,128)(2,1)} %bitcast.6), custom_call_target="tpu_custom_call" | custom-call | tf_op jit(solution)/shard_map/pallas_call | solution.py:144
  1.8 1.3 %collective-permute-start.2 = (bf16[5,96,384]{2,1,0:T(8,128)(2,1)S(1)}, bf16[5,96,384]{2,1,0:T(8,128)(2,1)S(1)}, u32[]{:S(2)}, u32[]{:S(2)}) collective-permute-start(bf16[5,96,384]{2,1,0:T(8,128)(2,1)S(1)} %get-tuple-element.28), channel_id=1, source_target_pairs={{0,2},{2,0},{4,6},{6,4},{8,10},{10,8},{12,14},{14,12},{1,3},{3,1},... | collective-permute-start | bytes 1105928 | tf_op jit(solution)/shard_map/ppermute | solution.py:139
  3.0 0.2 collective-permute-start
  3.2 2.8 %collective-permute-done.second_ref = bf16[1,48,256]{2,1,0:T(8,128)(2,1)S(1)} collective-permute-done((bf16[1,48,256]{2,1,0:T(8,128)(2,1)S(1)}, bf16[1,48,256]{2,1,0:T(8,128)(2,1)S(1)}, u32[]{:S(2)}, u32[]{:S(2)}) %collective-permute-start) | collective-permute-done | bytes 24608 | tf_op jit(solution)/shard_map/ppermute | solution.py:139
  6.0 0.1 collective-permute-start.1
  6.1 4.2 %collective-permute-done.1.second_ref = bf16[2,48,256]{2,1,0:T(8,128)(2,1)S(1)} collective-permute-done((bf16[2,48,256]{2,1,0:T(8,128)(2,1)S(1)}, bf16[2,48,256]{2,1,0:T(8,128)(2,1)S(1)}, u32[]{:S(2)}, u32[]{:S(2)}) %collective-permute-start.1) | collective-permute-done | bytes 49184 | tf_op jit(solution)/shard_map/ppermute | solution.py:139
  10.3 0.1 collective-permute-start.4
  10.4 0.1 collective-permute-start.6
  10.4 0.8 %collective-permute-done.2.w1 = bf16[5,96,384]{2,1,0:T(8,128)(2,1)S(1)} collective-permute-done((bf16[5,96,384]{2,1,0:T(8,128)(2,1)S(1)}, bf16[5,96,384]{2,1,0:T(8,128)(2,1)S(1)}, u32[]{:S(2)}, u32[]{:S(2)}) %collective-permute-start.2) | collective-permute-done | bytes 368672 | tf_op jit(solution)/shard_map/ppermute | solution.py:139
  11.3 1.2 %collective-permute-start.8 = (bf16[5,96,384]{2,1,0:T(8,128)(2,1)S(1)}, bf16[5,96,384]{2,1,0:T(8,128)(2,1)S(1)}, u32[]{:S(2)}, u32[]{:S(2)}) collective-permute-start(bf16[5,96,384]{2,1,0:T(8,128)(2,1)S(1)} %collective-permute-done.2.w1), channel_id=1, source_target_pairs={{0,16},{16,0},{1,17},{17,1},{2,18},{18,2},{3,19},{19,3},{4,20},{20... | collective-permute-start | bytes 1105928 | tf_op jit(solution)/shard_map/ppermute | solution.py:139
  12.5 1.3 %collective-permute-done.4.side_ref = bf16[4,48,256]{2,1,0:T(8,128)(2,1)S(1)} collective-permute-done((bf16[4,48,256]{2,1,0:T(8,128)(2,1)S(1)}, bf16[4,48,256]{2,1,0:T(8,128)(2,1)S(1)}, u32[]{:S(2)}, u32[]{:S(2)}) %collective-permute-start.4) | collective-permute-done | bytes 98336 | tf_op jit(solution)/shard_map/ppermute | solution.py:139
  13.8 4.1 %collective-permute-start.5 = (bf16[4,48,256]{2,1,0:T(8,128)(2,1)S(1)}, bf16[4,48,256]{2,1,0:T(8,128)(2,1)S(1)}, u32[]{:S(2)}, u32[]{:S(2)}) collective-permute-start(bf16[4,48,256]{2,1,0:T(8,128)(2,1)S(1)} %collective-permute-done.4.side_ref), channel_id=1, source_target_pairs={{0,1},{1,0},{2,3},{3,2},{4,5},{5,4},{6,7},{7,6},{8,9},{9,8},{10,11... | collective-permute-start | bytes 294920 | tf_op jit(solution)/shard_map/ppermute | solution.py:139
  17.9 0.0 collective-permute-start.3
  17.9 0.0 copy-done.1
  17.9 0.4 convolution_convert_fusion.query_ref
  18.3 0.0 copy-start.3
  18.3 0.0 copy-start.6
  18.3 0.0 copy-start.7
  18.3 0.0 copy-start
  18.4 0.5 %collective-permute-done.5.side_other_ref = bf16[4,48,256]{2,1,0:T(8,128)(2,1)S(1)} collective-permute-done((bf16[4,48,256]{2,1,0:T(8,128)(2,1)S(1)}, bf16[4,48,256]{2,1,0:T(8,128)(2,1)S(1)}, u32[]{:S(2)}, u32[]{:S(2)}) %collective-permute-start.5) | collective-permute-done | bytes 98336 | tf_op jit(solution)/shard_map/ppermute | solution.py:139
  18.9 0.4 collective-permute-done.3.near_other_ref
  19.2 0.0 copy-done.2
  19.2 0.0 copy-done.4
  19.2 0.0 copy-done.5
  19.2 1.8 %shard_map.94 = (bf16[80,1536]{1,0:T(8,128)(2,1)S(1)}, f32[8,1536]{1,0:T(8,128)S(1)}) custom-call(bf16[64,512]{1,0:T(8,128)(2,1)S(1)} %convolution_convert_fusion.query_ref, bf16[4,48,256]{2,1,0:T(8,128)(2,1)S(1)} %shard_map.93.near_ref, bf16[4,48,256]{2,1,0:T(8,128)(2,1)S(1)} %collective-permute-done.3.near_other_ref, ...), custom_call_target="tpu_custom_call" | custom-call | tf_op jit(solution)/shard_map/pallas_call | solution.py:144
  21.1 0.0 collective-permute-done.6.w3
  21.1 0.3 collective-permute-start.11
  21.4 0.0 collective-permute-done.8.w2
  21.4 0.2 collective-permute-start.12
  21.6 1.8 %collective-permute-start.7 = (bf16[80,1536]{1,0:T(8,128)(2,1)S(1)}, bf16[80,1536]{1,0:T(8,128)(2,1)S(1)}, u32[]{:S(2)}, u32[]{:S(2)}) collective-permute-start(bf16[80,1536]{1,0:T(8,128)(2,1)S(1)} %get-tuple-element.29.own_ref), channel_id=1, source_target_pairs={{0,1},{1,0},{2,3},{3,2},{4,5},{5,4},{6,7},{7,6},{8,9},{9,8},{10,11... | collective-permute-start | bytes 737288 | tf_op jit(solution)/shard_map/ppermute | solution.py:139
  23.4 1.2 %collective-permute-start.9 = (bf16[5,96,384]{2,1,0:T(8,128)(2,1)S(1)}, bf16[5,96,384]{2,1,0:T(8,128)(2,1)S(1)}, u32[]{:S(2)}, u32[]{:S(2)}) collective-permute-start(bf16[5,96,384]{2,1,0:T(8,128)(2,1)S(1)} %collective-permute-done.6.w3), channel_id=1, source_target_pairs={{0,16},{16,0},{1,17},{17,1},{2,18},{18,2},{3,19},{19,3},{4,20},{20... | collective-permute-start | bytes 1105928 | tf_op jit(solution)/shard_map/ppermute | solution.py:139
  24.6 0.0 collective-permute-done.7.other_ref
  24.6 0.0 copy-done.3
  24.6 0.0 copy-done.6
  24.6 0.0 copy-done.7
  24.6 0.7 %shard_map.95 = (bf16[144,768]{1,0:T(8,128)(2,1)S(1)}, bf16[144,384]{1,0:T(8,128)(2,1)S(1)}, f32[128,384]{1,0:T(8,128)S(1)}) custom-call(bf16[128,1536]{1,0:T(8,128)(2,1)S(1)} %bitcast.10, f32[8,1536]{1,0:T(8,128)S(1)} %get-tuple-element.26.edge_ref, bf16[80,1536]{1,0:T(8,128)(2,1)S(1)} %get-tuple-element.29.own_ref, ...), custom_call_target="tpu_custom_call" | custom-call | tf_op jit(solution)/shard_map/pallas_call | solution.py:144
  25.4 0.1 collective-permute-start.10
  25.5 5.8 %collective-permute-done.10.first_ref = bf16[144,384]{1,0:T(8,128)(2,1)S(1)} collective-permute-done((bf16[144,384]{1,0:T(8,128)(2,1)S(1)}, bf16[144,384]{1,0:T(8,128)(2,1)S(1)}, u32[]{:S(2)}, u32[]{:S(2)}) %collective-permute-start.10) | collective-permute-done | bytes 110624 | tf_op jit(solution)/shard_map/ppermute | solution.py:139
  31.2 0.0 collective-permute-done.11.w5
  31.2 0.4 collective-permute-done.12.w6
  31.7 3.1 %collective-permute-start.13 = (bf16[144,384]{1,0:T(8,128)(2,1)S(1)}, bf16[144,384]{1,0:T(8,128)(2,1)S(1)}, u32[]{:S(2)}, u32[]{:S(2)}) collective-permute-start(bf16[144,384]{1,0:T(8,128)(2,1)S(1)} %collective-permute-done.10.first_ref), channel_id=1, source_target_pairs={{0,1},{1,0},{2,3},{3,2},{4,5},{5,4},{6,7},{7,6},{8,9},{9,8},{10,11... | collective-permute-start | bytes 331784 | tf_op jit(solution)/shard_map/ppermute | solution.py:139
  34.8 0.0 collective-permute-done.9.w4
  34.8 1.0 %collective-permute-done.13.second_ref = bf16[144,384]{1,0:T(8,128)(2,1)S(1)} collective-permute-done((bf16[144,384]{1,0:T(8,128)(2,1)S(1)}, bf16[144,384]{1,0:T(8,128)(2,1)S(1)}, u32[]{:S(2)}, u32[]{:S(2)}) %collective-permute-start.13) | collective-permute-done | bytes 110624 | tf_op jit(solution)/shard_map/ppermute | solution.py:139
  35.7 0.0 copy-done
  35.7 1.0 %shard_map.97 = bf16[128,384]{1,0:T(8,128)(2,1)S(1)} custom-call(bf16[144,384]{1,0:T(8,128)(2,1)S(1)} %collective-permute-done.10.first_ref, bf16[144,384]{1,0:T(8,128)(2,1)S(1)} %collective-permute-done.13.second_ref, bf16[10,96,384]{2,1,0:T(8,128)(2,1)S(1)} %bitcast.7, bf16[5,96,384]{2,1,0:T(8,128)(2,1)S(1)} %collective-permute-done.2.w1, ...), custom_call_target="tpu_custom_call" | custom-call | tf_op jit(solution)/shard_map/pallas_call | solution.py:144
  36.8 1.1 %collective-permute-start.14 = (bf16[128,384]{1,0:T(8,128)(2,1)S(1)}, bf16[128,384]{1,0:T(8,128)(2,1)S(1)}, u32[]{:S(2)}, u32[]{:S(2)}) collective-permute-start(bf16[128,384]{1,0:T(8,128)(2,1)S(1)} %shard_map.97), channel_id=1, source_target_pairs={{0,8},{2,10},{4,12},{6,14},{8,0},{10,2},{12,4},{14,6},{1,9},{3,11}... | collective-permute-start | bytes 294920 | tf_op jit(solution)/shard_map/ppermute | solution.py:139
  37.9 1.0 %shard_map.96.own_ref = f32[128,384]{1,0:T(8,128)S(1)} custom-call(bf16[144,768]{1,0:T(8,128)(2,1)S(1)} %get-tuple-element.30.active_ref, f32[128,384]{1,0:T(8,128)S(1)} %get-tuple-element.31.base_ref, bf16[10,96,384]{2,1,0:T(8,128)(2,1)S(1)} %bitcast.8, bf16[5,96,384]{2,1,0:T(8,128)(2,1)S(1)} %collective-permute-done.2.w1, ...), custom_call_target="tpu_custom_call" | custom-call | tf_op jit(solution)/shard_map/pallas_call | solution.py:144
  38.9 5.1 %collective-permute-done.14.partial_ref = bf16[128,384]{1,0:T(8,128)(2,1)S(1)} collective-permute-done((bf16[128,384]{1,0:T(8,128)(2,1)S(1)}, bf16[128,384]{1,0:T(8,128)(2,1)S(1)}, u32[]{:S(2)}, u32[]{:S(2)}) %collective-permute-start.14) | collective-permute-done | bytes 98336 | tf_op jit(solution)/shard_map/ppermute | solution.py:139
  44.1 0.7 %shard_map.98 = bf16[128,384]{1,0:T(8,128)(2,1)} custom-call(f32[128,384]{1,0:T(8,128)S(1)} %shard_map.96.own_ref, bf16[128,384]{1,0:T(8,128)(2,1)S(1)} %collective-permute-done.14.partial_ref), custom_call_target="tpu_custom_call" | custom-call | tf_op jit(solution)/shard_map/pallas_call | solution.py:144
  (2 shorter events, 0.0 us)
Async XLA Ops:
  0.0 17.9 %copy-start.1 = (bf16[1536,512]{1,0:T(8,128)(2,1)S(1)}, bf16[1536,512]{1,0:T(8,128)(2,1)}, u32[]{:S(2)}) copy-start(bf16[1536,512]{1,0:T(8,128)(2,1)} %query_weight_ref.1) | copy-start | bytes 4718596
  0.0 19.2 %copy-start.2 = (bf16[512,1536]{1,0:T(8,128)(2,1)S(1)}, bf16[512,1536]{1,0:T(8,128)(2,1)}, u32[]{:S(2)}) copy-start(bf16[512,1536]{1,0:T(8,128)(2,1)} %out_weight_ref.1) | copy-start | bytes 4718596
  0.0 19.2 %copy-start.4 = (f32[1536]{0:T(1024)S(1)}, f32[1536]{0:T(1024)}, u32[]{:S(2)}) copy-start(f32[1536]{0:T(1024)} %gain_ref.2) | copy-start | bytes 18436
  0.0 19.2 %copy-start.5 = (f32[1,4,4,32]{3,2,1,0:T(4,128)S(1)}, f32[1,4,4,32]{3,2,1,0:T(4,128)}, u32[]{:S(2)}) copy-start(f32[1,4,4,32]{3,2,1,0:T(4,128)} %bias_ref.1) | copy-start | bytes 6148
  1.8 9.5 %collective-permute-start.2 = (bf16[5,96,384]{2,1,0:T(8,128)(2,1)S(1)}, bf16[5,96,384]{2,1,0:T(8,128)(2,1)S(1)}, u32[]{:S(2)}, u32[]{:S(2)}) collective-permute-start(bf16[5,96,384]{2,1,0:T(8,128)(2,1)S(1)} %get-tuple-element.28), channel_id=1, source_target_pairs={{0,2},{2,0},{4,6},{6,4},{8,10},{10,8},{12,14},{14,12},{1,3},{3,1},... | collective-permute-start | bytes 1105928 | tf_op jit(solution)/shard_map/ppermute | solution.py:139
  3.0 3.0 %collective-permute-start = (bf16[1,48,256]{2,1,0:T(8,128)(2,1)S(1)}, bf16[1,48,256]{2,1,0:T(8,128)(2,1)S(1)}, u32[]{:S(2)}, u32[]{:S(2)}) collective-permute-start(bf16[1,48,256]{2,1,0:T(8,128)(2,1)S(1)} %bitcast.11), channel_id=1, source_target_pairs={{0,4},{2,6},{4,0},{6,2},{8,12},{10,14},{12,8},{14,10},{1,5},{3,7},... | collective-permute-start | bytes 73736 | tf_op jit(solution)/shard_map/ppermute | solution.py:139
  6.0 4.3 %collective-permute-start.1 = (bf16[2,48,256]{2,1,0:T(8,128)(2,1)S(1)}, bf16[2,48,256]{2,1,0:T(8,128)(2,1)S(1)}, u32[]{:S(2)}, u32[]{:S(2)}) collective-permute-start(bf16[2,48,256]{2,1,0:T(8,128)(2,1)S(1)} %shard_map.92.first_ref), channel_id=1, source_target_pairs={{0,8},{2,10},{4,12},{6,14},{8,0},{10,2},{12,4},{14,6},{1,9},{3,11}... | collective-permute-start | bytes 147464 | tf_op jit(solution)/shard_map/ppermute | solution.py:139
  10.3 3.5 %collective-permute-start.4 = (bf16[4,48,256]{2,1,0:T(8,128)(2,1)S(1)}, bf16[4,48,256]{2,1,0:T(8,128)(2,1)S(1)}, u32[]{:S(2)}, u32[]{:S(2)}) collective-permute-start(bf16[4,48,256]{2,1,0:T(8,128)(2,1)S(1)} %shard_map.93.near_ref), channel_id=1, source_target_pairs={{0,2},{2,0},{4,6},{6,4},{8,10},{10,8},{12,14},{14,12},{1,3},{3,1},... | collective-permute-start | bytes 294920 | tf_op jit(solution)/shard_map/ppermute | solution.py:139
  10.4 10.7 %collective-permute-start.6 = (bf16[5,96,384]{2,1,0:T(8,128)(2,1)S(1)}, bf16[5,96,384]{2,1,0:T(8,128)(2,1)S(1)}, u32[]{:S(2)}, u32[]{:S(2)}) collective-permute-start(bf16[5,96,384]{2,1,0:T(8,128)(2,1)S(1)} %get-tuple-element.28), channel_id=1, source_target_pairs={{0,4},{2,6},{4,0},{6,2},{8,12},{10,14},{12,8},{14,10},{1,5},{3,7},... | collective-permute-start | bytes 1105928 | tf_op jit(solution)/shard_map/ppermute | solution.py:139
  11.3 10.1 %collective-permute-start.8 = (bf16[5,96,384]{2,1,0:T(8,128)(2,1)S(1)}, bf16[5,96,384]{2,1,0:T(8,128)(2,1)S(1)}, u32[]{:S(2)}, u32[]{:S(2)}) collective-permute-start(bf16[5,96,384]{2,1,0:T(8,128)(2,1)S(1)} %collective-permute-done.2.w1), channel_id=1, source_target_pairs={{0,16},{16,0},{1,17},{17,1},{2,18},{18,2},{3,19},{19,3},{4,20},{20... | collective-permute-start | bytes 1105928 | tf_op jit(solution)/shard_map/ppermute | solution.py:139
  13.8 5.1 %collective-permute-start.5 = (bf16[4,48,256]{2,1,0:T(8,128)(2,1)S(1)}, bf16[4,48,256]{2,1,0:T(8,128)(2,1)S(1)}, u32[]{:S(2)}, u32[]{:S(2)}) collective-permute-start(bf16[4,48,256]{2,1,0:T(8,128)(2,1)S(1)} %collective-permute-done.4.side_ref), channel_id=1, source_target_pairs={{0,1},{1,0},{2,3},{3,2},{4,5},{5,4},{6,7},{7,6},{8,9},{9,8},{10,11... | collective-permute-start | bytes 294920 | tf_op jit(solution)/shard_map/ppermute | solution.py:139
  17.9 1.3 %collective-permute-start.3 = (bf16[4,48,256]{2,1,0:T(8,128)(2,1)S(1)}, bf16[4,48,256]{2,1,0:T(8,128)(2,1)S(1)}, u32[]{:S(2)}, u32[]{:S(2)}) collective-permute-start(bf16[4,48,256]{2,1,0:T(8,128)(2,1)S(1)} %shard_map.93.near_ref), channel_id=1, source_target_pairs={{0,1},{1,0},{2,3},{3,2},{4,5},{5,4},{6,7},{7,6},{8,9},{9,8},{10,11... | collective-permute-start | bytes 294920 | tf_op jit(solution)/shard_map/ppermute | solution.py:139
  18.3 6.3 %copy-start.3 = (bf16[1,128,1536]{2,1,0:T(8,128)(2,1)S(1)}, bf16[1,128,1536]{2,1,0:T(8,128)(2,1)}, u32[]{:S(2)}) copy-start(bf16[1,128,1536]{2,1,0:T(8,128)(2,1)} %param.9) | copy-start | bytes 1179652
  18.3 6.3 %copy-start.6 = (f32[1536]{0:T(1024)S(1)}, f32[1536]{0:T(1024)}, u32[]{:S(2)}) copy-start(f32[1536]{0:T(1024)} %gain_ref.3) | copy-start | bytes 18436
  18.3 6.3 %copy-start.7 = (f32[384]{0:T(512)S(1)}, f32[384]{0:T(512)}, u32[]{:S(2)}) copy-start(f32[384]{0:T(512)} %dec_bias_ref.1) | copy-start | bytes 4612
  18.3 17.4 %copy-start = (bf16[5,192,384]{2,1,0:T(8,128)(2,1)S(1)}, bf16[5,192,384]{2,1,0:T(8,128)(2,1)}, u32[]{:S(2)}) copy-start(bf16[5,192,384]{2,1,0:T(8,128)(2,1)} %param.16) | copy-start | bytes 2211844
  21.1 10.1 %collective-permute-start.11 = (bf16[5,96,384]{2,1,0:T(8,128)(2,1)S(1)}, bf16[5,96,384]{2,1,0:T(8,128)(2,1)S(1)}, u32[]{:S(2)}, u32[]{:S(2)}) collective-permute-start(bf16[5,96,384]{2,1,0:T(8,128)(2,1)S(1)} %collective-permute-done.6.w3), channel_id=1, source_target_pairs={{0,2},{2,0},{4,6},{6,4},{8,10},{10,8},{12,14},{14,12},{1,3},{3,1},... | collective-permute-start | bytes 1105928 | tf_op jit(solution)/shard_map/ppermute | solution.py:139
  21.4 10.3 %collective-permute-start.12 = (bf16[5,96,384]{2,1,0:T(8,128)(2,1)S(1)}, bf16[5,96,384]{2,1,0:T(8,128)(2,1)S(1)}, u32[]{:S(2)}, u32[]{:S(2)}) collective-permute-start(bf16[5,96,384]{2,1,0:T(8,128)(2,1)S(1)} %collective-permute-done.8.w2), channel_id=1, source_target_pairs={{0,4},{2,6},{4,0},{6,2},{8,12},{10,14},{12,8},{14,10},{1,5},{3,7},... | collective-permute-start | bytes 1105928 | tf_op jit(solution)/shard_map/ppermute | solution.py:139
  21.6 3.1 %collective-permute-start.7 = (bf16[80,1536]{1,0:T(8,128)(2,1)S(1)}, bf16[80,1536]{1,0:T(8,128)(2,1)S(1)}, u32[]{:S(2)}, u32[]{:S(2)}) collective-permute-start(bf16[80,1536]{1,0:T(8,128)(2,1)S(1)} %get-tuple-element.29.own_ref), channel_id=1, source_target_pairs={{0,1},{1,0},{2,3},{3,2},{4,5},{5,4},{6,7},{7,6},{8,9},{9,8},{10,11... | collective-permute-start | bytes 737288 | tf_op jit(solution)/shard_map/ppermute | solution.py:139
  23.4 11.4 %collective-permute-start.9 = (bf16[5,96,384]{2,1,0:T(8,128)(2,1)S(1)}, bf16[5,96,384]{2,1,0:T(8,128)(2,1)S(1)}, u32[]{:S(2)}, u32[]{:S(2)}) collective-permute-start(bf16[5,96,384]{2,1,0:T(8,128)(2,1)S(1)} %collective-permute-done.6.w3), channel_id=1, source_target_pairs={{0,16},{16,0},{1,17},{17,1},{2,18},{18,2},{3,19},{19,3},{4,20},{20... | collective-permute-start | bytes 1105928 | tf_op jit(solution)/shard_map/ppermute | solution.py:139
  25.4 5.8 %collective-permute-start.10 = (bf16[144,384]{1,0:T(8,128)(2,1)S(1)}, bf16[144,384]{1,0:T(8,128)(2,1)S(1)}, u32[]{:S(2)}, u32[]{:S(2)}) collective-permute-start(bf16[144,384]{1,0:T(8,128)(2,1)S(1)} %get-tuple-element.34), channel_id=1, source_target_pairs={{0,8},{2,10},{4,12},{6,14},{8,0},{10,2},{12,4},{14,6},{1,9},{3,11}... | collective-permute-start | bytes 331784 | tf_op jit(solution)/shard_map/ppermute | solution.py:139
  31.7 4.1 %collective-permute-start.13 = (bf16[144,384]{1,0:T(8,128)(2,1)S(1)}, bf16[144,384]{1,0:T(8,128)(2,1)S(1)}, u32[]{:S(2)}, u32[]{:S(2)}) collective-permute-start(bf16[144,384]{1,0:T(8,128)(2,1)S(1)} %collective-permute-done.10.first_ref), channel_id=1, source_target_pairs={{0,1},{1,0},{2,3},{3,2},{4,5},{5,4},{6,7},{7,6},{8,9},{9,8},{10,11... | collective-permute-start | bytes 331784 | tf_op jit(solution)/shard_map/ppermute | solution.py:139
  36.8 7.3 %collective-permute-start.14 = (bf16[128,384]{1,0:T(8,128)(2,1)S(1)}, bf16[128,384]{1,0:T(8,128)(2,1)S(1)}, u32[]{:S(2)}, u32[]{:S(2)}) collective-permute-start(bf16[128,384]{1,0:T(8,128)(2,1)S(1)} %shard_map.97), channel_id=1, source_target_pairs={{0,8},{2,10},{4,12},{6,14},{8,0},{10,2},{12,4},{14,6},{1,9},{3,11}... | collective-permute-start | bytes 294920 | tf_op jit(solution)/shard_map/ppermute | solution.py:139
